TPU v7x, 32 devices: a whole 2x2x4 slice. The times are simulated.
32 devices in a mesh: region: 4 (over z), dom: 8 (over y, x, core).
Axes of the slice: x: 2, y: 2, z: 4, core: 2. Of those that a mesh axis runs over, the one named last changes fastest.
Arguments:
- fine_blocks: bfloat16 [1536, 7, 128, 128], P(('region', 'dom')), may hold values from -6 to 6
- interp: bfloat16 [1536, 8192], P(('region', 'dom')), may hold values from -0.5 to 0.5
- fine_cols: int32 [1536, 7], P(('region', 'dom')), may hold values from 0 to 1535, as said below
- fine_slot: int32 [1536, 7], P(('region', 'dom')), may hold values from 0 to 6
- fine_owner: int32 [1536, 1], P(('region', 'dom')), may hold values from 0 to 7; in each aligned block of 48 rows (0 to 47, 48 to 95, ...) at most 6 rows name the same one
- fine_place: int32 [1536], P(('region', 'dom')), may hold values from 0 to 23
- coarse_interp: bfloat16 [768, 2048], P(('region', 'dom')), may hold values from -0.75 to 0.75
- coarse_cols: int32 [768, 7], P(('region', 'dom')), may hold values from 0 to 767, as said below
- coarse_slot: int32 [768, 7], P(('region', 'dom')), may hold values from 0 to 6
- coarse_owner: int32 [768, 1], P(('region', 'dom')), may hold values from 0 to 7; in each aligned block of 24 rows (0 to 23, 24 to 47, ...) at most 3 rows name the same one
- coarse_place: int32 [768], P(('region', 'dom')), may hold values from 0 to 11
Outputs:
- coarse_blocks: bfloat16 [768, 7, 4096], P(('region', 'dom'))
- coarse2_blocks: bfloat16 [384, 7, 1024], P(('region', 'dom'))
Inputs may be any that keep to these rules, and one draw needn't show every extreme that they name: fine_cols[i, 0] = i; every other entry names a fine row held by the device of the same dom index in the same region or in an adjacent region. coarse_cols[q, 0] = q; every other entry names a coarse row of the same region or of an adjacent region. `fine_owner`: among the rows of one device, no owner is named more than 6 times, a bound that some block reaches. `coarse_owner`: among the rows of one device, no owner is named more than 3 times, a bound that some block reaches.
All inputs are finite; a program needn't handle non-finite values.
Results may differ from a plain program's by a relative error of at most 0.0065.
Values may be sent and summed in bfloat16 or wider, within the bound.
No kernel may reach another device: no remote copies, remote signals or barrier semaphores. Data moves between devices by JAX's collectives and lax.ppermute only.
A program may use at most 128 MiB of HBM per device.

v0:
```python
import jax
import jax.numpy as jnp
from jax import lax
from jax.sharding import PartitionSpec as P


def extended(cells, sides, width):
    for axis, dim in sides:
        count = lax.axis_size(axis)
        ends = count - 1
        head = lax.slice_in_dim(cells, 0, width, axis=dim)
        tail = lax.slice_in_dim(cells, cells.shape[dim] - width, cells.shape[dim], axis=dim)
        cells = jnp.concatenate(
            [
                lax.ppermute(tail, axis, [(i, (i + 1) % count) for i in range(ends)]),
                cells,
                lax.ppermute(head, axis, [((i + 1) % count, i) for i in range(ends)]),
            ],
            axis=dim,
        )
    return cells


def block_products(blocks, picked):
    return jnp.einsum("rkab,rkbc->rkac", blocks, picked, preferred_element_type=jnp.float32).astype(
        jnp.bfloat16
    )


def slot_table(slot, stencil):
    letters = jnp.arange(stencil, dtype=jnp.int32)
    return (slot[:, :, None] == letters[None, None, :]).astype(jnp.float32)


def restrict_terms(product, own_rows, choose):
    count = product.shape[0]
    stencil = product.shape[1]
    narrow = own_rows.shape[2]
    term = jnp.einsum("rac,rkad->rkcd", own_rows, product, preferred_element_type=jnp.float32)
    term = term.reshape(count, stencil, narrow * narrow)
    return jnp.einsum("rks,rkx->rsx", choose, term, precision=lax.Precision.HIGHEST)


def block_terms(blocks, picked, own_rows, slot):
    product = block_products(blocks, picked)
    return restrict_terms(product, own_rows, slot_table(slot, blocks.shape[1]))


def owner_positions(owner, parts, capacity):
    member = (owner[:, None] == jnp.arange(parts, dtype=jnp.int32)[None, :]).astype(jnp.int32)
    before = jnp.cumsum(member, axis=0) - member
    rank = jnp.sum(before * member, axis=1)
    return owner * capacity + rank


def place_into(values, position, slots):
    return jnp.zeros((slots,) + values.shape[1:], values.dtype).at[position].set(values)


def pack_owned(values, owner, place, parts, capacity, owned):
    position = owner_positions(owner, parts, capacity)
    buffer = place_into(values, position, parts * capacity)
    labels = (place[:, None] == jnp.arange(owned, dtype=jnp.int32)[None, :]).astype(jnp.float32)
    marks = place_into(labels, position, parts * capacity)
    return (buffer, marks)


def local(
    fine_blocks,
    interp,
    fine_cols,
    fine_slot,
    fine_owner,
    fine_place,
    coarse_interp,
    coarse_cols,
    coarse_slot,
    coarse_owner,
    coarse_place,
):
    rows = fine_blocks.shape[0]
    stencil = fine_blocks.shape[1]
    width = fine_blocks.shape[2]
    narrow = interp.shape[1] // width
    narrow2 = coarse_interp.shape[1] // narrow
    parts = lax.axis_size("dom")
    region = lax.axis_index("region")
    owned = rows // 2
    owned2 = owned // 2
    capacity = max(2, rows // 8)
    capacity2 = max(2, owned // 8)
    nearby_rows = extended(interp, (("region", 0),), rows)
    span = parts * rows
    index = (fine_cols // span - region + 1) * rows + fine_cols % rows
    picked = nearby_rows[index].reshape(rows, stencil, width, narrow)
    own_rows = interp.reshape(rows, width, narrow)
    slotted = block_terms(fine_blocks, picked, own_rows, fine_slot)
    sent, marks = pack_owned(slotted, fine_owner[:, 0], fine_place, parts, capacity, owned)
    arrived, labels = (
        lax.all_to_all(sent, "dom", split_axis=0, concat_axis=0, tiled=True),
        lax.all_to_all(marks, "dom", split_axis=0, concat_axis=0, tiled=True),
    )
    coarse_sum = jnp.einsum("rc,rkx->ckx", labels, arrived, precision=lax.Precision.HIGHEST)
    coarse_blocks = coarse_sum.astype(jnp.bfloat16)
    span2 = parts * owned
    flat = coarse_interp.shape[1]
    widened = extended(coarse_interp, (("region", 0),), owned)
    stacked = widened.reshape(3, owned, flat)
    collected = lax.all_gather(stacked, "dom", axis=1, tiled=True)
    table = collected.reshape(3 * span2, flat)
    index2 = (coarse_cols // span2 - region + 1) * span2 + coarse_cols % span2
    picked2 = table[index2].reshape(owned, stencil, narrow, narrow2)
    square = coarse_blocks.reshape(owned, stencil, narrow, narrow)
    own_coarse = coarse_interp.reshape(owned, narrow, narrow2)
    slotted2 = block_terms(square, picked2, own_coarse, coarse_slot)
    sent2, marks2 = pack_owned(slotted2, coarse_owner[:, 0], coarse_place, parts, capacity2, owned2)
    arrived2, labels2 = (
        lax.all_to_all(sent2, "dom", split_axis=0, concat_axis=0, tiled=True),
        lax.all_to_all(marks2, "dom", split_axis=0, concat_axis=0, tiled=True),
    )
    second_sum = jnp.einsum("rc,rkx->ckx", labels2, arrived2, precision=lax.Precision.HIGHEST)
    return (coarse_blocks, second_sum.astype(jnp.bfloat16))


def solution(mesh):
    in_specs = (
        P(("region", "dom"), None, None, None),
        P(("region", "dom"), None),
        P(("region", "dom"), None),
        P(("region", "dom"), None),
        P(("region", "dom"), None),
        P(("region", "dom")),
        P(("region", "dom"), None),
        P(("region", "dom"), None),
        P(("region", "dom"), None),
        P(("region", "dom"), None),
        P(("region", "dom")),
    )
    out_specs = (P(("region", "dom"), None, None), P(("region", "dom"), None, None))
    return jax.shard_map(local, mesh=mesh, in_specs=in_specs, out_specs=out_specs, check_vma=False)
```

profile of v0, /device:TPU:0, one launch (start us, length us, event | category | flops | bytes accessed | tf_op | source)
XLA Modules:
  0.0 265.8 jit_solution(9862358425277935994)
XLA Ops:
  7.2 5.0 %collective-permute-start = (bf16[48,8192]{1,0:T(8,128)(2,1)}, bf16[48,8192]{1,0:T(8,128)(2,1)S(1)}, u32[]{:S(2)}, u32[]{:S(2)}) collective-permute-start(bf16[48,8192]{1,0:T(8,128)(2,1)} %param.12), channel_id=1, source_target_pairs={{0,8},{8,16},{16,24},{1,9},{9,17},{17,25},{2,10},{10,18},{18,26},{... | collective-permute-start | bytes 2359304 | tf_op jit(solution)/shard_map/ppermute | solution.py:15
  12.2 1.3 collective-permute-start.1
  13.4 0.7 fusion.30
  14.3 0.8 select_reduce_fusion
  15.8 0.9 scatter_custom_fusion
  16.7 0.7 reshape.114
  17.4 3.7 %all-to-all-start = ((f32[8,1,144]{2,1,0:T(1,128)}), f32[8,1,144]{2,1,0:T(1,128)S(1)}, u32[]{:S(2)}, u32[]{:S(2)}) async-start(f32[8,1,144]{2,1,0:T(1,128)} %reshape.114), calls=%async_computation | async-start | bytes 16384 | tf_op jit(solution)/shard_map/all_to_all | solution.py:101
  21.1 3.4 %reshape.42 = bf16[48,128,64]{2,1,0:T(8,128)(2,1)} reshape(bf16[48,8192]{1,0:T(8,128)(2,1)} %param.12) | data formatting | bytes 1572864 | tf_op jit(solution)/shard_map/reshape | solution.py:96
  24.5 0.7 compare_select_fusion.1
  25.4 0.8 copy.31
  26.2 3.0 %collective-permute-done = bf16[48,8192]{1,0:T(8,128)(2,1)S(1)} collective-permute-done((bf16[48,8192]{1,0:T(8,128)(2,1)}, bf16[48,8192]{1,0:T(8,128)(2,1)S(1)}, u32[]{:S(2)}, u32[]{:S(2)}) %collective-permute-start) | collective-permute-done | bytes 786464 | tf_op jit(solution)/shard_map/ppermute | solution.py:15
  29.2 4.2 %collective-permute-done.1 = bf16[48,8192]{1,0:T(8,128)(2,1)} collective-permute-done((bf16[48,8192]{1,0:T(8,128)(2,1)}, bf16[48,8192]{1,0:T(8,128)(2,1)}, u32[]{:S(2)}, u32[]{:S(2)}) %collective-permute-start.1) | collective-permute-done | bytes 786464 | tf_op jit(solution)/shard_map/ppermute | solution.py:17
  33.4 1.5 pad_maximum_fusion
  34.9 6.9 %gather_fusion = bf16[336,8192]{1,0:T(8,128)(2,1)} fusion(bf16[144,8192]{1,0:T(8,128)(2,1)S(1)} %pad_maximum_fusion, s32[1024]{0:T(1024)S(1)} %pad_clamp_fusion.1), kind=kCustom, calls=%fused_computation | custom fusion | bytes 11011392 | tf_op jit(solution)/shard_map/gather | solution.py:95
  41.8 16.0 %reshape.41 = bf16[48,7,128,64]{3,2,1,0:T(8,128)(2,1)} reshape(bf16[336,8192]{1,0:T(8,128)(2,1)} %gather_fusion) | data formatting | bytes 11010048 | tf_op jit(solution)/shard_map/reshape | solution.py:95
  57.9 16.6 %fusion.10 = f32[48,7,64,64]{2,3,1,0:T(8,128)} fusion(bf16[48,7,128,64]{3,2,1,0:T(8,128)(2,1)} %reshape.41, bf16[48,7,128,128]{3,2,1,0:T(8,128)(2,1)} %param.11, bf16[48,128,64]{2,1,0:T(8,128)(2,1)S(1)} %copy-done), kind=kOutput, calls=%fused_computation.13 | convolution fusion | flops 1059717120 | bytes 22806528 | tf_op jit(solution)/shard_map/rac,rkad->rkcd/dot_general | solution.py:39
  74.4 12.2 %copy.58 = f32[48,7,64,64]{3,2,1,0:T(8,128)} copy(f32[48,7,64,64]{2,3,1,0:T(8,128)} %fusion.10) | data formatting | bytes 11010048 | tf_op jit(solution)/shard_map/reshape | solution.py:40
  86.6 10.3 %reshape.108 = f32[48,7,4096]{2,1,0:T(8,128)} reshape(f32[48,7,64,64]{3,2,1,0:T(8,128)} %copy.58) | data formatting | bytes 11010048 | tf_op jit(solution)/shard_map/reshape | solution.py:40
  96.9 8.4 %fusion.23 = f32[48,7,4096]{2,1,0:T(8,128)} fusion(f32[48,7,4096]{2,1,0:T(8,128)} %reshape.108, s32[48,7]{1,0:T(8,128)S(1)} %copy.31), kind=kOutput, calls=%fused_computation.25 | convolution fusion | flops 115607856 | bytes 11011392 | tf_op jit(solution)/shard_map/rks,rkx->rsx/dot_general | solution.py:41
  105.3 3.4 %broadcast_in_dim.13 = f32[48,7,4096]{2,1,0:T(8,128)} broadcast(f32[]{:T(128)} %constant.30.clone.1), dimensions={} | broadcast | bytes 5505028 | tf_op jit(solution)/shard_map/broadcast_in_dim | solution.py:57
  108.7 12.3 %scatter_fusion = f32[48,7,4096]{2,1,0:T(8,128)} fusion(f32[48,7,4096]{2,1,0:T(8,128)} %broadcast_in_dim.13, s32[48]{0:T(128)S(1)} %fusion.49, f32[48,7,4096]{2,1,0:T(8,128)} %fusion.23), kind=kCustom, calls=%fused_computation.3 | custom fusion | bytes 16515264 | tf_op jit(solution)/shard_map/scatter | solution.py:57
  121.1 4.9 %all-to-all-start.1 = ((f32[48,7,4096]{2,1,0:T(8,128)}), f32[48,7,4096]{2,1,0:T(8,128)}, u32[]{:S(2)}, u32[]{:S(2)}) async-start(f32[48,7,4096]{2,1,0:T(8,128)} %scatter_fusion), calls=%async_computation.1 | async-start | bytes 12582912 | tf_op jit(solution)/shard_map/all_to_all | solution.py:100
  126.0 3.4 %collective-permute-start.2 = (bf16[24,2048]{1,0:T(8,128)(2,1)S(1)}, bf16[24,2048]{1,0:T(8,128)(2,1)S(1)}, u32[]{:S(2)}, u32[]{:S(2)}) collective-permute-start(bf16[24,2048]{1,0:T(8,128)(2,1)S(1)} %copy-done.2), channel_id=1, source_target_pairs={{0,8},{8,16},{16,24},{1,9},{9,17},{17,25},{2,10},{10,18},{18,26},{... | collective-permute-start | bytes 294920 | tf_op jit(solution)/shard_map/ppermute | solution.py:15
  129.4 1.5 collective-permute-start.3
  130.9 1.0 collective-permute-done.2
  132.0 4.1 %collective-permute-done.3 = bf16[24,2048]{1,0:T(8,128)(2,1)S(1)} collective-permute-done((bf16[24,2048]{1,0:T(8,128)(2,1)S(1)}, bf16[24,2048]{1,0:T(8,128)(2,1)S(1)}, u32[]{:S(2)}, u32[]{:S(2)}) %collective-permute-start.3) | collective-permute-done | bytes 98336 | tf_op jit(solution)/shard_map/ppermute | solution.py:17
  136.1 0.7 pad_maximum_fusion.1
  136.8 1.0 reshape.48
  138.1 0.7 copy.39
  139.1 0.7 scatter_custom_fusion.2
  141.0 0.7 reduce
  141.8 48.3 %all-gather.2.cloned.1.call-done = bf16[3,192,2048]{2,1,0:T(8,128)(2,1)} async-done(((bf16[3,24,2048]{2,1,0:T(8,128)(2,1)}), bf16[3,192,2048]{2,1,0:T(8,128)(2,1)}) %all-gather.2.cloned.1.call-update) | async-done | bytes 2359312 | tf_op jit(solution)/shard_map/all_gather | solution.py:109
  190.1 3.7 %gather_fusion.1 = bf16[168,2048]{1,0:T(8,128)(2,1)S(1)} fusion(bf16[576,2048]{1,0:T(8,128)(2,1)} %bitcast.52, s32[1024]{0:T(1024)S(1)} %pad_clamp_fusion), kind=kCustom, calls=%fused_computation.1 | custom fusion | bytes 1376928 | tf_op jit(solution)/shard_map/gather | solution.py:112
  193.8 2.0 reshape.47
  195.8 11.2 %all-to-all-done.1 = f32[48,7,4096]{2,1,0:T(8,128)} async-done(((f32[48,7,4096]{2,1,0:T(8,128)}), f32[48,7,4096]{2,1,0:T(8,128)}, u32[]{:S(2)}, u32[]{:S(2)}) %all-to-all-start.1) | async-done | bytes 5505056 | tf_op jit(solution)/shard_map/all_to_all | solution.py:100
  207.0 3.3 %all-to-all-start.2 = ((f32[8,3,12]{2,1,0:T(4,128)}), f32[8,3,12]{2,1,0:T(4,128)S(1)}, u32[]{:S(2)}, u32[]{:S(2)}) async-start(f32[8,3,12]{2,1,0:T(4,128)} %all_to_all.26), calls=%async_computation.2 | async-start | bytes 32768 | tf_op jit(solution)/shard_map/all_to_all | solution.py:119
  210.4 9.4 %fusion.7 = bf16[24,7,4096]{2,0,1:T(8,128)(2,1)} fusion(f32[48,7,4096]{2,1,0:T(8,128)} %all-to-all-done.1, f32[48,24]{1,0:T(8,128)S(1)} %all_to_all.24), kind=kOutput, calls=%fused_computation.12 | convolution fusion | flops 397049856 | bytes 6885888 | tf_op jit(solution)/shard_map/rc,rkx->ckx/dot_general | solution.py:103
  219.7 5.0 %reshape.44 = bf16[24,7,64,64]{3,2,0,1:T(8,128)(2,1)} reshape(bf16[24,7,4096]{2,0,1:T(8,128)(2,1)} %fusion.7) | data formatting | bytes 2752512 | tf_op jit(solution)/shard_map/reshape | solution.py:113
  224.7 5.3 %convolution_bitcast_fusion = f32[24,7,32,32]{2,3,1,0:T(8,128)} fusion(bf16[24,7,64,32]{3,2,1,0:T(8,128)(2,1)S(1)} %reshape.47, bf16[24,7,64,64]{3,2,0,1:T(8,128)(2,1)} %reshape.44, bf16[24,64,32]{2,1,0:T(8,128)(2,1)S(1)} %copy-done.1), kind=kOutput, calls=%fused_computation.17 | convolution fusion | flops 66404352 | bytes 2850816 | tf_op jit(solution)/shard_map/rac,rkad->rkcd/dot_general | solution.py:39
  230.0 2.2 copy.62
  232.3 1.2 reshape.109
  233.4 1.2 fusion.25
  234.6 1.0 broadcast_in_dim.16
  235.6 5.0 %scatter_fusion.1 = f32[24,7,1024]{2,1,0:T(8,128)} fusion(f32[24,7,1024]{2,1,0:T(8,128)} %broadcast_in_dim.16, s32[24]{0:T(128)} %copy-done.6, f32[24,7,1024]{2,1,0:T(8,128)S(1)} %fusion.25), kind=kCustom, calls=%fused_computation.5 | custom fusion | bytes 2064480 | tf_op jit(solution)/shard_map/scatter | solution.py:57
  240.6 4.1 %all-to-all-start.3 = ((f32[24,7,1024]{2,1,0:T(8,128)}), f32[24,7,1024]{2,1,0:T(8,128)S(1)}, u32[]{:S(2)}, u32[]{:S(2)}) async-start(f32[24,7,1024]{2,1,0:T(8,128)} %scatter_fusion.1), calls=%async_computation.3 | async-start | bytes 1572864 | tf_op jit(solution)/shard_map/all_to_all | solution.py:118
  244.7 12.6 %all-to-all-done.3 = f32[24,7,1024]{2,1,0:T(8,128)S(1)} async-done(((f32[24,7,1024]{2,1,0:T(8,128)}), f32[24,7,1024]{2,1,0:T(8,128)S(1)}, u32[]{:S(2)}, u32[]{:S(2)}) %all-to-all-start.3) | async-done | bytes 688160 | tf_op jit(solution)/shard_map/all_to_all | solution.py:118
  257.3 0.9 convolution_convert_fusion
  258.2 0.8 copy.48
  (39 shorter events, 2.9 us)
Async XLA Ops:
  7.2 22.0 %collective-permute-start = (bf16[48,8192]{1,0:T(8,128)(2,1)}, bf16[48,8192]{1,0:T(8,128)(2,1)S(1)}, u32[]{:S(2)}, u32[]{:S(2)}) collective-permute-start(bf16[48,8192]{1,0:T(8,128)(2,1)} %param.12), channel_id=1, source_target_pairs={{0,8},{8,16},{16,24},{1,9},{9,17},{17,25},{2,10},{10,18},{18,26},{... | collective-permute-start | bytes 2359304 | tf_op jit(solution)/shard_map/ppermute | solution.py:15
  12.2 21.2 %collective-permute-start.1 = (bf16[48,8192]{1,0:T(8,128)(2,1)}, bf16[48,8192]{1,0:T(8,128)(2,1)}, u32[]{:S(2)}, u32[]{:S(2)}) collective-permute-start(bf16[48,8192]{1,0:T(8,128)(2,1)} %param.12), channel_id=1, source_target_pairs={{8,0},{16,8},{24,16},{9,1},{17,9},{25,17},{10,2},{18,10},{26,18},{... | collective-permute-start | bytes 2359304 | tf_op jit(solution)/shard_map/ppermute | solution.py:17
  17.4 103.7 %all-to-all-start = ((f32[8,1,144]{2,1,0:T(1,128)}), f32[8,1,144]{2,1,0:T(1,128)S(1)}, u32[]{:S(2)}, u32[]{:S(2)}) async-start(f32[8,1,144]{2,1,0:T(1,128)} %reshape.114), calls=%async_computation | async-start | bytes 16384 | tf_op jit(solution)/shard_map/all_to_all | solution.py:101
  41.8 16.0 %copy-start = (bf16[48,128,64]{2,1,0:T(8,128)(2,1)S(1)}, bf16[48,128,64]{2,1,0:T(8,128)(2,1)}, u32[]{:S(2)}) copy-start(bf16[48,128,64]{2,1,0:T(8,128)(2,1)} %reshape.42) | copy-start | bytes 2359300
  121.0 5.0 %copy-start.2 = (bf16[24,2048]{1,0:T(8,128)(2,1)S(1)}, bf16[24,2048]{1,0:T(8,128)(2,1)}, u32[]{:S(2)}) copy-start(bf16[24,2048]{1,0:T(8,128)(2,1)} %param.17) | copy-start | bytes 294916
  121.0 16.8 %copy-start.3 = (s32[24,7]{0,1:T(8,128)S(1)}, s32[24,7]{0,1:T(8,128)}, u32[]{:S(2)}) copy-start(s32[24,7]{0,1:T(8,128)} %param.18) | copy-start | bytes 2020
  121.0 17.0 %copy-start.4 = (s32[24,7]{0,1:T(8,128)S(1)}, s32[24,7]{0,1:T(8,128)}, u32[]{:S(2)}) copy-start(s32[24,7]{0,1:T(8,128)} %param.19) | copy-start | bytes 2020
  121.0 17.7 %copy-start.5 = (s32[24,1]{0,1:T(1,128)S(1)}, s32[24,1]{0,1:T(1,128)}, u32[]{:S(2)}) copy-start(s32[24,1]{0,1:T(1,128)} %param.20) | copy-start | bytes 292
  121.0 18.0 %copy-start.7 = (s32[24]{0:T(128)S(1)}, s32[24]{0:T(128)}, u32[]{:S(2)}) copy-start(s32[24]{0:T(128)} %param.21) | copy-start | bytes 292
  121.1 85.9 %all-to-all-start.1 = ((f32[48,7,4096]{2,1,0:T(8,128)}), f32[48,7,4096]{2,1,0:T(8,128)}, u32[]{:S(2)}, u32[]{:S(2)}) async-start(f32[48,7,4096]{2,1,0:T(8,128)} %scatter_fusion), calls=%async_computation.1 | async-start | bytes 12582912 | tf_op jit(solution)/shard_map/all_to_all | solution.py:100
  126.0 64.1 %all-gather.2.cloned.1.call-start = ((), (), s32[]{:S(2)}) async-start(), calls=%async_computation.4 | async-start | bytes 2654208 | tf_op jit(solution)/shard_map/all_gather | solution.py:109
  126.0 5.9 %collective-permute-start.2 = (bf16[24,2048]{1,0:T(8,128)(2,1)S(1)}, bf16[24,2048]{1,0:T(8,128)(2,1)S(1)}, u32[]{:S(2)}, u32[]{:S(2)}) collective-permute-start(bf16[24,2048]{1,0:T(8,128)(2,1)S(1)} %copy-done.2), channel_id=1, source_target_pairs={{0,8},{8,16},{16,24},{1,9},{9,17},{17,25},{2,10},{10,18},{18,26},{... | collective-permute-start | bytes 294920 | tf_op jit(solution)/shard_map/ppermute | solution.py:15
  129.4 6.6 %collective-permute-start.3 = (bf16[24,2048]{1,0:T(8,128)(2,1)S(1)}, bf16[24,2048]{1,0:T(8,128)(2,1)S(1)}, u32[]{:S(2)}, u32[]{:S(2)}) collective-permute-start(bf16[24,2048]{1,0:T(8,128)(2,1)S(1)} %copy-done.2), channel_id=1, source_target_pairs={{8,0},{16,8},{24,16},{9,1},{17,9},{25,17},{10,2},{18,10},{26,18},{... | collective-permute-start | bytes 294920 | tf_op jit(solution)/shard_map/ppermute | solution.py:17
  139.1 1.9 copy-start.6
  207.0 33.6 %all-to-all-start.2 = ((f32[8,3,12]{2,1,0:T(4,128)}), f32[8,3,12]{2,1,0:T(4,128)S(1)}, u32[]{:S(2)}, u32[]{:S(2)}) async-start(f32[8,3,12]{2,1,0:T(4,128)} %all_to_all.26), calls=%async_computation.2 | async-start | bytes 32768 | tf_op jit(solution)/shard_map/all_to_all | solution.py:119
  210.3 14.4 %copy-start.1 = (bf16[24,64,32]{2,1,0:T(8,128)(2,1)S(1)}, bf16[24,64,32]{2,1,0:T(8,128)(2,1)}, u32[]{:S(2)}) copy-start(bf16[24,64,32]{2,1,0:T(8,128)(2,1)} %reshape.48) | copy-start | bytes 294916
  240.6 16.7 %all-to-all-start.3 = ((f32[24,7,1024]{2,1,0:T(8,128)}), f32[24,7,1024]{2,1,0:T(8,128)S(1)}, u32[]{:S(2)}, u32[]{:S(2)}) async-start(f32[24,7,1024]{2,1,0:T(8,128)} %scatter_fusion.1), calls=%async_computation.3 | async-start | bytes 1572864 | tf_op jit(solution)/shard_map/all_to_all | solution.py:118
Sparse Core Ops, SparseCore 0:
  137.0 53.0 all-gather.1
where the time goes:
time: 268 us; the launch traced here: 266 us
  local copies, waits for them, and re-layouts  90.2 us (34%)
  waiting for transfers between devices  84.4 us (31%)
  matrix products  41.8 us (16%)
  starting transfers between devices  27.2 us (10%)
  between operations  14.2 us (5%)
  other arithmetic  7.92 us (3%)
    all_gather x1, waiting for transfers between devices, local(): collected = lax.all_gather(stacked, 'dom', axis=1, tiled=True)  48.3 us
    reshape x4, local copies, waits for them, and re-layouts, restrict_terms(): term = term.reshape(count, stencil, narrow * narrow)  25.8 us
    dot_general x2, matrix products, restrict_terms(): jnp.einsum('rac,rkad->rkcd', own_rows, product, preferred_element_type=jn...  21.9 us
    scatter x2, local copies, waits for them, and re-layouts, place_into(): jnp.zeros((slots,) + values.shape[1:], values.dtype).at[position]  17.3 us
    reshape x1, local copies, waits for them, and re-layouts, local(): picked = nearby_rows[index].reshape(rows, stencil, width, narrow)  16 us
    all_to_all x1, waiting for transfers between devices, local(): lax.all_to_all(sent2, 'dom', split_axis=0, concat_axis=0, tiled=True)  12.6 us
    all_to_all x1, waiting for transfers between devices, local(): lax.all_to_all(sent, 'dom', split_axis=0, concat_axis=0, tiled=True)  11.2 us
    dot_general x2, matrix products, restrict_terms(): jnp.einsum('rks,rkx->rsx', choose, term, precision=lax.Precision.HIGHEST)  9.63 us
  transfers between devices with their start and end apart: 9, of which 7 were waited for; matrix products, arithmetic and copies ran while one was open for 52% of the time, Pallas kernels for 0%

commit v1 on v0

v1 whole, which is shorter than its diff:
```python
import functools

import jax
import jax.numpy as jnp
from jax import lax
from jax.experimental import pallas as pl
from jax.experimental.pallas import tpu as pltpu
from jax.sharding import PartitionSpec as P

BF16 = jnp.bfloat16
F32 = jnp.float32
I32 = jnp.int32
LANES = 128
VMEM_LIMIT = 48 * 1024 * 1024


def vmem():
    return pl.BlockSpec(memory_space=pltpu.VMEM)


def smem():
    return pl.BlockSpec(memory_space=pltpu.SMEM)


def hbm():
    return pl.BlockSpec(memory_space=pl.ANY)


def params():
    return pltpu.CompilerParams(vmem_limit_bytes=VMEM_LIMIT)


def low_lanes(shape, bound):
    return lax.broadcasted_iota(I32, shape, len(shape) - 1) < bound


def exchange(cells, axis, offset):
    count = lax.axis_size(axis)
    return lax.ppermute(cells, axis, [(i, i ^ offset) for i in range(count)])


def neighbours(cells, axis):
    count = lax.axis_size(axis)
    previous = lax.ppermute(cells, axis, [(i, i + 1) for i in range(count - 1)])
    following = lax.ppermute(cells, axis, [(i + 1, i) for i in range(count - 1)])
    return previous, following


def halves_kernel(flat_ref, out_ref, wide_ref):
    rows = flat_ref.shape[0]
    deep = flat_ref.shape[1] // LANES
    half = deep // 2
    group = 16
    left = low_lanes((group, LANES), LANES // 2)
    for g in range(rows // group):
        for t in range(half):
            upper = flat_ref[pl.ds(g * group, group), pl.ds(t * LANES, LANES)].astype(F32)
            lower = flat_ref[pl.ds(g * group, group), pl.ds((t + half) * LANES, LANES)].astype(F32)
            even = jnp.where(left, upper, pltpu.roll(lower, LANES // 2, 1))
            odd = jnp.where(left, pltpu.roll(upper, LANES // 2, 1), lower)
            wide_ref[pl.ds(g * group * deep + 2 * t, group, stride=deep), :] = even
            wide_ref[pl.ds(g * group * deep + 2 * t + 1, group, stride=deep), :] = odd
    for r in range(rows):
        out_ref[r] = wide_ref[pl.ds(r * deep, deep), :].astype(BF16)


def halves(flat):
    rows, size = flat.shape
    deep = size // LANES
    return pl.pallas_call(
        halves_kernel,
        out_shape=jax.ShapeDtypeStruct((rows, deep, LANES), BF16),
        in_specs=[vmem()],
        out_specs=vmem(),
        scratch_shapes=[pltpu.VMEM((rows * deep, LANES), F32)],
        compiler_params=params(),
    )(flat)


def index_kernel(
    where_ref,
    cols_ref,
    slot_ref,
    owner_ref,
    place_ref,
    slot2_ref,
    owner2_ref,
    place2_ref,
    source_ref,
    near_ref,
    target_ref,
    source2_ref,
    count_ref,
    *,
    parts,
    capacity,
    capacity2,
    owned,
    owned2,
):
    region = where_ref[0]
    dom = where_ref[1]
    stencil, rows = cols_ref.shape
    rows2 = slot2_ref.shape[1]
    span = parts * rows
    first = region * span
    slots = parts * capacity
    slots2 = parts * capacity2

    def clear_counts(d, carry):
        count_ref[d] = 0
        return carry

    if slots > rows or slots2 > rows2:

        def clear(p, carry):
            source_ref[p] = 0
            for k in range(stencil):
                near_ref[p * stencil + k] = 0
                target_ref[p * stencil + k] = -1
            return carry

        lax.fori_loop(0, slots, clear, 0)

        def clear2(p, carry):
            source2_ref[p] = 0
            for k in range(stencil):
                target_ref[(slots + p) * stencil + k] = -1
            return carry

        lax.fori_loop(0, slots2, clear2, 0)
    lax.fori_loop(0, parts, clear_counts, 0)

    def fine(i, carry):
        owner = owner_ref[i]
        rank = count_ref[owner]
        count_ref[owner] = rank + 1
        here = (owner ^ dom) * capacity + rank
        there = (owner * capacity + rank) * stencil
        place = place_ref[i]
        source_ref[here] = i
        for k in range(stencil):
            col = cols_ref[k, i]
            step = jnp.where(col < first, 0, jnp.where(col >= first + span, 2, 1))
            begin = ((region + step - 1) * parts + dom) * rows
            near_ref[here * stencil + k] = step * rows + col - begin
            target_ref[there + k] = slot_ref[k, i] * owned + place
        return carry

    lax.fori_loop(0, rows, fine, 0)
    lax.fori_loop(0, parts, clear_counts, 0)

    def coarse(i, carry):
        owner = owner2_ref[i]
        rank = count_ref[owner]
        count_ref[owner] = rank + 1
        source2_ref[(owner ^ dom) * capacity2 + rank] = i
        there = (slots + owner * capacity2 + rank) * stencil
        place = place2_ref[i]
        for k in range(stencil):
            target_ref[there + k] = place * (stencil + 1) + slot2_ref[k, i]
        return carry

    lax.fori_loop(0, rows2, coarse, 0)


def terms_kernel(
    source_ref,
    near_ref,
    blocks_ref,
    before_ref,
    own_ref,
    after_ref,
    *rest,
    offsets,
    capacity,
):
    outs = rest[: len(offsets)]
    table_ref, buffer_ref, table_sem, row_sem = rest[len(offsets) :]
    rows = own_ref.shape[0]
    stencil, width = buffer_ref.shape[1], buffer_ref.shape[2]
    half = width // 2
    narrow = LANES // 2
    flat = narrow * narrow // LANES
    for n, part in enumerate((before_ref, own_ref, after_ref)):
        pltpu.make_async_copy(part, table_ref.at[pl.ds(n * rows, rows)], table_sem.at[n]).start()

    def row_copy(n, slot):
        return pltpu.make_async_copy(blocks_ref.at[source_ref[slot]], buffer_ref.at[n], row_sem.at[n])

    for n, offset in enumerate(offsets):
        for r in range(capacity):
            row_copy(n * capacity + r, offset * capacity + r).start()
    for n, part in enumerate((before_ref, own_ref, after_ref)):
        pltpu.make_async_copy(part, table_ref.at[pl.ds(n * rows, rows)], table_sem.at[n]).wait()

    left = low_lanes((half, LANES), narrow)
    left_flat = low_lanes((flat, LANES), narrow)
    out_row = lax.broadcasted_iota(I32, (narrow, LANES), 0)
    in_col = lax.broadcasted_iota(I32, (narrow, LANES), 1)
    chosen = jnp.where(out_row < flat, 2 * out_row, 2 * (out_row - flat) + 1)
    pick = jnp.where(in_col == chosen, 1.0, 0.0).astype(BF16)
    zero = jnp.zeros((half, LANES), BF16)

    def one_row(n, slot, out_ref, r):
        row_copy(n, slot).wait()
        mine = own_half = table_ref[rows + source_ref[slot]]
        column = jnp.concatenate([mine, pltpu.roll(own_half, narrow, 1)], axis=0)
        turned = lax.dot_general(
            pick, column, (((1,), (1,)), ((), ())), preferred_element_type=F32
        ).astype(BF16)
        products = []
        for k in range(0, stencil, 2):
            one = table_ref[near_ref[slot * stencil + k]]
            weights = [jnp.where(left, one, zero), jnp.where(left, pltpu.roll(one, narrow, 1), zero)]
            lhs = buffer_ref[n, k]
            if k + 1 < stencil:
                two = table_ref[near_ref[slot * stencil + k + 1]]
                weights += [jnp.where(left, zero, pltpu.roll(two, narrow, 1)), jnp.where(left, zero, two)]
                lhs = jnp.concatenate([lhs, buffer_ref[n, k + 1]], axis=1)
            products.append(
                jnp.dot(lhs, jnp.concatenate(weights, axis=0), preferred_element_type=F32).astype(BF16)
            )
        term = jnp.dot(turned, jnp.concatenate(products, axis=1), preferred_element_type=F32)
        for k in range(0, stencil, 2):
            pair = term[:, k // 2 * LANES : (k // 2 + 1) * LANES]
            even = pair[:flat]
            odd = pair[flat:]
            base = (r * stencil + k) * flat
            out_ref[pl.ds(base, flat), :] = jnp.where(left_flat, even, pltpu.roll(odd, narrow, 1)).astype(BF16)
            if k + 1 < stencil:
                out_ref[pl.ds(base + flat, flat), :] = jnp.where(
                    left_flat, pltpu.roll(even, narrow, 1), odd
                ).astype(BF16)

    for n, offset in enumerate(offsets):

        def body(r, carry, n=n, offset=offset):
            one_row(n * capacity + r, offset * capacity + r, outs[n], r)
            return carry

        lax.fori_loop(0, capacity, body, 0)


def level_one(source, near, blocks, before, own, after, offsets, capacity):
    rows, stencil, width, _ = blocks.shape
    narrow = LANES // 2
    flat = narrow * narrow // LANES
    shape = jax.ShapeDtypeStruct((capacity * stencil * flat, LANES), BF16)
    count = len(offsets) * capacity
    return pl.pallas_call(
        functools.partial(terms_kernel, offsets=offsets, capacity=capacity),
        out_shape=tuple(shape for _ in offsets),
        in_specs=[smem(), smem(), hbm(), hbm(), hbm(), hbm()],
        out_specs=tuple(vmem() for _ in offsets),
        scratch_shapes=[
            pltpu.VMEM((3 * rows,) + own.shape[1:], BF16),
            pltpu.VMEM((count, stencil, width, width), BF16),
            pltpu.SemaphoreType.DMA((3,)),
            pltpu.SemaphoreType.DMA((count,)),
        ],
        compiler_params=params(),
    )(source, near, blocks, before, own, after)


def owner_kernel(
    where_ref,
    target_ref,
    source2_ref,
    weights_ref,
    own_ref,
    *rest,
    parts,
    capacity,
    capacity2,
    owned,
    stencil,
):
    arrived = rest[:parts]
    out_ref = rest[parts]
    sends = rest[parts + 1 : 2 * parts + 1]
    (sum_ref,) = rest[2 * parts + 1 :]
    dom = where_ref[1]
    flat = sum_ref.shape[1]
    narrow = LANES // 2
    sum_ref[...] = jnp.zeros(sum_ref.shape, F32)
    for d in range(parts):
        part_ref = arrived[d]

        def add(r, carry, d=d, part_ref=part_ref):
            base = (dom * capacity + r) * stencil
            for k in range(stencil):
                target = target_ref[dom ^ d, base + k]
                value = part_ref[pl.ds((r * stencil + k) * flat, flat), :].astype(F32)

                @pl.when(target >= 0)
                def _():
                    sum_ref[target] += value

            return carry

        lax.fori_loop(0, capacity, add, 0)

    left = low_lanes((flat, LANES), narrow)
    quarter = LANES // 4
    eighth = lax.broadcasted_iota(I32, (8, LANES), 1) // quarter

    for d in range(parts):
        send_ref = sends[d]

        def second(r, carry, d=d, send_ref=send_ref):
            q = source2_ref[d * capacity2 + r]
            rows = []
            for k in range(0, stencil, 2):
                one = sum_ref[k * owned + q].astype(BF16)
                if k + 1 < stencil:
                    two = sum_ref[(k + 1) * owned + q].astype(BF16)
                else:
                    two = jnp.zeros((flat, LANES), BF16)
                even = jnp.where(left, one, pltpu.roll(two, narrow, 1))
                odd = jnp.where(left, pltpu.roll(one, narrow, 1), two)
                rows.append(jnp.concatenate([even, odd], axis=0))
            own = own_ref[q]
            groups = []
            for g in range((stencil + 3) // 4):
                lhs = jnp.concatenate(rows[2 * g : 2 * g + 2], axis=1)
                product = jnp.dot(lhs, weights_ref[q, g], preferred_element_type=F32).astype(BF16)
                groups.append(product)
            term = jnp.dot(own, jnp.concatenate(groups, axis=1), preferred_element_type=F32)
            for k in range(stencil):
                g = k // 4
                total = None
                for w in range(4):
                    piece = term[w * 8 : (w + 1) * 8, g * LANES : (g + 1) * LANES]
                    shift = (w - k) % 4 * quarter
                    if shift:
                        piece = pltpu.roll(piece, shift, 1)
                    total = piece if total is None else jnp.where(eighth == w, piece, total)
                send_ref[pl.ds((r * stencil + k) * 8, 8), :] = total
            return carry

        lax.fori_loop(0, capacity2, second, 0)
    for s in range(stencil * owned):
        out_ref[s] = sum_ref[s].astype(BF16)


def owner_level(where, targets, source2, weights, own, arrived, parts, capacity, capacity2, owned, stencil):
    flat = LANES // 4
    send = jax.ShapeDtypeStruct((capacity2 * stencil * 8, LANES), F32)
    return pl.pallas_call(
        functools.partial(
            owner_kernel, parts=parts, capacity=capacity, capacity2=capacity2, owned=owned, stencil=stencil
        ),
        out_shape=(jax.ShapeDtypeStruct((stencil * owned, flat, LANES), BF16),) + (send,) * parts,
        in_specs=[smem(), smem(), smem()] + [vmem()] * (2 + parts),
        out_specs=(vmem(),) * (1 + parts),
        scratch_shapes=[pltpu.VMEM((stencil * owned, flat, LANES), F32)],
        compiler_params=params(),
    )(where, targets, source2, weights, own, *arrived)


def final_kernel(where_ref, target_ref, *rest, parts, first, capacity2, stencil):
    arrived = rest[:parts]
    out_ref = rest[parts]
    (sum_ref,) = rest[parts + 1 :]
    dom = where_ref[1]
    deep = stencil + 1
    sum_ref[...] = jnp.zeros(sum_ref.shape, F32)
    for d in range(parts):
        for r in range(capacity2):
            base = (first + dom * capacity2 + r) * stencil
            for k in range(stencil):
                target = target_ref[dom ^ d, base + k]
                value = arrived[d][pl.ds((r * stencil + k) * 8, 8), :].astype(F32)

                @pl.when(target >= 0)
                def _(target=target, value=value):
                    sum_ref[pl.ds(target * 8, 8), :] += value

    for u in range(out_ref.shape[0]):
        for t in range(8):
            tile = sum_ref[pl.ds(u * deep * 8 + t, deep, stride=8), :]
            out_ref[u, :, pl.ds(t * LANES, LANES)] = tile[:stencil].astype(BF16)


def final_level(where, targets, arrived, parts, first, capacity2, owned2, stencil):
    return pl.pallas_call(
        functools.partial(final_kernel, parts=parts, first=first, capacity2=capacity2, stencil=stencil),
        out_shape=jax.ShapeDtypeStruct((owned2, stencil, 8 * LANES), BF16),
        in_specs=[smem(), smem()] + [vmem()] * parts,
        out_specs=vmem(),
        scratch_shapes=[pltpu.VMEM((owned2 * (stencil + 1) * 8, LANES), F32)],
        compiler_params=params(),
    )(where, targets, *arrived)


def chunks_of(parts):
    order = list(range(parts - 1, -1, -1))
    return [tuple(order[i : i + 2]) for i in range(0, parts, 2)]


def local(
    fine_blocks,
    interp,
    fine_cols,
    fine_slot,
    fine_owner,
    fine_place,
    coarse_interp,
    coarse_cols,
    coarse_slot,
    coarse_owner,
    coarse_place,
):
    rows, stencil, width, _ = fine_blocks.shape
    narrow = interp.shape[1] // width
    narrow2 = coarse_interp.shape[1] // narrow
    parts = lax.axis_size("dom")
    region = lax.axis_index("region")
    dom = lax.axis_index("dom")
    owned = rows // 2
    owned2 = owned // 2
    capacity = max(2, rows // 8)
    capacity2 = max(2, owned // 8)
    slots = parts * capacity
    slots2 = parts * capacity2
    where = jnp.stack([region, dom]).astype(I32)

    coarse_before, coarse_after = neighbours(coarse_interp, "region")
    own = halves(interp)
    before, after = neighbours(own, "region")

    source, near, target, source2 = pl.pallas_call(
        functools.partial(
            index_kernel, parts=parts, capacity=capacity, capacity2=capacity2, owned=owned, owned2=owned2
        ),
        out_shape=(
            jax.ShapeDtypeStruct((slots,), I32),
            jax.ShapeDtypeStruct((slots * stencil,), I32),
            jax.ShapeDtypeStruct(((slots + slots2) * stencil,), I32),
            jax.ShapeDtypeStruct((slots2,), I32),
        ),
        in_specs=[smem()] * 8,
        out_specs=(smem(),) * 4,
        scratch_shapes=[pltpu.SMEM((parts,), I32)],
    )(
        where,
        fine_cols.T,
        fine_slot.T,
        fine_owner[:, 0],
        fine_place,
        coarse_slot.T,
        coarse_owner[:, 0],
        coarse_place,
    )

    size2 = coarse_interp.shape[1]
    extra = 8 * pl.cdiv(target.shape[0], 8 * size2)
    codes = jnp.pad(target, (0, extra * size2 - target.shape[0])).astype(BF16).reshape(extra, size2)
    stacked = jnp.concatenate([coarse_before, coarse_interp, coarse_after, codes], axis=0)
    collected = lax.all_gather(stacked, "dom", axis=0, tiled=False)
    targets = collected[:, 3 * owned :].reshape(parts, extra * size2)[:, : target.shape[0]].astype(I32)
    span2 = parts * owned
    inside = coarse_cols % span2
    index2 = (inside // owned) * (3 * owned + extra) + (coarse_cols // span2 - region + 1) * owned + inside % owned
    picked = collected.reshape(parts * (3 * owned + extra), size2)[index2.reshape(-1)]
    picked = picked.reshape(owned, stencil, narrow, narrow2)
    groups = (stencil + 3) // 4
    picked = jnp.pad(picked, ((0, 0), (0, 4 * groups - stencil), (0, 0), (0, 0)))
    picked = picked.reshape(owned, groups, 4, narrow, 1, narrow2)
    corner = jnp.eye(4, dtype=jnp.bool_).reshape(1, 1, 4, 1, 4, 1)
    weights = jnp.where(corner, picked, jnp.zeros((), BF16)).reshape(owned, groups, 4 * narrow, 4 * narrow2)
    turned = coarse_interp.reshape(owned, narrow // 2, 2, narrow2 // 4, 4)
    turned = turned.transpose(0, 4, 3, 2, 1).reshape(owned, narrow2, narrow)

    arrived = [None] * parts
    for offsets in chunks_of(parts):
        sent = level_one(source, near, fine_blocks, before, own, after, offsets, capacity)
        for offset, cells in zip(offsets, sent):
            arrived[offset] = exchange(cells, "dom", offset) if offset else cells
    outs = owner_level(
        where, targets, source2, weights, turned, arrived, parts, capacity, capacity2, owned, stencil
    )
    coarse_blocks = outs[0].reshape(stencil, owned, narrow * narrow).transpose(1, 0, 2)
    arrived2 = [exchange(cells.astype(BF16), "dom", d) if d else cells for d, cells in enumerate(outs[1:])]
    second = final_level(where, targets, arrived2, parts, slots, capacity2, owned2, stencil)
    return (coarse_blocks, second)


def solution(mesh):
    in_specs = (
        P(("region", "dom"), None, None, None),
        P(("region", "dom"), None),
        P(("region", "dom"), None),
        P(("region", "dom"), None),
        P(("region", "dom"), None),
        P(("region", "dom")),
        P(("region", "dom"), None),
        P(("region", "dom"), None),
        P(("region", "dom"), None),
        P(("region", "dom"), None),
        P(("region", "dom")),
    )
    out_specs = (P(("region", "dom"), None, None), P(("region", "dom"), None, None))
    return jax.shard_map(local, mesh=mesh, in_specs=in_specs, out_specs=out_specs, check_vma=False)
```

time: 268 us -> 188 us (0.70)
  Pallas kernels: 0 us -> 59.1 us
  waiting for transfers between devices: 84.4 us -> 32.8 us
  local copies, waits for them, and re-layouts: 90.2 us -> 48.2 us
  matrix products: 41.8 us -> 0 us
    pallas_call x0 -> x8, Pallas kernels: none -> 59.1 us  [the longest x4 32.8 us: level_one(): pl.pallas_call(functools.partial(terms_kernel, offsets=offsets, capacity=...]
    all_gather x1, waiting for transfers between devices: 48.3 us -> 0.01 us  [local(): collected = lax.all_gather(stacked, 'dom', axis=0, tiled=False)]
    reshape x9 -> x5, local copies, waits for them, and re-layouts: 53.3 us -> 6.18 us  [the longest x1 3.18 us: local(): picked = picked.reshape(owned, stencil, narrow, narrow2)]
    dot_general x6 -> x0, matrix products: 41.8 us -> none  [the longest x2 21.9 us: restrict_terms(): jnp.einsum('rac,rkad->rkcd', own_rows, product, preferred_element_type=jn...]
    all_to_all x4 -> x0, waiting for transfers between devices: 23.8 us -> none  [the longest x1 12.6 us: local(): lax.all_to_all(sent2, 'dom', split_axis=0, concat_axis=0, tiled=True)]
    ppermute x4 -> x18, waiting for transfers between devices: 12.3 us -> 32.8 us  [the longest x14 14.6 us: exchange(): return lax.ppermute(cells, axis, [(i, i ^ offset) for i in range(count)])]
    broadcast_in_dim x4 -> x7, local copies, waits for them, and re-layouts: 4.61 us -> 24.2 us  [local(): jnp.where(corner, picked, jnp.zeros((), BF16))]
    scatter x2 -> x0, local copies, waits for them, and re-layouts: 17.3 us -> none  [place_into(): jnp.zeros((slots,) + values.shape[1:], values.dtype).at[position]]
  transfers between devices with their start and end apart: 9 -> 19, of which waited for: 7 -> 6; matrix products, arithmetic and copies ran while one was open for 52% -> 26% of each run, Pallas kernels for 0% -> 21%
where the time goes in v1:
time: 188 us; the launch traced here: 187 us
  Pallas kernels  59.1 us (31%)
  local copies, waits for them, and re-layouts  48.2 us (26%)
  waiting for transfers between devices  32.8 us (17%)
  starting transfers between devices  25.1 us (13%)
  between operations  14.3 us (8%)
  other arithmetic  7.43 us (4%)
    pallas_call x4, Pallas kernels, level_one(): pl.pallas_call(functools.partial(terms_kernel, offsets=offsets, capacity=...  32.8 us
    broadcast_in_dim x7, local copies, waits for them, and re-layouts, local(): jnp.where(corner, picked, jnp.zeros((), BF16))  24.2 us
    pallas_call x1, Pallas kernels, owner_level(): pl.pallas_call(functools.partial(owner_kernel, parts=parts, capacity=capa...  16.8 us
    ppermute x14, waiting for transfers between devices, exchange(): return lax.ppermute(cells, axis, [(i, i ^ offset) for i in range(count)])  14.6 us
    ppermute x2, waiting for transfers between devices, neighbours(): previous = lax.ppermute(cells, axis, [(i, i + 1) for i in range(count - 1)])  14 us
    ppermute x14, starting transfers between devices, exchange(): return lax.ppermute(cells, axis, [(i, i ^ offset) for i in range(count)])  13 us
    ppermute x2, starting transfers between devices, neighbours(): previous = lax.ppermute(cells, axis, [(i, i + 1) for i in range(count - 1)])  9.53 us
    unnamed x28, local copies, waits for them, and re-layouts  5.87 us
  transfers between devices with their start and end apart: 19, of which 6 were waited for; matrix products, arithmetic and copies ran while one was open for 26% of the time, Pallas kernels for 21%

profile of v1, /device:TPU:0, one launch (start us, length us, event | category | flops | bytes accessed | tf_op | source)
XLA Modules:
  0.0 187.0 jit_solution(8495058350778627956)
XLA Ops:
  7.2 1.3 collective-permute-start.1
  8.5 5.6 %collective-permute-start = (bf16[24,2048]{1,0:T(8,128)(2,1)}, bf16[24,2048]{1,0:T(8,128)(2,1)S(1)}, u32[]{:S(2)}, u32[]{:S(2)}) collective-permute-start(bf16[24,2048]{1,0:T(8,128)(2,1)} %param.17), channel_id=1, source_target_pairs={{0,8},{8,16},{16,24},{1,9},{9,17},{17,25},{2,10},{10,18},{18,26},{... | collective-permute-start | bytes 294920 | tf_op jit(solution)/shard_map/ppermute | solution.py:44
  14.1 0.6 pad_add_fusion.where_ref
  14.7 4.5 %shard_map.122 = (s32[48]{0:T(128)}, s32[336]{0:T(512)}, s32[504]{0:T(512)}, s32[24]{0:T(128)}) custom-call(s32[2]{0:T(128)} %pad_add_fusion.where_ref, s32[7,48]{1,0:T(8,128)} %bitcast.25, s32[7,48]{1,0:T(8,128)} %bitcast.26, s32[48]{0:T(128)} %bitcast.28, s32[48]{0:T(128)} %place_ref.1, s32[7,24]{1,0:T(8,128)} %bitcast.27, s32[24]{0:T(128)} %bitcast.29, ...), custom_call_target="tpu_custom_call" | custom-call | tf_op jit(solution)/shard_map/pallas_call | solution.py:433
  19.2 0.7 convert.4
  19.9 1.6 pad_maximum_fusion
  21.6 1.1 copy-done
  22.7 1.5 shard_map.123.own_ref
  24.2 4.0 %collective-permute-start.2 = (bf16[48,64,128]{2,1,0:T(8,128)(2,1)S(1)}, bf16[48,64,128]{2,1,0:T(8,128)(2,1)S(1)}, u32[]{:S(2)}, u32[]{:S(2)}) collective-permute-start(bf16[48,64,128]{2,1,0:T(8,128)(2,1)S(1)} %shard_map.123.own_ref), channel_id=1, source_target_pairs={{0,8},{8,16},{16,24},{1,9},{9,17},{17,25},{2,10},{10,18},{18,26},{... | collective-permute-start | bytes 2359304 | tf_op jit(solution)/shard_map/ppermute | solution.py:44
  28.2 1.3 collective-permute-start.3
  29.5 0.7 fusion.2
  30.4 14.0 %collective-permute-done.2.before_ref = bf16[48,64,128]{2,1,0:T(8,128)(2,1)S(1)} collective-permute-done((bf16[48,64,128]{2,1,0:T(8,128)(2,1)S(1)}, bf16[48,64,128]{2,1,0:T(8,128)(2,1)S(1)}, u32[]{:S(2)}, u32[]{:S(2)}) %collective-permute-start.2) | collective-permute-done | bytes 786464 | tf_op jit(solution)/shard_map/ppermute | solution.py:44
  44.3 4.2 %collective-permute-done.3.after_ref = bf16[48,64,128]{2,1,0:T(8,128)(2,1)S(1)} collective-permute-done((bf16[48,64,128]{2,1,0:T(8,128)(2,1)S(1)}, bf16[48,64,128]{2,1,0:T(8,128)(2,1)S(1)}, u32[]{:S(2)}, u32[]{:S(2)}) %collective-permute-start.3) | collective-permute-done | bytes 786464 | tf_op jit(solution)/shard_map/ppermute | solution.py:45
  48.5 0.7 copy-done.1
  49.2 0.6 copy-done.3
  49.8 8.4 %shard_map.124 = (bf16[1344,128]{1,0:T(8,128)(2,1)}, bf16[1344,128]{1,0:T(8,128)(2,1)S(1)}) custom-call(s32[48]{0:T(128)S(1)} %copy-done.3, s32[336]{0:T(512)S(1)} %copy-done.1, bf16[48,7,128,128]{3,2,1,0:T(8,128)(2,1)} %blocks_ref.7, bf16[48,64,128]{2,1,0:T(8,128)(2,1)S(1)} %collective-permute-done.2.before_ref, ...), custom_call_target="tpu_custom_call" | custom-call | tf_op jit(solution)/shard_map/pallas_call | solution.py:251
  58.3 8.4 %shard_map.125 = (bf16[1344,128]{1,0:T(8,128)(2,1)S(1)}, bf16[1344,128]{1,0:T(8,128)(2,1)}) custom-call(s32[48]{0:T(128)S(1)} %copy-done.3, s32[336]{0:T(512)S(1)} %copy-done.1, bf16[48,7,128,128]{3,2,1,0:T(8,128)(2,1)} %blocks_ref.7, bf16[48,64,128]{2,1,0:T(8,128)(2,1)S(1)} %collective-permute-done.2.before_ref, ...), custom_call_target="tpu_custom_call" | custom-call | tf_op jit(solution)/shard_map/pallas_call | solution.py:251
  66.7 0.7 copy-done.7
  67.4 1.5 collective-permute-start.5
  68.9 1.0 copy.20
  70.3 2.6 %copy.21 = bf16[24,4,8,2,32]{4,3,2,1,0:T(2,128)(2,1)} copy(bf16[24,4,8,2,32]{0,1,2,3,4:T(4,128)(2,1)} %bitcast.21) | data formatting | bytes 196608 | tf_op jit(solution)/shard_map/transpose | solution.py:474
  72.9 1.2 reshape.75.own_ref
  74.2 0.4 collective-permute-start.6
  74.6 8.4 %shard_map.126 = (bf16[1344,128]{1,0:T(8,128)(2,1)}, bf16[1344,128]{1,0:T(8,128)(2,1)}) custom-call(s32[48]{0:T(128)S(1)} %copy-done.4, s32[336]{0:T(512)S(1)} %copy-done.2, bf16[48,7,128,128]{3,2,1,0:T(8,128)(2,1)} %blocks_ref.7, bf16[48,64,128]{2,1,0:T(8,128)(2,1)S(1)} %collective-permute-done.2.before_ref, bf16[48,64,128]{2,1,0:T(8,128)(2,1)S(1)} %shard_map.123.own_ref, ...), custom_call_target="tpu_custom_call" | custom-call | tf_op jit(solution)/shard_map/pallas_call | solution.py:251
  83.0 1.6 collective-permute-start.7
  84.8 7.7 %shard_map.127 = (bf16[1344,128]{1,0:T(8,128)(2,1)S(1)}, bf16[1344,128]{1,0:T(8,128)(2,1)S(1)}) custom-call(s32[48]{0:T(128)S(1)} %copy-done.4, s32[336]{0:T(512)S(1)} %copy-done.2, bf16[48,7,128,128]{3,2,1,0:T(8,128)(2,1)} %blocks_ref.7, bf16[48,64,128]{2,1,0:T(8,128)(2,1)S(1)} %collective-permute-done.2.before_ref, ...), custom_call_target="tpu_custom_call" | custom-call | tf_op jit(solution)/shard_map/pallas_call | solution.py:251
  92.4 0.7 copy-done.8
  93.2 0.8 copy-done.10
  93.9 1.0 slice.10
  95.1 3.8 %gather_fusion = bf16[168,2048]{1,0:T(8,128)(2,1)S(1)} fusion(bf16[640,2048]{1,0:T(8,128)(2,1)} %all-gather.3.cloned.1.call-done, s32[1024]{0:T(1024)S(1)} %pad_clamp_fusion), kind=kCustom, calls=%fused_computation | custom fusion | bytes 1376928 | tf_op jit(solution)/shard_map/gather | solution.py:466
  98.9 3.2 %reshape.73 = bf16[24,7,64,32]{3,2,1,0:T(8,128)(2,1)} reshape(bf16[168,2048]{1,0:T(8,128)(2,1)S(1)} %gather_fusion) | data formatting | bytes 1376256 | tf_op jit(solution)/shard_map/reshape | solution.py:467
  102.1 4.4 %pad.10 = bf16[24,8,64,32]{3,2,1,0:T(8,128)(2,1)} pad(bf16[24,7,64,32]{3,2,1,0:T(8,128)(2,1)} %reshape.73, bf16[]{:T(256)} %constant.44.clone.1), padding=0_0x0_1x0_0x0_0 | pad | bytes 1474562 | tf_op jit(solution)/shard_map/jit(_pad)/pad | solution.py:469
  106.5 3.4 %copy.18 = bf16[24,2,4,64,32]{3,2,4,1,0:T(4,128)(2,1)S(1)} copy(bf16[24,2,4,64,32]{4,3,2,1,0:T(8,128)(2,1)} %bitcast.20) | data formatting | bytes 1572864 | tf_op jit(solution)/shard_map/jit(_where)/broadcast_in_dim | solution.py:472
  109.9 5.8 %broadcast_in_dim.33 = bf16[24,2,4,64,4,32]{3,2,5,4,1,0:T(4,128)(2,1)} broadcast(bf16[24,2,4,64,32]{3,2,4,1,0:T(4,128)(2,1)S(1)} %copy.18), dimensions={0,1,2,3,5} | broadcast | bytes 3932160 | tf_op jit(solution)/shard_map/jit(_where)/broadcast_in_dim | solution.py:472
  115.7 10.0 %broadcast_in_dim.34 = bf16[24,2,256,128]{2,3,1,0:T(8,128)(2,1)} reshape(bf16[24,2,4,64,4,32]{3,2,5,4,1,0:T(4,128)(2,1)} %broadcast_in_dim.33) | data formatting | bytes 6291456 | tf_op jit(solution)/shard_map/jit(_where)/broadcast_in_dim | solution.py:472
  125.7 4.7 %copy.19 = bf16[24,2,256,128]{3,2,1,0:T(8,128)(2,1)} copy(bf16[24,2,256,128]{2,3,1,0:T(8,128)(2,1)} %broadcast_in_dim.34) | data formatting | bytes 6291456 | tf_op jit(solution)/shard_map/jit(_where)/broadcast_in_dim | solution.py:472
  130.4 2.5 %collective-permute-start.9 = (bf16[1344,128]{1,0:T(8,128)(2,1)S(1)}, bf16[1344,128]{1,0:T(8,128)(2,1)S(1)}, u32[]{:S(2)}, u32[]{:S(2)}) collective-permute-start(bf16[1344,128]{1,0:T(8,128)(2,1)S(1)} %copy-done.11), channel_id=1, source_target_pairs={{0,6},{1,7},{2,4},{3,5},{4,2},{5,3},{6,0},{7,1},{8,14},{9,15},{10,... | collective-permute-start | bytes 1032200 | tf_op jit(solution)/shard_map/ppermute | solution.py:39
  133.3 3.7 %broadcast_select_fusion.weights_ref = bf16[24,2,256,128]{3,2,1,0:T(8,128)(2,1)} fusion(bf16[24,2,256,128]{3,2,1,0:T(8,128)(2,1)} %copy.19, pred[256,128]{1,0:T(8,128)(4,1)S(1)} %copy.16), kind=kLoop, calls=%fused_computation.1 | loop fusion | flops 1572864 | bytes 6324224 | tf_op jit(solution)/shard_map/jit(_where)/select_n | solution.py:472
  137.0 5.2 %collective-permute-done.9.rest_6_ = bf16[1344,128]{1,0:T(8,128)(2,1)S(1)} collective-permute-done((bf16[1344,128]{1,0:T(8,128)(2,1)S(1)}, bf16[1344,128]{1,0:T(8,128)(2,1)S(1)}, u32[]{:S(2)}, u32[]{:S(2)}) %collective-permute-start.9) | collective-permute-done | bytes 344096 | tf_op jit(solution)/shard_map/ppermute | solution.py:39
  142.2 6.6 %collective-permute-done.10.rest_7_ = bf16[1344,128]{1,0:T(8,128)(2,1)S(1)} collective-permute-done((bf16[1344,128]{1,0:T(8,128)(2,1)S(1)}, bf16[1344,128]{1,0:T(8,128)(2,1)S(1)}, u32[]{:S(2)}, u32[]{:S(2)}) %collective-permute-start.10) | collective-permute-done | bytes 344096 | tf_op jit(solution)/shard_map/ppermute | solution.py:39
  148.8 16.8 %shard_map.128 = (bf16[168,32,128]{2,1,0:T(8,128)(2,1)S(1)}, f32[168,128]{1,0:T(8,128)S(1)}, f32[168,128]{1,0:T(8,128)S(1)}, f32[168,128]{1,0:T(8,128)S(1)}, f32...) custom-call(s32[2]{0:T(128)S(1)} %copy-done.5, ...), custom_call_target="tpu_custom_call" | custom-call | tf_op jit(solution)/shard_map/pallas_call | solution.py:350
  165.9 1.5 collective-permute-start.12
  167.6 1.5 collective-permute-start.14
  169.5 2.5 %collective-permute-start.16 = (bf16[168,128]{1,0:T(8,128)(2,1)S(1)}, bf16[168,128]{1,0:T(8,128)(2,1)S(1)}, u32[]{:S(2)}, u32[]{:S(2)}) collective-permute-start(bf16[168,128]{1,0:T(8,128)(2,1)S(1)} %convert_element_type.33), channel_id=1, source_target_pairs={{0,6},{1,7},{2,4},{3,5},{4,2},{5,3},{6,0},{7,1},{8,14},{9,15},{10,... | collective-permute-start | bytes 129032 | tf_op jit(solution)/shard_map/ppermute | solution.py:39
  172.1 1.7 reshape.76
  173.8 0.7 collective-permute-done.16.rest_6_
  174.5 2.1 %collective-permute-done.17.rest_7_ = bf16[168,128]{1,0:T(8,128)(2,1)S(1)} collective-permute-done((bf16[168,128]{1,0:T(8,128)(2,1)S(1)}, bf16[168,128]{1,0:T(8,128)(2,1)S(1)}, u32[]{:S(2)}, u32[]{:S(2)}) %collective-permute-start.17) | collective-permute-done | bytes 43040 | tf_op jit(solution)/shard_map/ppermute | solution.py:39
  176.6 3.5 %shard_map.129 = bf16[12,7,1024]{2,1,0:T(8,128)(2,1)} custom-call(s32[2]{0:T(128)S(1)} %copy-done.5, s32[8,504]{1,0:T(8,128)S(1)} %slice_convert_fusion.target_ref, f32[168,128]{1,0:T(8,128)S(1)} %get-tuple-element.36.rest_0_, bf16[168,128]{1,0:T(8,128)(2,1)S(1)} %collective-permute-done.11.rest_1_, bf16[168,128]{1,0:T(8,128)(2,1)S(1)} %collective-permute-done.12.rest_2_, ...), custom_call_target="tpu_custom_call" | custom-call | tf_op jit(solution)/shard_map/pallas_call | solution.py:387
  (61 shorter events, 2.4 us)
Async XLA Ops:
  7.2 86.8 %all-gather.3.cloned.1.call-start = ((), (), s32[]{:S(2)}) async-start(), calls=%async_computation | async-start | bytes 2949120 | tf_op jit(solution)/shard_map/all_gather | solution.py:461
  7.2 12.7 %collective-permute-start.1 = (bf16[24,2048]{1,0:T(8,128)(2,1)}, bf16[24,2048]{1,0:T(8,128)(2,1)S(1)}, u32[]{:S(2)}, u32[]{:S(2)}) collective-permute-start(bf16[24,2048]{1,0:T(8,128)(2,1)} %param.17), channel_id=1, source_target_pairs={{8,0},{16,8},{24,16},{9,1},{17,9},{25,17},{10,2},{18,10},{26,18},{... | collective-permute-start | bytes 294920 | tf_op jit(solution)/shard_map/ppermute | solution.py:45
  8.5 11.4 %collective-permute-start = (bf16[24,2048]{1,0:T(8,128)(2,1)}, bf16[24,2048]{1,0:T(8,128)(2,1)S(1)}, u32[]{:S(2)}, u32[]{:S(2)}) collective-permute-start(bf16[24,2048]{1,0:T(8,128)(2,1)} %param.17), channel_id=1, source_target_pairs={{0,8},{8,16},{16,24},{1,9},{9,17},{17,25},{2,10},{10,18},{18,26},{... | collective-permute-start | bytes 294920 | tf_op jit(solution)/shard_map/ppermute | solution.py:44
  21.6 1.1 copy-start
  24.2 20.1 %collective-permute-start.2 = (bf16[48,64,128]{2,1,0:T(8,128)(2,1)S(1)}, bf16[48,64,128]{2,1,0:T(8,128)(2,1)S(1)}, u32[]{:S(2)}, u32[]{:S(2)}) collective-permute-start(bf16[48,64,128]{2,1,0:T(8,128)(2,1)S(1)} %shard_map.123.own_ref), channel_id=1, source_target_pairs={{0,8},{8,16},{16,24},{1,9},{9,17},{17,25},{2,10},{10,18},{18,26},{... | collective-permute-start | bytes 2359304 | tf_op jit(solution)/shard_map/ppermute | solution.py:44
  28.2 20.3 %collective-permute-start.3 = (bf16[48,64,128]{2,1,0:T(8,128)(2,1)S(1)}, bf16[48,64,128]{2,1,0:T(8,128)(2,1)S(1)}, u32[]{:S(2)}, u32[]{:S(2)}) collective-permute-start(bf16[48,64,128]{2,1,0:T(8,128)(2,1)S(1)} %shard_map.123.own_ref), channel_id=1, source_target_pairs={{8,0},{16,8},{24,16},{9,1},{17,9},{25,17},{10,2},{18,10},{26,18},{... | collective-permute-start | bytes 2359304 | tf_op jit(solution)/shard_map/ppermute | solution.py:45
  48.5 0.7 copy-start.1
  49.2 0.6 copy-start.3
  58.2 10.7 %copy-start.12 = (bf16[24,2048]{1,0:T(8,128)(2,1)S(1)}, bf16[24,2048]{1,0:T(8,128)(2,1)}, u32[]{:S(2)}) copy-start(bf16[24,2048]{1,0:T(8,128)(2,1)} %param.17) | copy-start | bytes 294916
  58.2 16.4 %copy-start.2 = (s32[336]{0:T(512)S(1)}, s32[336]{0:T(512)}, u32[]{:S(2)}) copy-start(s32[336]{0:T(512)} %get-tuple-element.26.near_ref) | copy-start | bytes 4036
  58.2 16.4 %copy-start.4 = (s32[48]{0:T(128)S(1)}, s32[48]{0:T(128)}, u32[]{:S(2)}) copy-start(s32[48]{0:T(128)} %get-tuple-element.25.source_ref) | copy-start | bytes 580
  58.2 72.2 %collective-permute-start.4 = (bf16[1344,128]{1,0:T(8,128)(2,1)}, bf16[1344,128]{1,0:T(8,128)(2,1)S(1)}, u32[]{:S(2)}, u32[]{:S(2)}) collective-permute-start(bf16[1344,128]{1,0:T(8,128)(2,1)} %get-tuple-element.28), channel_id=1, source_target_pairs={{0,1},{1,0},{2,3},{3,2},{4,5},{5,4},{6,7},{7,6},{8,9},{9,8},{10,11... | collective-permute-start | bytes 1032200 | tf_op jit(solution)/shard_map/ppermute | solution.py:39
  66.7 0.8 copy-start.7
  67.4 65.5 %collective-permute-start.5 = (bf16[1344,128]{1,0:T(8,128)(2,1)}, bf16[1344,128]{1,0:T(8,128)(2,1)}, u32[]{:S(2)}, u32[]{:S(2)}) collective-permute-start(bf16[1344,128]{1,0:T(8,128)(2,1)} %get-tuple-element.29), channel_id=1, source_target_pairs={{0,2},{1,3},{2,0},{3,1},{4,6},{5,7},{6,4},{7,5},{8,10},{9,11},{10,... | collective-permute-start | bytes 1032200 | tf_op jit(solution)/shard_map/ppermute | solution.py:39
  74.2 62.8 %collective-permute-start.6 = (bf16[1344,128]{1,0:T(8,128)(2,1)}, bf16[1344,128]{1,0:T(8,128)(2,1)}, u32[]{:S(2)}, u32[]{:S(2)}) collective-permute-start(bf16[1344,128]{1,0:T(8,128)(2,1)} %copy-done.7), channel_id=1, source_target_pairs={{0,3},{1,2},{2,1},{3,0},{4,7},{5,6},{6,5},{7,4},{8,11},{9,10},{10,... | collective-permute-start | bytes 1032200 | tf_op jit(solution)/shard_map/ppermute | solution.py:39
  83.0 54.0 %collective-permute-start.7 = (bf16[1344,128]{1,0:T(8,128)(2,1)}, bf16[1344,128]{1,0:T(8,128)(2,1)}, u32[]{:S(2)}, u32[]{:S(2)}) collective-permute-start(bf16[1344,128]{1,0:T(8,128)(2,1)} %get-tuple-element.31), channel_id=1, source_target_pairs={{0,4},{1,5},{2,6},{3,7},{4,0},{5,1},{6,2},{7,3},{8,12},{9,13},{10,... | collective-permute-start | bytes 1032200 | tf_op jit(solution)/shard_map/ppermute | solution.py:39
  84.6 52.4 %collective-permute-start.8 = (bf16[1344,128]{1,0:T(8,128)(2,1)}, bf16[1344,128]{1,0:T(8,128)(2,1)}, u32[]{:S(2)}, u32[]{:S(2)}) collective-permute-start(bf16[1344,128]{1,0:T(8,128)(2,1)} %get-tuple-element.32), channel_id=1, source_target_pairs={{0,5},{1,4},{2,7},{3,6},{4,1},{5,0},{6,3},{7,2},{8,13},{9,12},{10,... | collective-permute-start | bytes 1032200 | tf_op jit(solution)/shard_map/ppermute | solution.py:39
  92.4 0.7 copy-start.8
  93.2 0.8 copy-start.10
  125.7 4.7 %copy-start.11 = (bf16[1344,128]{1,0:T(8,128)(2,1)S(1)}, bf16[1344,128]{1,0:T(8,128)(2,1)}, u32[]{:S(2)}) copy-start(bf16[1344,128]{1,0:T(8,128)(2,1)} %copy-done.10) | copy-start | bytes 1032196
  125.7 7.2 %copy-start.9 = (bf16[1344,128]{1,0:T(8,128)(2,1)S(1)}, bf16[1344,128]{1,0:T(8,128)(2,1)}, u32[]{:S(2)}) copy-start(bf16[1344,128]{1,0:T(8,128)(2,1)} %copy-done.8) | copy-start | bytes 1032196
  130.4 11.8 %collective-permute-start.9 = (bf16[1344,128]{1,0:T(8,128)(2,1)S(1)}, bf16[1344,128]{1,0:T(8,128)(2,1)S(1)}, u32[]{:S(2)}, u32[]{:S(2)}) collective-permute-start(bf16[1344,128]{1,0:T(8,128)(2,1)S(1)} %copy-done.11), channel_id=1, source_target_pairs={{0,6},{1,7},{2,4},{3,5},{4,2},{5,3},{6,0},{7,1},{8,14},{9,15},{10,... | collective-permute-start | bytes 1032200 | tf_op jit(solution)/shard_map/ppermute | solution.py:39
  132.9 15.9 %copy-start.5 = (s32[2]{0:T(128)S(1)}, s32[2]{0:T(128)}, u32[]{:S(2)}) copy-start(s32[2]{0:T(128)} %pad_add_fusion.where_ref) | copy-start | bytes 28
  132.9 15.9 %copy-start.6 = (s32[24]{0:T(128)S(1)}, s32[24]{0:T(128)}, u32[]{:S(2)}) copy-start(s32[24]{0:T(128)} %get-tuple-element.24.source2_ref) | copy-start | bytes 292
  132.9 15.9 %collective-permute-start.10 = (bf16[1344,128]{1,0:T(8,128)(2,1)S(1)}, bf16[1344,128]{1,0:T(8,128)(2,1)S(1)}, u32[]{:S(2)}, u32[]{:S(2)}) collective-permute-start(bf16[1344,128]{1,0:T(8,128)(2,1)S(1)} %copy-done.9), channel_id=1, source_target_pairs={{0,7},{1,6},{2,5},{3,4},{4,3},{5,2},{6,1},{7,0},{8,15},{9,14},{10,... | collective-permute-start | bytes 1032200 | tf_op jit(solution)/shard_map/ppermute | solution.py:39
  165.6 3.8 %collective-permute-start.11 = (bf16[168,128]{1,0:T(8,128)(2,1)S(1)}, bf16[168,128]{1,0:T(8,128)(2,1)S(1)}, u32[]{:S(2)}, u32[]{:S(2)}) collective-permute-start(bf16[168,128]{1,0:T(8,128)(2,1)S(1)} %convert_element_type.28), channel_id=1, source_target_pairs={{0,1},{1,0},{2,3},{3,2},{4,5},{5,4},{6,7},{7,6},{8,9},{9,8},{10,11... | collective-permute-start | bytes 129032 | tf_op jit(solution)/shard_map/ppermute | solution.py:39
  165.9 6.1 %collective-permute-start.12 = (bf16[168,128]{1,0:T(8,128)(2,1)S(1)}, bf16[168,128]{1,0:T(8,128)(2,1)S(1)}, u32[]{:S(2)}, u32[]{:S(2)}) collective-permute-start(bf16[168,128]{1,0:T(8,128)(2,1)S(1)} %convert_element_type.29), channel_id=1, source_target_pairs={{0,2},{1,3},{2,0},{3,1},{4,6},{5,7},{6,4},{7,5},{8,10},{9,11},{10,... | collective-permute-start | bytes 129032 | tf_op jit(solution)/shard_map/ppermute | solution.py:39
  167.4 6.3 %collective-permute-start.13 = (bf16[168,128]{1,0:T(8,128)(2,1)S(1)}, bf16[168,128]{1,0:T(8,128)(2,1)S(1)}, u32[]{:S(2)}, u32[]{:S(2)}) collective-permute-start(bf16[168,128]{1,0:T(8,128)(2,1)S(1)} %convert_element_type.30), channel_id=1, source_target_pairs={{0,3},{1,2},{2,1},{3,0},{4,7},{5,6},{6,5},{7,4},{8,11},{9,10},{10,... | collective-permute-start | bytes 129032 | tf_op jit(solution)/shard_map/ppermute | solution.py:39
  167.6 6.2 %collective-permute-start.14 = (bf16[168,128]{1,0:T(8,128)(2,1)S(1)}, bf16[168,128]{1,0:T(8,128)(2,1)S(1)}, u32[]{:S(2)}, u32[]{:S(2)}) collective-permute-start(bf16[168,128]{1,0:T(8,128)(2,1)S(1)} %convert_element_type.31), channel_id=1, source_target_pairs={{0,4},{1,5},{2,6},{3,7},{4,0},{5,1},{6,2},{7,3},{8,12},{9,13},{10,... | collective-permute-start | bytes 129032 | tf_op jit(solution)/shard_map/ppermute | solution.py:39
  169.1 4.6 %collective-permute-start.15 = (bf16[168,128]{1,0:T(8,128)(2,1)S(1)}, bf16[168,128]{1,0:T(8,128)(2,1)S(1)}, u32[]{:S(2)}, u32[]{:S(2)}) collective-permute-start(bf16[168,128]{1,0:T(8,128)(2,1)S(1)} %convert_element_type.32), channel_id=1, source_target_pairs={{0,5},{1,4},{2,7},{3,6},{4,1},{5,0},{6,3},{7,2},{8,13},{9,12},{10,... | collective-permute-start | bytes 129032 | tf_op jit(solution)/shard_map/ppermute | solution.py:39
  169.5 5.0 %collective-permute-start.16 = (bf16[168,128]{1,0:T(8,128)(2,1)S(1)}, bf16[168,128]{1,0:T(8,128)(2,1)S(1)}, u32[]{:S(2)}, u32[]{:S(2)}) collective-permute-start(bf16[168,128]{1,0:T(8,128)(2,1)S(1)} %convert_element_type.33), channel_id=1, source_target_pairs={{0,6},{1,7},{2,4},{3,5},{4,2},{5,3},{6,0},{7,1},{8,14},{9,15},{10,... | collective-permute-start | bytes 129032 | tf_op jit(solution)/shard_map/ppermute | solution.py:39
  172.0 4.6 %collective-permute-start.17 = (bf16[168,128]{1,0:T(8,128)(2,1)S(1)}, bf16[168,128]{1,0:T(8,128)(2,1)S(1)}, u32[]{:S(2)}, u32[]{:S(2)}) collective-permute-start(bf16[168,128]{1,0:T(8,128)(2,1)S(1)} %convert_element_type.34), channel_id=1, source_target_pairs={{0,7},{1,6},{2,5},{3,4},{4,3},{5,2},{6,1},{7,0},{8,15},{9,14},{10,... | collective-permute-start | bytes 129032 | tf_op jit(solution)/shard_map/ppermute | solution.py:39
Sparse Core Ops, SparseCore 0:
  21.7 30.7 all-gather.2

commit v2 on v1

v2 whole, which is shorter than its diff:
```python
import functools

import jax
import jax.numpy as jnp
from jax import lax
from jax.experimental import pallas as pl
from jax.experimental.pallas import tpu as pltpu
from jax.sharding import PartitionSpec as P

BF16 = jnp.bfloat16
F32 = jnp.float32
I32 = jnp.int32
LANES = 128
VMEM_LIMIT = 48 * 1024 * 1024


def vmem():
    return pl.BlockSpec(memory_space=pltpu.VMEM)


def smem():
    return pl.BlockSpec(memory_space=pltpu.SMEM)


def hbm():
    return pl.BlockSpec(memory_space=pl.ANY)


def params():
    return pltpu.CompilerParams(vmem_limit_bytes=VMEM_LIMIT)


def low_lanes(shape, bound):
    return lax.broadcasted_iota(I32, shape, len(shape) - 1) < bound


def exchange(cells, axis, offset):
    count = lax.axis_size(axis)
    return lax.ppermute(cells, axis, [(i, i ^ offset) for i in range(count)])


def neighbours(cells, axis):
    count = lax.axis_size(axis)
    previous = lax.ppermute(cells, axis, [(i, i + 1) for i in range(count - 1)])
    following = lax.ppermute(cells, axis, [(i + 1, i) for i in range(count - 1)])
    return previous, following


def halves_kernel(flat_ref, coarse_ref, out_ref, quarters_ref, wide_ref):
    group = flat_ref.shape[0]
    deep = flat_ref.shape[1] // LANES
    half = deep // 2
    left = low_lanes((group, LANES), LANES // 2)
    for t in range(half):
        upper = flat_ref[:, pl.ds(t * LANES, LANES)].astype(F32)
        lower = flat_ref[:, pl.ds((t + half) * LANES, LANES)].astype(F32)
        even = jnp.where(left, upper, pltpu.roll(lower, LANES // 2, 1))
        odd = jnp.where(left, pltpu.roll(upper, LANES // 2, 1), lower)
        wide_ref[pl.ds(2 * t, group, stride=deep), :] = even
        wide_ref[pl.ds(2 * t + 1, group, stride=deep), :] = odd
    for r in range(group):
        out_ref[r] = wide_ref[pl.ds(r * deep, deep), :].astype(BF16)
    count = coarse_ref.shape[0]
    deep2 = coarse_ref.shape[1] // LANES
    quarter = LANES // 4
    lane = lax.broadcasted_iota(I32, (count, LANES), 1) // quarter
    for t in range(deep2 // 4):
        tiles = [coarse_ref[:, pl.ds((h * deep2 // 4 + t) * LANES, LANES)].astype(F32) for h in range(4)]
        for u in range(4):
            total = None
            for h in range(4):
                shift = (h - u) % 4 * quarter
                piece = pltpu.roll(tiles[h], shift, 1) if shift else tiles[h]
                total = piece if total is None else jnp.where(lane == h, piece, total)
            wide_ref[pl.ds(4 * t + u, count, stride=deep2), :] = total
    for r in range(count):
        quarters_ref[r] = wide_ref[pl.ds(r * deep2, deep2), :].astype(BF16)


def halves(flat, coarse):
    rows, size = flat.shape
    count, size2 = coarse.shape
    deep = size // LANES
    deep2 = size2 // LANES
    group = 16
    steps = rows // group
    group2 = count // steps
    return pl.pallas_call(
        halves_kernel,
        grid=(steps,),
        out_shape=(
            jax.ShapeDtypeStruct((rows, deep, LANES), BF16),
            jax.ShapeDtypeStruct((count, deep2, LANES), BF16),
        ),
        in_specs=[
            pl.BlockSpec((group, size), lambda i: (i, 0)),
            pl.BlockSpec((group2, size2), lambda i: (i, 0)),
        ],
        out_specs=(
            pl.BlockSpec((group, deep, LANES), lambda i: (i, 0, 0)),
            pl.BlockSpec((group2, deep2, LANES), lambda i: (i, 0, 0)),
        ),
        scratch_shapes=[pltpu.VMEM((group * deep, LANES), F32)],
        compiler_params=params(),
    )(flat, coarse)


def index_kernel(
    where_ref,
    cols_ref,
    slot_ref,
    owner_ref,
    place_ref,
    slot2_ref,
    owner2_ref,
    place2_ref,
    plan_ref,
    target_ref,
    count_ref,
    *,
    parts,
    capacity,
    capacity2,
    owned,
    owned2,
):
    region = where_ref[0]
    dom = where_ref[1]
    stencil, rows = cols_ref.shape
    rows2 = slot2_ref.shape[1]
    span = parts * rows
    first = region * span
    slots = parts * capacity
    slots2 = parts * capacity2
    second = slots * (stencil + 1)

    def clear_counts(d, carry):
        count_ref[d] = 0
        return carry

    if slots > rows or slots2 > rows2:

        def clear(p, carry):
            plan_ref[p] = 0
            for k in range(stencil):
                plan_ref[slots + p * stencil + k] = 1
                target_ref[p * stencil + k] = stencil * owned
            return carry

        lax.fori_loop(0, slots, clear, 0)

        def clear2(p, carry):
            plan_ref[second + p] = 0
            for k in range(stencil):
                target_ref[(slots + p) * stencil + k] = (stencil + 1) * owned2
            return carry

        lax.fori_loop(0, slots2, clear2, 0)
    lax.fori_loop(0, parts, clear_counts, 0)

    def fine(i, carry):
        owner = owner_ref[i]
        rank = count_ref[owner]
        count_ref[owner] = rank + 1
        here = (owner ^ dom) * capacity + rank
        there = (owner * capacity + rank) * stencil
        place = place_ref[i]
        plan_ref[here] = i
        for k in range(stencil):
            col = cols_ref[k, i]
            step = jnp.where(col < first, 0, jnp.where(col >= first + span, 2, 1))
            begin = ((region + step - 1) * parts + dom) * rows
            plan_ref[slots + here * stencil + k] = (col - begin) * 4 + step
            target_ref[there + k] = slot_ref[k, i] * owned + place
        return carry

    lax.fori_loop(0, rows, fine, 0)
    lax.fori_loop(0, parts, clear_counts, 0)

    def coarse(i, carry):
        owner = owner2_ref[i]
        rank = count_ref[owner]
        count_ref[owner] = rank + 1
        plan_ref[second + (owner ^ dom) * capacity2 + rank] = i
        there = (slots + owner * capacity2 + rank) * stencil
        place = place2_ref[i]
        for k in range(stencil):
            target_ref[there + k] = place * (stencil + 1) + slot2_ref[k, i]
        return carry

    lax.fori_loop(0, rows2, coarse, 0)


def terms_kernel(plan_ref, blocks_ref, before_ref, own_ref, after_ref, *rest, offsets, capacity, slots):
    outs = rest[: len(offsets)]
    buffer_ref, row_sem = rest[len(offsets) :]
    stencil, width = buffer_ref.shape[1], buffer_ref.shape[2]
    half = width // 2
    narrow = LANES // 2
    flat = narrow * narrow // LANES

    def row_copy(n, slot):
        return pltpu.make_async_copy(blocks_ref.at[plan_ref[slot]], buffer_ref.at[n], row_sem.at[n])

    for n, offset in enumerate(offsets):
        for r in range(capacity):
            row_copy(n * capacity + r, offset * capacity + r).start()

    left = low_lanes((half, LANES), narrow)
    left_flat = low_lanes((flat, LANES), narrow)
    out_row = lax.broadcasted_iota(I32, (narrow, LANES), 0)
    in_col = lax.broadcasted_iota(I32, (narrow, LANES), 1)
    chosen = jnp.where(out_row < flat, 2 * out_row, 2 * (out_row - flat) + 1)
    pick = jnp.where(in_col == chosen, 1.0, 0.0).astype(BF16)
    zero = jnp.zeros((half, LANES), BF16)

    def neighbour(slot, k):
        code = plan_ref[slots + slot * stencil + k]
        row = lax.shift_right_logical(code, 2)
        step = code & 3
        return jnp.where(step == 0, before_ref[row], jnp.where(step == 1, own_ref[row], after_ref[row]))

    def one_row(n, slot, out_ref, r):
        mine = own_ref[plan_ref[slot]]
        column = jnp.concatenate([mine, pltpu.roll(mine, narrow, 1)], axis=0)
        turned = lax.dot_general(
            pick, column, (((1,), (1,)), ((), ())), preferred_element_type=F32
        ).astype(BF16)
        products = []
        for k in range(0, stencil, 2):
            one = neighbour(slot, k)
            weights = [jnp.where(left, one, zero), jnp.where(left, pltpu.roll(one, narrow, 1), zero)]
            lhs = buffer_ref[n, k]
            if k + 1 < stencil:
                two = neighbour(slot, k + 1)
                weights += [jnp.where(left, zero, pltpu.roll(two, narrow, 1)), jnp.where(left, zero, two)]
                lhs = jnp.concatenate([lhs, buffer_ref[n, k + 1]], axis=1)
            products.append(
                jnp.dot(lhs, jnp.concatenate(weights, axis=0), preferred_element_type=F32).astype(BF16)
            )
        term = jnp.dot(turned, jnp.concatenate(products, axis=1), preferred_element_type=F32)
        for k in range(0, stencil, 2):
            pair = term[:, k // 2 * LANES : (k // 2 + 1) * LANES]
            even = pair[:flat]
            odd = pair[flat:]
            base = (r * stencil + k) * flat
            out_ref[pl.ds(base, flat), :] = jnp.where(left_flat, even, pltpu.roll(odd, narrow, 1)).astype(BF16)
            if k + 1 < stencil:
                out_ref[pl.ds(base + flat, flat), :] = jnp.where(
                    left_flat, pltpu.roll(even, narrow, 1), odd
                ).astype(BF16)

    for n, offset in enumerate(offsets):
        for r in range(capacity):
            row_copy(n * capacity + r, offset * capacity + r).wait()
        for r in range(capacity):
            one_row(n * capacity + r, offset * capacity + r, outs[n], r)


def level_one(plan, blocks, before, own, after, offsets, capacity, slots):
    rows, stencil, width, _ = blocks.shape
    narrow = LANES // 2
    flat = narrow * narrow // LANES
    shape = jax.ShapeDtypeStruct((capacity * stencil * flat, LANES), BF16)
    count = len(offsets) * capacity
    return pl.pallas_call(
        functools.partial(terms_kernel, offsets=offsets, capacity=capacity, slots=slots),
        out_shape=tuple(shape for _ in offsets),
        in_specs=[smem(), hbm(), vmem(), vmem(), vmem()],
        out_specs=tuple(vmem() for _ in offsets),
        scratch_shapes=[
            pltpu.VMEM((count, stencil, width, width), BF16),
            pltpu.SemaphoreType.DMA((count,)),
        ],
        compiler_params=params(),
    )(plan, blocks, before, own, after)


def pick_kernel(index_ref, before_ref, own_ref, after_ref, out_ref):
    stencil, count = index_ref.shape

    def body(q, carry):
        for k in range(stencil):
            code = index_ref[k, q]
            row = lax.shift_right_logical(code, 2)
            step = code & 3
            out_ref[q * stencil + k] = jnp.where(
                step == 0, before_ref[row], jnp.where(step == 1, own_ref[row], after_ref[row])
            )
        return carry

    lax.fori_loop(0, count, body, 0, unroll=4)


def pick_rows(index, before, own, after):
    stencil, count = index.shape
    return pl.pallas_call(
        pick_kernel,
        out_shape=jax.ShapeDtypeStruct((count * stencil,) + own.shape[1:], own.dtype),
        in_specs=[smem(), vmem(), vmem(), vmem()],
        out_specs=vmem(),
        compiler_params=params(),
    )(index, before, own, after)


def owner_kernel(
    where_ref,
    target_ref,
    plan_ref,
    picked_ref,
    own_ref,
    *rest,
    parts,
    capacity,
    capacity2,
    owned,
    stencil,
):
    arrived = rest[:parts]
    out_ref = rest[parts]
    sends = rest[parts + 1 : 2 * parts + 1]
    sum_ref, term_ref = rest[2 * parts + 1 :]
    dom = where_ref[1]
    second_slot = parts * capacity * (stencil + 1)
    flat = sum_ref.shape[1]
    narrow = LANES // 2
    sum_ref[...] = jnp.zeros(sum_ref.shape, F32)
    for d in range(parts):
        part_ref = arrived[d]

        def add(r, carry, d=d, part_ref=part_ref):
            base = (dom * capacity + r) * stencil
            for k in range(stencil):
                target = target_ref[dom ^ d, base + k]
                sum_ref[target] += part_ref[pl.ds((r * stencil + k) * flat, flat), :].astype(F32)
            return carry

        lax.fori_loop(0, capacity, add, 0, unroll=True)

    left = low_lanes((flat, LANES), narrow)
    quarter = LANES // 4
    eighth = lax.broadcasted_iota(I32, (8, LANES), 1) // quarter
    block = lax.broadcasted_iota(I32, (16, LANES), 1) // quarter
    none = jnp.zeros((16, LANES), BF16)

    def second(d, carry):
        for r in range(capacity2):
            q = plan_ref[second_slot + d * capacity2 + r]
            rows = []
            weights = []
            for k in range(0, stencil, 2):
                one = sum_ref[k * owned + q].astype(BF16)
                out_ref[k * owned + q] = one
                if k + 1 < stencil:
                    two = sum_ref[(k + 1) * owned + q].astype(BF16)
                    out_ref[(k + 1) * owned + q] = two
                else:
                    two = jnp.zeros((flat, LANES), BF16)
                even = jnp.where(left, one, pltpu.roll(two, narrow, 1))
                odd = jnp.where(left, pltpu.roll(one, narrow, 1), two)
                rows.append(jnp.concatenate([even, odd], axis=0))
            for k in range(stencil):
                packed = picked_ref[q * stencil + k]
                for h in range(4):
                    shift = (k - h) % 4 * quarter
                    turned = pltpu.roll(packed, shift, 1) if shift else packed
                    weights.append(jnp.where(block == k % 4, turned, none))
            own = own_ref[q]
            groups = []
            for g in range((stencil + 3) // 4):
                lhs = jnp.concatenate(rows[2 * g : 2 * g + 2], axis=1)
                rhs = jnp.concatenate(weights[16 * g : 16 * g + 16], axis=0)
                product = jnp.dot(lhs[:, : rhs.shape[0]], rhs, preferred_element_type=F32)
                groups.append(product.astype(BF16))
            term = jnp.dot(own, jnp.concatenate(groups, axis=1), preferred_element_type=F32)
            for k in range(stencil):
                g = k // 4
                total = None
                for w in range(4):
                    piece = term[w * 8 : (w + 1) * 8, g * LANES : (g + 1) * LANES]
                    shift = (w - k) % 4 * quarter
                    if shift:
                        piece = pltpu.roll(piece, shift, 1)
                    total = piece if total is None else jnp.where(eighth == w, piece, total)
                term_ref[d, pl.ds((r * stencil + k) * 8, 8), :] = total
        return carry

    lax.fori_loop(0, parts, second, 0, unroll=4)
    for d in range(parts):
        sends[d][...] = term_ref[d].astype(BF16)


def owner_level(where, targets, plan, picked, own, arrived, parts, capacity, capacity2, owned, stencil):
    flat = LANES // 4
    send = jax.ShapeDtypeStruct((capacity2 * stencil * 8, LANES), BF16)
    return pl.pallas_call(
        functools.partial(
            owner_kernel, parts=parts, capacity=capacity, capacity2=capacity2, owned=owned, stencil=stencil
        ),
        out_shape=(jax.ShapeDtypeStruct((stencil * owned, flat, LANES), BF16),) + (send,) * parts,
        in_specs=[smem(), smem(), smem()] + [vmem()] * (2 + parts),
        out_specs=(vmem(),) * (1 + parts),
        scratch_shapes=[
            pltpu.VMEM((stencil * owned + 1, flat, LANES), F32),
            pltpu.VMEM((parts, capacity2 * stencil * 8, LANES), F32),
        ],
        compiler_params=params(),
    )(where, targets, plan, picked, own, *arrived)


def final_kernel(where_ref, target_ref, *rest, parts, first, capacity2, stencil):
    arrived = rest[:parts]
    out_ref = rest[parts]
    (sum_ref,) = rest[parts + 1 :]
    dom = where_ref[1]
    deep = stencil + 1
    sum_ref[...] = jnp.zeros(sum_ref.shape, F32)
    for d in range(parts):
        values = arrived[d][...].astype(F32)
        for r in range(capacity2):
            base = (first + dom * capacity2 + r) * stencil
            for k in range(stencil):
                at = r * stencil + k
                sum_ref[target_ref[dom ^ d, base + k]] += values[at * 8 : (at + 1) * 8]
    for u in range(out_ref.shape[0]):
        for t in range(8):
            tile = sum_ref[pl.ds(u * deep, deep), t, :]
            out_ref[u, :, pl.ds(t * LANES, LANES)] = tile[:stencil].astype(BF16)


def final_level(where, targets, arrived, parts, first, capacity2, owned2, stencil):
    return pl.pallas_call(
        functools.partial(final_kernel, parts=parts, first=first, capacity2=capacity2, stencil=stencil),
        out_shape=jax.ShapeDtypeStruct((owned2, stencil, 8 * LANES), BF16),
        in_specs=[smem(), smem()] + [vmem()] * parts,
        out_specs=vmem(),
        scratch_shapes=[pltpu.VMEM((owned2 * (stencil + 1) + 1, 8, LANES), F32)],
        compiler_params=params(),
    )(where, targets, *arrived)


def chunks_of(parts):
    order = list(range(parts - 1, -1, -1))
    return [(order[0],)] + [tuple(order[i : i + 2]) for i in range(1, parts - 1, 2)] + [(order[-1],)]


def local(
    fine_blocks,
    interp,
    fine_cols,
    fine_slot,
    fine_owner,
    fine_place,
    coarse_interp,
    coarse_cols,
    coarse_slot,
    coarse_owner,
    coarse_place,
):
    rows, stencil, width, _ = fine_blocks.shape
    narrow = interp.shape[1] // width
    narrow2 = coarse_interp.shape[1] // narrow
    parts = lax.axis_size("dom")
    region = lax.axis_index("region")
    dom = lax.axis_index("dom")
    owned = rows // 2
    owned2 = owned // 2
    capacity = max(2, rows // 8)
    capacity2 = max(2, owned // 8)
    slots = parts * capacity
    slots2 = parts * capacity2
    where = jnp.stack([region, dom]).astype(I32)

    own, quarters = halves(interp, coarse_interp)
    before, after = neighbours(own, "region")

    plan, target = pl.pallas_call(
        functools.partial(
            index_kernel, parts=parts, capacity=capacity, capacity2=capacity2, owned=owned, owned2=owned2
        ),
        out_shape=(
            jax.ShapeDtypeStruct((slots * (stencil + 1) + slots2,), I32),
            jax.ShapeDtypeStruct(((slots + slots2) * stencil,), I32),
        ),
        in_specs=[smem()] * 8,
        out_specs=(smem(),) * 2,
        scratch_shapes=[pltpu.SMEM((parts,), I32)],
    )(
        where,
        fine_cols.T,
        fine_slot.T,
        fine_owner[:, 0],
        fine_place,
        coarse_slot.T,
        coarse_owner[:, 0],
        coarse_place,
    )

    size2 = coarse_interp.shape[1]
    extra = pl.cdiv(target.shape[0], size2)
    codes = jnp.pad(target, (0, extra * size2 - target.shape[0])).astype(BF16)
    stacked = jnp.concatenate([quarters, codes.reshape((extra,) + quarters.shape[1:])], axis=0)
    table = lax.all_gather(stacked, "dom", axis=0, tiled=True)
    table_before, table_after = neighbours(table, "region")
    pitch = owned + extra
    targets = table.reshape((parts, pitch) + quarters.shape[1:])[:, owned:].reshape(parts, extra * size2)
    targets = targets[:, : target.shape[0]].astype(I32)
    span2 = parts * owned
    inside = coarse_cols % span2
    index2 = (inside // owned * pitch + inside % owned) * 4 + coarse_cols // span2 - region + 1
    picked = pick_rows(index2.T, table_before, table, table_after)
    turned = coarse_interp.reshape(owned, narrow // 2, 2, narrow2 // 4, 4)
    turned = turned.transpose(0, 4, 3, 2, 1).reshape(owned, narrow2, narrow)

    arrived = [None] * parts
    for offsets in chunks_of(parts):
        sent = level_one(plan, fine_blocks, before, own, after, offsets, capacity, slots)
        for offset, cells in zip(offsets, sent):
            arrived[offset] = exchange(cells, "dom", offset) if offset else cells
    outs = owner_level(
        where, targets, plan, picked, turned, arrived, parts, capacity, capacity2, owned, stencil
    )
    coarse_blocks = outs[0].reshape(stencil, owned, narrow * narrow).transpose(1, 0, 2)
    arrived2 = [exchange(cells, "dom", d) if d else cells for d, cells in enumerate(outs[1:])]
    second = final_level(where, targets, arrived2, parts, slots, capacity2, owned2, stencil)
    return (coarse_blocks, second)


def solution(mesh):
    in_specs = (
        P(("region", "dom"), None, None, None),
        P(("region", "dom"), None),
        P(("region", "dom"), None),
        P(("region", "dom"), None),
        P(("region", "dom"), None),
        P(("region", "dom")),
        P(("region", "dom"), None),
        P(("region", "dom"), None),
        P(("region", "dom"), None),
        P(("region", "dom"), None),
        P(("region", "dom")),
    )
    out_specs = (P(("region", "dom"), None, None), P(("region", "dom"), None, None))
    return jax.shard_map(local, mesh=mesh, in_specs=in_specs, out_specs=out_specs, check_vma=False)
```

time: 188 us -> 114 us (0.61)
  local copies, waits for them, and re-layouts: 48.2 us -> 9.43 us
  Pallas kernels: 59.1 us -> 42.1 us
  between operations: 14.3 us -> 0.85 us
  blocking collectives: 0 us -> 10.6 us
  waiting for transfers between devices: 32.8 us -> 23.7 us
  other arithmetic: 7.43 us -> 1.39 us
    broadcast_in_dim x7 -> x0, local copies, waits for them, and re-layouts: 24.2 us -> none  [local(): jnp.where(corner, picked, jnp.zeros((), BF16))]
    ppermute x2, waiting for transfers between devices: 14 us -> 0.01 us  [neighbours(): previous = lax.ppermute(cells, axis, [(i, i + 1) for i in range(count - 1)])]
    all_gather x0 -> x1, blocking collectives: none -> 10.6 us  [local(): table = lax.all_gather(stacked, 'dom', axis=0, tiled=True)]
    pallas_call x4 -> x5, Pallas kernels: 32.8 us -> 23.4 us  [level_one(): pl.pallas_call(functools.partial(terms_kernel, offsets=offsets, capacity=...]
    pallas_call x1, Pallas kernels: 16.8 us -> 7.57 us  [owner_level(): pl.pallas_call(functools.partial(owner_kernel, parts=parts, capacity=capa...]
    ppermute x14, waiting for transfers between devices: 14.6 us -> 23.7 us  [exchange(): return lax.ppermute(cells, axis, [(i, i ^ offset) for i in range(count)])]
    pad x2 -> x0, local copies, waits for them, and re-layouts: 4.43 us -> none  [the longest x1 4.42 us: local(): jnp.pad(picked, ((0, 0), (0, 4 * groups - stencil), (0, 0), (0, 0)))]
    ppermute x2, waiting for transfers between devices: 4.16 us -> 0.01 us  [neighbours(): lax.ppermute(cells, axis, [(i + 1, i) for i in range(count - 1)])]
  transfers between devices with their start and end apart: 19 -> 18, of which waited for: 6 -> 4; matrix products, arithmetic and copies ran while one was open for 26% -> 7% of each run, Pallas kernels for 21% -> 26%
where the time goes in v2:
time: 114 us
  Pallas kernels  42.1 us (37%)
  starting transfers between devices  25.8 us (23%)
  waiting for transfers between devices  23.7 us (21%)
  blocking collectives  10.6 us (9%)
  local copies, waits for them, and re-layouts  9.43 us (8%)
  other arithmetic  1.39 us (1%)
    ppermute x14, waiting for transfers between devices, exchange(): return lax.ppermute(cells, axis, [(i, i ^ offset) for i in range(count)])  23.7 us
    pallas_call x5, Pallas kernels, level_one(): pl.pallas_call(functools.partial(terms_kernel, offsets=offsets, capacity=...  23.4 us
    ppermute x14, starting transfers between devices, exchange(): return lax.ppermute(cells, axis, [(i, i ^ offset) for i in range(count)])  12.8 us
    all_gather x1, blocking collectives, local(): table = lax.all_gather(stacked, 'dom', axis=0, tiled=True)  10.6 us
    ppermute x2, starting transfers between devices, neighbours(): previous = lax.ppermute(cells, axis, [(i, i + 1) for i in range(count - 1)])  10.4 us
    pallas_call x1, Pallas kernels, owner_level(): pl.pallas_call(functools.partial(owner_kernel, parts=parts, capacity=capa...  7.57 us
    pallas_call x1, Pallas kernels, local(): pl.pallas_call(functools.partial(index_kernel, parts=parts, capacity=capa...  4.54 us
    unnamed x16, local copies, waits for them, and re-layouts  3.73 us
  transfers between devices with their start and end apart: 18, of which 4 were waited for; matrix products, arithmetic and copies ran while one was open for 7% of the time, Pallas kernels for 26%

profile of v2, /device:TPU:0, one launch (start us, length us, event | category | flops | bytes accessed | tf_op | source)
XLA Modules:
  0.0 113.9 jit_solution(3477244406991259944)
XLA Ops:
  0.6 1.1 copy-done
  1.8 0.9 copy-done.1
  2.7 1.7 %shard_map.122 = (bf16[48,64,128]{2,1,0:T(8,128)(2,1)S(1)}, bf16[24,16,128]{2,1,0:T(8,128)(2,1)S(1)}) custom-call(bf16[48,8192]{1,0:T(8,128)(2,1)S(1)} %copy-done, bf16[24,2048]{1,0:T(8,128)(2,1)S(1)} %copy-done.1), custom_call_target="tpu_custom_call" | custom-call | tf_op jit(solution)/shard_map/pallas_call | solution.py:88
  4.4 5.0 %collective-permute-start.2 = (bf16[48,64,128]{2,1,0:T(8,128)(2,1)S(1)}, bf16[48,64,128]{2,1,0:T(8,128)(2,1)S(1)}, u32[]{:S(2)}, u32[]{:S(2)}) collective-permute-start(bf16[48,64,128]{2,1,0:T(8,128)(2,1)S(1)} %get-tuple-element.24.own_ref), channel_id=1, source_target_pairs={{0,8},{8,16},{16,24},{1,9},{9,17},{17,25},{2,10},{10,18},{18,26},{... | collective-permute-start | bytes 2359304 | tf_op jit(solution)/shard_map/ppermute | solution.py:44
  9.4 1.3 %collective-permute-start.3 = (bf16[48,64,128]{2,1,0:T(8,128)(2,1)S(1)}, bf16[48,64,128]{2,1,0:T(8,128)(2,1)S(1)}, u32[]{:S(2)}, u32[]{:S(2)}) collective-permute-start(bf16[48,64,128]{2,1,0:T(8,128)(2,1)S(1)} %get-tuple-element.24.own_ref), channel_id=1, source_target_pairs={{8,0},{16,8},{24,16},{9,1},{17,9},{25,17},{10,2},{18,10},{26,18},{... | collective-permute-start | bytes 2359304 | tf_op jit(solution)/shard_map/ppermute | solution.py:45
  10.7 0.7 pad_add_fusion.where_ref
  11.3 4.5 %shard_map.123 = (s32[408]{0:T(512)}, s32[504]{0:T(512)}) custom-call(s32[2]{0:T(128)} %pad_add_fusion.where_ref, s32[7,48]{1,0:T(8,128)} %bitcast.23, s32[7,48]{1,0:T(8,128)} %bitcast.24, s32[48]{0:T(128)} %bitcast.26, s32[48]{0:T(128)} %place_ref.1, s32[7,24]{1,0:T(8,128)} %bitcast.25, s32[24]{0:T(128)} %bitcast.27, s32[24]{0:T(128)} %place2_ref.1), custom_call_target="tpu_custom_call" | custom-call | tf_op jit(solution)/shard_map/pallas_call | solution.py:477
  15.9 0.7 convert.4
  16.6 10.6 %all_gather.3.own_ref = bf16[200,16,128]{2,1,0:T(8,128)(2,1)S(1)} all-gather(bf16[25,16,128]{2,1,0:T(8,128)(2,1)S(1)} %pad_maximum_fusion), channel_id=1, replica_groups=mesh['region'=4,'dom'=8] {'dom'}, dimensions={0}, use_global_device_ids=true | all-gather | bytes 921600 | tf_op jit(solution)/shard_map/all_gather | solution.py:503
  27.1 5.4 %collective-permute-start = (bf16[200,16,128]{2,1,0:T(8,128)(2,1)S(1)}, bf16[200,16,128]{2,1,0:T(8,128)(2,1)}, u32[]{:S(2)}, u32[]{:S(2)}) collective-permute-start(bf16[200,16,128]{2,1,0:T(8,128)(2,1)S(1)} %all_gather.3.own_ref), channel_id=1, source_target_pairs={{0,8},{8,16},{16,24},{1,9},{9,17},{17,25},{2,10},{10,18},{18,26},{... | collective-permute-start | bytes 2457608 | tf_op jit(solution)/shard_map/ppermute | solution.py:44
  32.6 1.3 %collective-permute-start.1 = (bf16[200,16,128]{2,1,0:T(8,128)(2,1)S(1)}, bf16[200,16,128]{2,1,0:T(8,128)(2,1)}, u32[]{:S(2)}, u32[]{:S(2)}) collective-permute-start(bf16[200,16,128]{2,1,0:T(8,128)(2,1)S(1)} %all_gather.3.own_ref), channel_id=1, source_target_pairs={{8,0},{16,8},{24,16},{9,1},{17,9},{25,17},{10,2},{18,10},{26,18},{... | collective-permute-start | bytes 2457608 | tf_op jit(solution)/shard_map/ppermute | solution.py:45
  33.9 0.0 collective-permute-done.2.before_ref
  33.9 0.0 collective-permute-done.3.after_ref
  33.9 0.0 copy-start.3
  33.9 0.7 copy-done.3
  34.6 5.9 %shard_map.126 = (bf16[1344,128]{1,0:T(8,128)(2,1)}, bf16[1344,128]{1,0:T(8,128)(2,1)}) custom-call(s32[408]{0:T(512)S(1)} %copy-done.3, bf16[48,7,128,128]{3,2,1,0:T(8,128)(2,1)} %blocks_ref.9, bf16[48,64,128]{2,1,0:T(8,128)(2,1)S(1)} %collective-permute-done.2.before_ref, bf16[48,64,128]{2,1,0:T(8,128)(2,1)S(1)} %get-tuple-element.24.own_ref, ...), custom_call_target="tpu_custom_call" | custom-call | tf_op jit(solution)/shard_map/pallas_call | solution.py:266
  40.5 0.0 copy-start.4
  40.5 0.1 collective-permute-start.4
  40.6 1.5 %collective-permute-start.5 = (bf16[1344,128]{1,0:T(8,128)(2,1)}, bf16[1344,128]{1,0:T(8,128)(2,1)}, u32[]{:S(2)}, u32[]{:S(2)}) collective-permute-start(bf16[1344,128]{1,0:T(8,128)(2,1)} %get-tuple-element.26), channel_id=1, source_target_pairs={{0,2},{1,3},{2,0},{3,1},{4,6},{5,7},{6,4},{7,5},{8,10},{9,11},{10,... | collective-permute-start | bytes 1032200 | tf_op jit(solution)/shard_map/ppermute | solution.py:39
  42.1 1.0 copy.19
  43.2 2.8 %copy.20 = bf16[24,4,8,2,32]{4,3,2,1,0:T(2,128)(2,1)} copy(bf16[24,4,8,2,32]{0,1,2,3,4:T(4,128)(2,1)} %bitcast.20) | data formatting | bytes 196608 | tf_op jit(solution)/shard_map/transpose | solution.py:513
  46.0 1.2 %reshape.26.own_ref = bf16[24,32,64]{2,1,0:T(8,128)(2,1)S(1)} reshape(bf16[24,4,8,2,32]{4,3,2,1,0:T(2,128)(2,1)} %copy.20) | data formatting | bytes 196608 | tf_op jit(solution)/shard_map/reshape | solution.py:513
  47.2 5.2 %shard_map.127 = (bf16[1344,128]{1,0:T(8,128)(2,1)S(1)}, bf16[1344,128]{1,0:T(8,128)(2,1)S(1)}) custom-call(s32[408]{0:T(512)S(1)} %copy-done.4, bf16[48,7,128,128]{3,2,1,0:T(8,128)(2,1)} %blocks_ref.9, bf16[48,64,128]{2,1,0:T(8,128)(2,1)S(1)} %collective-permute-done.2.before_ref, bf16[48,64,128]{2,1,0:T(8,128)(2,1)S(1)} %get-tuple-element.24.own_ref, ...), custom_call_target="tpu_custom_call" | custom-call | tf_op jit(solution)/shard_map/pallas_call | solution.py:266
  52.4 0.4 collective-permute-start.6
  52.8 5.2 %shard_map.128 = (bf16[1344,128]{1,0:T(8,128)(2,1)S(1)}, bf16[1344,128]{1,0:T(8,128)(2,1)S(1)}) custom-call(s32[408]{0:T(512)S(1)} %copy-done.4, bf16[48,7,128,128]{3,2,1,0:T(8,128)(2,1)} %blocks_ref.9, bf16[48,64,128]{2,1,0:T(8,128)(2,1)S(1)} %collective-permute-done.2.before_ref, bf16[48,64,128]{2,1,0:T(8,128)(2,1)S(1)} %get-tuple-element.24.own_ref, ...), custom_call_target="tpu_custom_call" | custom-call | tf_op jit(solution)/shard_map/pallas_call | solution.py:266
  57.9 0.0 copy-start.6
  57.9 3.6 %shard_map.129 = bf16[1344,128]{1,0:T(8,128)(2,1)S(1)} custom-call(s32[408]{0:T(512)S(1)} %copy-done.4, bf16[48,7,128,128]{3,2,1,0:T(8,128)(2,1)} %blocks_ref.9, bf16[48,64,128]{2,1,0:T(8,128)(2,1)S(1)} %collective-permute-done.2.before_ref, bf16[48,64,128]{2,1,0:T(8,128)(2,1)S(1)} %get-tuple-element.24.own_ref, ...), custom_call_target="tpu_custom_call" | custom-call | tf_op jit(solution)/shard_map/pallas_call | solution.py:266
  61.5 1.6 %collective-permute-start.7 = (bf16[1344,128]{1,0:T(8,128)(2,1)S(1)}, bf16[1344,128]{1,0:T(8,128)(2,1)S(1)}, u32[]{:S(2)}, u32[]{:S(2)}) collective-permute-start(bf16[1344,128]{1,0:T(8,128)(2,1)S(1)} %get-tuple-element.28), channel_id=1, source_target_pairs={{0,4},{1,5},{2,6},{3,7},{4,0},{5,1},{6,2},{7,3},{8,12},{9,13},{10,... | collective-permute-start | bytes 1032200 | tf_op jit(solution)/shard_map/ppermute | solution.py:39
  63.1 0.2 collective-permute-start.8
  63.3 0.0 collective-permute-done.4.rest_1_
  63.3 1.5 %collective-permute-start.9 = (bf16[1344,128]{1,0:T(8,128)(2,1)S(1)}, bf16[1344,128]{1,0:T(8,128)(2,1)S(1)}, u32[]{:S(2)}, u32[]{:S(2)}) collective-permute-start(bf16[1344,128]{1,0:T(8,128)(2,1)S(1)} %get-tuple-element.30), channel_id=1, source_target_pairs={{0,6},{1,7},{2,4},{3,5},{4,2},{5,3},{6,0},{7,1},{8,14},{9,15},{10,... | collective-permute-start | bytes 1032200 | tf_op jit(solution)/shard_map/ppermute | solution.py:39
  64.8 0.0 collective-permute-done.5.rest_2_
  64.8 1.2 %collective-permute-start.10 = (bf16[1344,128]{1,0:T(8,128)(2,1)S(1)}, bf16[1344,128]{1,0:T(8,128)(2,1)S(1)}, u32[]{:S(2)}, u32[]{:S(2)}) collective-permute-start(bf16[1344,128]{1,0:T(8,128)(2,1)S(1)} %shard_map.129), channel_id=1, source_target_pairs={{0,7},{1,6},{2,5},{3,4},{4,3},{5,2},{6,1},{7,0},{8,15},{9,14},{10,... | collective-permute-start | bytes 1032200 | tf_op jit(solution)/shard_map/ppermute | solution.py:39
  66.1 3.6 %shard_map.125.rest_0_ = bf16[1344,128]{1,0:T(8,128)(2,1)S(1)} custom-call(s32[408]{0:T(512)S(1)} %copy-done.4, bf16[48,7,128,128]{3,2,1,0:T(8,128)(2,1)} %blocks_ref.9, bf16[48,64,128]{2,1,0:T(8,128)(2,1)S(1)} %collective-permute-done.2.before_ref, bf16[48,64,128]{2,1,0:T(8,128)(2,1)S(1)} %get-tuple-element.24.own_ref, ...), custom_call_target="tpu_custom_call" | custom-call | tf_op jit(solution)/shard_map/pallas_call | solution.py:266
  69.7 2.2 %shard_map.124.picked_ref = bf16[168,16,128]{2,1,0:T(8,128)(2,1)S(1)} custom-call(s32[7,24]{1,0:T(8,128)S(1)} %fusion.6.index_ref, bf16[200,16,128]{2,1,0:T(8,128)(2,1)} %collective-permute-done.before_ref, bf16[200,16,128]{2,1,0:T(8,128)(2,1)S(1)} %all_gather.3.own_ref, bf16[200,16,128]{2,1,0:T(8,128)(2,1)} %collective-permute-done.1.after_ref), custom_call_target="tpu_custom_call" | custom-call | tf_op jit(solution)/shard_map/pallas_call | solution.py:297
  71.9 15.4 %collective-permute-done.7.rest_4_ = bf16[1344,128]{1,0:T(8,128)(2,1)S(1)} collective-permute-done((bf16[1344,128]{1,0:T(8,128)(2,1)S(1)}, bf16[1344,128]{1,0:T(8,128)(2,1)S(1)}, u32[]{:S(2)}, u32[]{:S(2)}) %collective-permute-start.7) | collective-permute-done | bytes 344096 | tf_op jit(solution)/shard_map/ppermute | solution.py:39
  87.2 6.2 %collective-permute-done.8.rest_5_ = bf16[1344,128]{1,0:T(8,128)(2,1)S(1)} collective-permute-done((bf16[1344,128]{1,0:T(8,128)(2,1)S(1)}, bf16[1344,128]{1,0:T(8,128)(2,1)S(1)}, u32[]{:S(2)}, u32[]{:S(2)}) %collective-permute-start.8) | collective-permute-done | bytes 344096 | tf_op jit(solution)/shard_map/ppermute | solution.py:39
  93.5 7.6 %shard_map.130 = (bf16[168,32,128]{2,1,0:T(8,128)(2,1)S(1)}, bf16[168,128]{1,0:T(8,128)(2,1)S(1)}, bf16[168,128]{1,0:T(8,128)(2,1)S(1)}, bf16[168,128]{1,0:T(8,1...) custom-call(s32[2]{0:T(128)S(1)} %copy-done.5, ...), custom_call_target="tpu_custom_call" | custom-call | tf_op jit(solution)/shard_map/pallas_call | solution.py:396
  101.1 0.5 collective-permute-start.11
  101.5 1.5 %collective-permute-start.12 = (bf16[168,128]{1,0:T(8,128)(2,1)S(1)}, bf16[168,128]{1,0:T(8,128)(2,1)S(1)}, u32[]{:S(2)}, u32[]{:S(2)}) collective-permute-start(bf16[168,128]{1,0:T(8,128)(2,1)S(1)} %get-tuple-element.34), channel_id=1, source_target_pairs={{0,2},{1,3},{2,0},{3,1},{4,6},{5,7},{6,4},{7,5},{8,10},{9,11},{10,... | collective-permute-start | bytes 129032 | tf_op jit(solution)/shard_map/ppermute | solution.py:39
  103.0 1.4 %collective-permute-start.14 = (bf16[168,128]{1,0:T(8,128)(2,1)S(1)}, bf16[168,128]{1,0:T(8,128)(2,1)S(1)}, u32[]{:S(2)}, u32[]{:S(2)}) collective-permute-start(bf16[168,128]{1,0:T(8,128)(2,1)S(1)} %get-tuple-element.36), channel_id=1, source_target_pairs={{0,4},{1,5},{2,6},{3,7},{4,0},{5,1},{6,2},{7,3},{8,12},{9,13},{10,... | collective-permute-start | bytes 129032 | tf_op jit(solution)/shard_map/ppermute | solution.py:39
  104.5 0.5 collective-permute-start.15
  105.0 1.4 %collective-permute-start.16 = (bf16[168,128]{1,0:T(8,128)(2,1)S(1)}, bf16[168,128]{1,0:T(8,128)(2,1)S(1)}, u32[]{:S(2)}, u32[]{:S(2)}) collective-permute-start(bf16[168,128]{1,0:T(8,128)(2,1)S(1)} %get-tuple-element.38), channel_id=1, source_target_pairs={{0,6},{1,7},{2,4},{3,5},{4,2},{5,3},{6,0},{7,1},{8,14},{9,15},{10,... | collective-permute-start | bytes 129032 | tf_op jit(solution)/shard_map/ppermute | solution.py:39
  106.5 1.0 collective-permute-start.17
  107.4 1.7 %reshape.27 = bf16[7,24,4096]{2,1,0:T(8,128)(2,1)} reshape(bf16[168,32,128]{2,1,0:T(8,128)(2,1)S(1)} %get-tuple-element.31) | data formatting | bytes 2752512 | tf_op jit(solution)/shard_map/reshape | solution.py:523
  109.1 0.8 collective-permute-done.16.rest_6_
  109.9 1.3 %collective-permute-done.17.rest_7_ = bf16[168,128]{1,0:T(8,128)(2,1)S(1)} collective-permute-done((bf16[168,128]{1,0:T(8,128)(2,1)S(1)}, bf16[168,128]{1,0:T(8,128)(2,1)S(1)}, u32[]{:S(2)}, u32[]{:S(2)}) %collective-permute-start.17) | collective-permute-done | bytes 43040 | tf_op jit(solution)/shard_map/ppermute | solution.py:39
  111.2 2.7 %shard_map.131 = bf16[12,7,1024]{2,1,0:T(8,128)(2,1)} custom-call(s32[2]{0:T(128)S(1)} %copy-done.5, s32[8,504]{1,0:T(8,128)S(1)} %slice_convert_fusion.target_ref, bf16[168,128]{1,0:T(8,128)(2,1)S(1)} %get-tuple-element.32.rest_0_, bf16[168,128]{1,0:T(8,128)(2,1)S(1)} %collective-permute-done.11.rest_1_, ...), custom_call_target="tpu_custom_call" | custom-call | tf_op jit(solution)/shard_map/pallas_call | solution.py:432
  (25 shorter events, 0.1 us)
Async XLA Ops:
  0.6 1.1 copy-start
  1.8 0.9 copy-start.1
  4.4 29.5 %collective-permute-start.2 = (bf16[48,64,128]{2,1,0:T(8,128)(2,1)S(1)}, bf16[48,64,128]{2,1,0:T(8,128)(2,1)S(1)}, u32[]{:S(2)}, u32[]{:S(2)}) collective-permute-start(bf16[48,64,128]{2,1,0:T(8,128)(2,1)S(1)} %get-tuple-element.24.own_ref), channel_id=1, source_target_pairs={{0,8},{8,16},{16,24},{1,9},{9,17},{17,25},{2,10},{10,18},{18,26},{... | collective-permute-start | bytes 2359304 | tf_op jit(solution)/shard_map/ppermute | solution.py:44
  9.4 24.5 %collective-permute-start.3 = (bf16[48,64,128]{2,1,0:T(8,128)(2,1)S(1)}, bf16[48,64,128]{2,1,0:T(8,128)(2,1)S(1)}, u32[]{:S(2)}, u32[]{:S(2)}) collective-permute-start(bf16[48,64,128]{2,1,0:T(8,128)(2,1)S(1)} %get-tuple-element.24.own_ref), channel_id=1, source_target_pairs={{8,0},{16,8},{24,16},{9,1},{17,9},{25,17},{10,2},{18,10},{26,18},{... | collective-permute-start | bytes 2359304 | tf_op jit(solution)/shard_map/ppermute | solution.py:45
  27.1 34.4 %collective-permute-start = (bf16[200,16,128]{2,1,0:T(8,128)(2,1)S(1)}, bf16[200,16,128]{2,1,0:T(8,128)(2,1)}, u32[]{:S(2)}, u32[]{:S(2)}) collective-permute-start(bf16[200,16,128]{2,1,0:T(8,128)(2,1)S(1)} %all_gather.3.own_ref), channel_id=1, source_target_pairs={{0,8},{8,16},{16,24},{1,9},{9,17},{17,25},{2,10},{10,18},{18,26},{... | collective-permute-start | bytes 2457608 | tf_op jit(solution)/shard_map/ppermute | solution.py:44
  32.6 30.5 %collective-permute-start.1 = (bf16[200,16,128]{2,1,0:T(8,128)(2,1)S(1)}, bf16[200,16,128]{2,1,0:T(8,128)(2,1)}, u32[]{:S(2)}, u32[]{:S(2)}) collective-permute-start(bf16[200,16,128]{2,1,0:T(8,128)(2,1)S(1)} %all_gather.3.own_ref), channel_id=1, source_target_pairs={{8,0},{16,8},{24,16},{9,1},{17,9},{25,17},{10,2},{18,10},{26,18},{... | collective-permute-start | bytes 2457608 | tf_op jit(solution)/shard_map/ppermute | solution.py:45
  33.9 0.7 copy-start.3
  34.6 7.6 %copy-start.2 = (bf16[24,2048]{1,0:T(8,128)(2,1)S(1)}, bf16[24,2048]{1,0:T(8,128)(2,1)}, u32[]{:S(2)}) copy-start(bf16[24,2048]{1,0:T(8,128)(2,1)} %coarse_ref.1) | copy-start | bytes 294916
  40.5 6.7 %copy-start.4 = (s32[408]{0:T(512)S(1)}, s32[408]{0:T(512)}, u32[]{:S(2)}) copy-start(s32[408]{0:T(512)} %get-tuple-element.23.plan_ref) | copy-start | bytes 4900
  40.5 22.8 %collective-permute-start.4 = (bf16[1344,128]{1,0:T(8,128)(2,1)}, bf16[1344,128]{1,0:T(8,128)(2,1)}, u32[]{:S(2)}, u32[]{:S(2)}) collective-permute-start(bf16[1344,128]{1,0:T(8,128)(2,1)} %get-tuple-element.25), channel_id=1, source_target_pairs={{0,1},{1,0},{2,3},{3,2},{4,5},{5,4},{6,7},{7,6},{8,9},{9,8},{10,11... | collective-permute-start | bytes 1032200 | tf_op jit(solution)/shard_map/ppermute | solution.py:39
  40.6 24.1 %collective-permute-start.5 = (bf16[1344,128]{1,0:T(8,128)(2,1)}, bf16[1344,128]{1,0:T(8,128)(2,1)}, u32[]{:S(2)}, u32[]{:S(2)}) collective-permute-start(bf16[1344,128]{1,0:T(8,128)(2,1)} %get-tuple-element.26), channel_id=1, source_target_pairs={{0,2},{1,3},{2,0},{3,1},{4,6},{5,7},{6,4},{7,5},{8,10},{9,11},{10,... | collective-permute-start | bytes 1032200 | tf_op jit(solution)/shard_map/ppermute | solution.py:39
  52.4 19.5 %collective-permute-start.6 = (bf16[1344,128]{1,0:T(8,128)(2,1)S(1)}, bf16[1344,128]{1,0:T(8,128)(2,1)S(1)}, u32[]{:S(2)}, u32[]{:S(2)}) collective-permute-start(bf16[1344,128]{1,0:T(8,128)(2,1)S(1)} %get-tuple-element.27), channel_id=1, source_target_pairs={{0,3},{1,2},{2,1},{3,0},{4,7},{5,6},{6,5},{7,4},{8,11},{9,10},{10,... | collective-permute-start | bytes 1032200 | tf_op jit(solution)/shard_map/ppermute | solution.py:39
  57.9 8.1 %copy-start.6 = (s32[24,7]{0,1:T(8,128)S(1)}, s32[24,7]{0,1:T(8,128)}, u32[]{:S(2)}) copy-start(s32[24,7]{0,1:T(8,128)} %param.18) | copy-start | bytes 2020
  61.5 25.7 %collective-permute-start.7 = (bf16[1344,128]{1,0:T(8,128)(2,1)S(1)}, bf16[1344,128]{1,0:T(8,128)(2,1)S(1)}, u32[]{:S(2)}, u32[]{:S(2)}) collective-permute-start(bf16[1344,128]{1,0:T(8,128)(2,1)S(1)} %get-tuple-element.28), channel_id=1, source_target_pairs={{0,4},{1,5},{2,6},{3,7},{4,0},{5,1},{6,2},{7,3},{8,12},{9,13},{10,... | collective-permute-start | bytes 1032200 | tf_op jit(solution)/shard_map/ppermute | solution.py:39
  63.1 30.4 %collective-permute-start.8 = (bf16[1344,128]{1,0:T(8,128)(2,1)S(1)}, bf16[1344,128]{1,0:T(8,128)(2,1)S(1)}, u32[]{:S(2)}, u32[]{:S(2)}) collective-permute-start(bf16[1344,128]{1,0:T(8,128)(2,1)S(1)} %get-tuple-element.29), channel_id=1, source_target_pairs={{0,5},{1,4},{2,7},{3,6},{4,1},{5,0},{6,3},{7,2},{8,13},{9,12},{10,... | collective-permute-start | bytes 1032200 | tf_op jit(solution)/shard_map/ppermute | solution.py:39
  63.3 30.2 %collective-permute-start.9 = (bf16[1344,128]{1,0:T(8,128)(2,1)S(1)}, bf16[1344,128]{1,0:T(8,128)(2,1)S(1)}, u32[]{:S(2)}, u32[]{:S(2)}) collective-permute-start(bf16[1344,128]{1,0:T(8,128)(2,1)S(1)} %get-tuple-element.30), channel_id=1, source_target_pairs={{0,6},{1,7},{2,4},{3,5},{4,2},{5,3},{6,0},{7,1},{8,14},{9,15},{10,... | collective-permute-start | bytes 1032200 | tf_op jit(solution)/shard_map/ppermute | solution.py:39
  64.8 28.7 %collective-permute-start.10 = (bf16[1344,128]{1,0:T(8,128)(2,1)S(1)}, bf16[1344,128]{1,0:T(8,128)(2,1)S(1)}, u32[]{:S(2)}, u32[]{:S(2)}) collective-permute-start(bf16[1344,128]{1,0:T(8,128)(2,1)S(1)} %shard_map.129), channel_id=1, source_target_pairs={{0,7},{1,6},{2,5},{3,4},{4,3},{5,2},{6,1},{7,0},{8,15},{9,14},{10,... | collective-permute-start | bytes 1032200 | tf_op jit(solution)/shard_map/ppermute | solution.py:39
  69.6 23.8 %copy-start.5 = (s32[2]{0:T(128)S(1)}, s32[2]{0:T(128)}, u32[]{:S(2)}) copy-start(s32[2]{0:T(128)} %pad_add_fusion.where_ref) | copy-start | bytes 28
  101.1 4.0 %collective-permute-start.11 = (bf16[168,128]{1,0:T(8,128)(2,1)S(1)}, bf16[168,128]{1,0:T(8,128)(2,1)S(1)}, u32[]{:S(2)}, u32[]{:S(2)}) collective-permute-start(bf16[168,128]{1,0:T(8,128)(2,1)S(1)} %get-tuple-element.33), channel_id=1, source_target_pairs={{0,1},{1,0},{2,3},{3,2},{4,5},{5,4},{6,7},{7,6},{8,9},{9,8},{10,11... | collective-permute-start | bytes 129032 | tf_op jit(solution)/shard_map/ppermute | solution.py:39
  101.5 4.9 %collective-permute-start.12 = (bf16[168,128]{1,0:T(8,128)(2,1)S(1)}, bf16[168,128]{1,0:T(8,128)(2,1)S(1)}, u32[]{:S(2)}, u32[]{:S(2)}) collective-permute-start(bf16[168,128]{1,0:T(8,128)(2,1)S(1)} %get-tuple-element.34), channel_id=1, source_target_pairs={{0,2},{1,3},{2,0},{3,1},{4,6},{5,7},{6,4},{7,5},{8,10},{9,11},{10,... | collective-permute-start | bytes 129032 | tf_op jit(solution)/shard_map/ppermute | solution.py:39
  103.0 6.1 %collective-permute-start.13 = (bf16[168,128]{1,0:T(8,128)(2,1)S(1)}, bf16[168,128]{1,0:T(8,128)(2,1)S(1)}, u32[]{:S(2)}, u32[]{:S(2)}) collective-permute-start(bf16[168,128]{1,0:T(8,128)(2,1)S(1)} %get-tuple-element.35), channel_id=1, source_target_pairs={{0,3},{1,2},{2,1},{3,0},{4,7},{5,6},{6,5},{7,4},{8,11},{9,10},{10,... | collective-permute-start | bytes 129032 | tf_op jit(solution)/shard_map/ppermute | solution.py:39
  103.0 6.1 %collective-permute-start.14 = (bf16[168,128]{1,0:T(8,128)(2,1)S(1)}, bf16[168,128]{1,0:T(8,128)(2,1)S(1)}, u32[]{:S(2)}, u32[]{:S(2)}) collective-permute-start(bf16[168,128]{1,0:T(8,128)(2,1)S(1)} %get-tuple-element.36), channel_id=1, source_target_pairs={{0,4},{1,5},{2,6},{3,7},{4,0},{5,1},{6,2},{7,3},{8,12},{9,13},{10,... | collective-permute-start | bytes 129032 | tf_op jit(solution)/shard_map/ppermute | solution.py:39
  104.5 4.6 %collective-permute-start.15 = (bf16[168,128]{1,0:T(8,128)(2,1)S(1)}, bf16[168,128]{1,0:T(8,128)(2,1)S(1)}, u32[]{:S(2)}, u32[]{:S(2)}) collective-permute-start(bf16[168,128]{1,0:T(8,128)(2,1)S(1)} %get-tuple-element.37), channel_id=1, source_target_pairs={{0,5},{1,4},{2,7},{3,6},{4,1},{5,0},{6,3},{7,2},{8,13},{9,12},{10,... | collective-permute-start | bytes 129032 | tf_op jit(solution)/shard_map/ppermute | solution.py:39
  105.0 4.9 %collective-permute-start.16 = (bf16[168,128]{1,0:T(8,128)(2,1)S(1)}, bf16[168,128]{1,0:T(8,128)(2,1)S(1)}, u32[]{:S(2)}, u32[]{:S(2)}) collective-permute-start(bf16[168,128]{1,0:T(8,128)(2,1)S(1)} %get-tuple-element.38), channel_id=1, source_target_pairs={{0,6},{1,7},{2,4},{3,5},{4,2},{5,3},{6,0},{7,1},{8,14},{9,15},{10,... | collective-permute-start | bytes 129032 | tf_op jit(solution)/shard_map/ppermute | solution.py:39
  106.5 4.7 %collective-permute-start.17 = (bf16[168,128]{1,0:T(8,128)(2,1)S(1)}, bf16[168,128]{1,0:T(8,128)(2,1)S(1)}, u32[]{:S(2)}, u32[]{:S(2)}) collective-permute-start(bf16[168,128]{1,0:T(8,128)(2,1)S(1)} %get-tuple-element.39), channel_id=1, source_target_pairs={{0,7},{1,6},{2,5},{3,4},{4,3},{5,2},{6,1},{7,0},{8,15},{9,14},{10,... | collective-permute-start | bytes 129032 | tf_op jit(solution)/shard_map/ppermute | solution.py:39

commit v3 on v2

--- a/solution.py
+++ b/solution.py
@@ -11,7 +11,7 @@
 F32 = jnp.float32
 I32 = jnp.int32
 LANES = 128
-VMEM_LIMIT = 48 * 1024 * 1024
+VMEM_LIMIT = 32 * 1024 * 1024
 
 
 def vmem():
@@ -39,70 +39,80 @@
     return lax.ppermute(cells, axis, [(i, i ^ offset) for i in range(count)])
 
 
+def partner(index, odd, count):
+    other = ((index + odd) ^ 1) - odd
+    return other if 0 <= other < count else index
+
+
 def neighbours(cells, axis):
     count = lax.axis_size(axis)
-    previous = lax.ppermute(cells, axis, [(i, i + 1) for i in range(count - 1)])
-    following = lax.ppermute(cells, axis, [(i + 1, i) for i in range(count - 1)])
-    return previous, following
-
-
-def halves_kernel(flat_ref, coarse_ref, out_ref, quarters_ref, wide_ref):
-    group = flat_ref.shape[0]
-    deep = flat_ref.shape[1] // LANES
+    return tuple(lax.ppermute(cells, axis, [(i, partner(i, odd, count)) for i in range(count)]) for odd in (0, 1))
+
+
+def table_of(step, region):
+    swapped = jnp.where(region % 2 == 0, 2 - step, step)
+    return jnp.where(step == 1, 1, swapped)
+
+
+def halves_kernel(flat_ref, out_ref, rows_ref, wide_ref, sems):
+    steps, group = rows_ref.shape[:2]
+    deep = rows_ref.shape[2] // LANES
     half = deep // 2
     left = low_lanes((group, LANES), LANES // 2)
-    for t in range(half):
-        upper = flat_ref[:, pl.ds(t * LANES, LANES)].astype(F32)
-        lower = flat_ref[:, pl.ds((t + half) * LANES, LANES)].astype(F32)
-        even = jnp.where(left, upper, pltpu.roll(lower, LANES // 2, 1))
-        odd = jnp.where(left, pltpu.roll(upper, LANES // 2, 1), lower)
-        wide_ref[pl.ds(2 * t, group, stride=deep), :] = even
-        wide_ref[pl.ds(2 * t + 1, group, stride=deep), :] = odd
-    for r in range(group):
-        out_ref[r] = wide_ref[pl.ds(r * deep, deep), :].astype(BF16)
+
+    def copy(g):
+        return pltpu.make_async_copy(flat_ref.at[pl.ds(g * group, group)], rows_ref.at[g], sems.at[g])
+
+    for g in range(steps):
+        copy(g).start()
+    for g in range(steps):
+        copy(g).wait()
+        for t in range(half):
+            upper = rows_ref[g, :, pl.ds(t * LANES, LANES)].astype(F32)
+            lower = rows_ref[g, :, pl.ds((t + half) * LANES, LANES)].astype(F32)
+            even = jnp.where(left, upper, pltpu.roll(lower, LANES // 2, 1))
+            odd = jnp.where(left, pltpu.roll(upper, LANES // 2, 1), lower)
+            wide_ref[g, pl.ds(2 * t, group, stride=deep), :] = even
+            wide_ref[g, pl.ds(2 * t + 1, group, stride=deep), :] = odd
+        for r in range(group):
+            out_ref[g * group + r] = wide_ref[g, pl.ds(r * deep, deep), :].astype(BF16)
+
+
+def halves(flat):
+    rows, size = flat.shape
+    deep = size // LANES
+    group = 16
+    steps = rows // group
+    return pl.pallas_call(
+        halves_kernel,
+        out_shape=jax.ShapeDtypeStruct((rows, deep, LANES), BF16),
+        in_specs=[pl.BlockSpec(memory_space=pltpu.HBM)],
+        out_specs=vmem(),
+        scratch_shapes=[
+            pltpu.VMEM((steps, group, size), BF16),
+            pltpu.VMEM((steps, group * deep, LANES), F32),
+            pltpu.SemaphoreType.DMA((steps,)),
+        ],
+        compiler_params=params(),
+    )(pltpu.with_memory_space_constraint(flat, pltpu.HBM))
+
+
+def quarters_of(coarse_ref, quarters_ref, wide_ref):
     count = coarse_ref.shape[0]
-    deep2 = coarse_ref.shape[1] // LANES
+    deep = coarse_ref.shape[1] // LANES
     quarter = LANES // 4
     lane = lax.broadcasted_iota(I32, (count, LANES), 1) // quarter
-    for t in range(deep2 // 4):
-        tiles = [coarse_ref[:, pl.ds((h * deep2 // 4 + t) * LANES, LANES)].astype(F32) for h in range(4)]
+    for t in range(deep // 4):
+        tiles = [coarse_ref[:, pl.ds((h * deep // 4 + t) * LANES, LANES)].astype(F32) for h in range(4)]
         for u in range(4):
             total = None
             for h in range(4):
                 shift = (h - u) % 4 * quarter
                 piece = pltpu.roll(tiles[h], shift, 1) if shift else tiles[h]
                 total = piece if total is None else jnp.where(lane == h, piece, total)
-            wide_ref[pl.ds(4 * t + u, count, stride=deep2), :] = total
+            wide_ref[pl.ds(4 * t + u, count, stride=deep), :] = total
     for r in range(count):
-        quarters_ref[r] = wide_ref[pl.ds(r * deep2, deep2), :].astype(BF16)
-
-
-def halves(flat, coarse):
-    rows, size = flat.shape
-    count, size2 = coarse.shape
-    deep = size // LANES
-    deep2 = size2 // LANES
-    group = 16
-    steps = rows // group
-    group2 = count // steps
-    return pl.pallas_call(
-        halves_kernel,
-        grid=(steps,),
-        out_shape=(
-            jax.ShapeDtypeStruct((rows, deep, LANES), BF16),
-            jax.ShapeDtypeStruct((count, deep2, LANES), BF16),
-        ),
-        in_specs=[
-            pl.BlockSpec((group, size), lambda i: (i, 0)),
-            pl.BlockSpec((group2, size2), lambda i: (i, 0)),
-        ],
-        out_specs=(
-            pl.BlockSpec((group, deep, LANES), lambda i: (i, 0, 0)),
-            pl.BlockSpec((group2, deep2, LANES), lambda i: (i, 0, 0)),
-        ),
-        scratch_shapes=[pltpu.VMEM((group * deep, LANES), F32)],
-        compiler_params=params(),
-    )(flat, coarse)
+        quarters_ref[r] = wide_ref[pl.ds(r * deep, deep), :].astype(BF16)
 
 
 def index_kernel(
@@ -114,9 +124,12 @@
     slot2_ref,
     owner2_ref,
     place2_ref,
+    coarse_ref,
     plan_ref,
     target_ref,
+    quarters_ref,
     count_ref,
+    wide_ref,
     *,
     parts,
     capacity,
@@ -124,6 +137,7 @@
     owned,
     owned2,
 ):
+    quarters_of(coarse_ref, quarters_ref, wide_ref)
     region = where_ref[0]
     dom = where_ref[1]
     stencil, rows = cols_ref.shape
@@ -170,7 +184,7 @@
             col = cols_ref[k, i]
             step = jnp.where(col < first, 0, jnp.where(col >= first + span, 2, 1))
             begin = ((region + step - 1) * parts + dom) * rows
-            plan_ref[slots + here * stencil + k] = (col - begin) * 4 + step
+            plan_ref[slots + here * stencil + k] = (col - begin) * 4 + table_of(step, region)
             target_ref[there + k] = slot_ref[k, i] * owned + place
         return carry
 
@@ -191,9 +205,9 @@
     lax.fori_loop(0, rows2, coarse, 0)
 
 
-def terms_kernel(plan_ref, blocks_ref, before_ref, own_ref, after_ref, *rest, offsets, capacity, slots):
-    outs = rest[: len(offsets)]
-    buffer_ref, row_sem = rest[len(offsets) :]
+def terms_kernel(plan_ref, blocks_ref, before_ref, own_ref, after_ref, *rest, offsets, capacity, slots, waited):
+    outs = rest[waited : waited + len(offsets)]
+    buffer_ref, row_sem = rest[waited + len(offsets) :]
     stencil, width = buffer_ref.shape[1], buffer_ref.shape[2]
     half = width // 2
     narrow = LANES // 2
@@ -257,27 +271,29 @@
             one_row(n * capacity + r, offset * capacity + r, outs[n], r)
 
 
-def level_one(plan, blocks, before, own, after, offsets, capacity, slots):
+def level_one(plan, blocks, before, own, after, offsets, capacity, slots, waited):
     rows, stencil, width, _ = blocks.shape
     narrow = LANES // 2
     flat = narrow * narrow // LANES
     shape = jax.ShapeDtypeStruct((capacity * stencil * flat, LANES), BF16)
     count = len(offsets) * capacity
     return pl.pallas_call(
-        functools.partial(terms_kernel, offsets=offsets, capacity=capacity, slots=slots),
+        functools.partial(terms_kernel, offsets=offsets, capacity=capacity, slots=slots, waited=len(waited)),
         out_shape=tuple(shape for _ in offsets),
-        in_specs=[smem(), hbm(), vmem(), vmem(), vmem()],
+        in_specs=[smem(), hbm(), vmem(), vmem(), vmem()] + [hbm()] * len(waited),
         out_specs=tuple(vmem() for _ in offsets),
         scratch_shapes=[
             pltpu.VMEM((count, stencil, width, width), BF16),
             pltpu.SemaphoreType.DMA((count,)),
         ],
         compiler_params=params(),
-    )(plan, blocks, before, own, after)
-
-
-def pick_kernel(index_ref, before_ref, own_ref, after_ref, out_ref):
+    )(plan, pltpu.with_memory_space_constraint(blocks, pltpu.HBM), before, own, after, *waited)
+
+
+def pick_kernel(index_ref, first_ref, own_ref, second_ref, mine_ref, waited_ref, out_ref, turned_ref):
     stencil, count = index_ref.shape
+    quarter = LANES // 4
+    narrow = LANES // 2
 
     def body(q, carry):
         for k in range(stencil):
@@ -285,22 +301,40 @@
             row = lax.shift_right_logical(code, 2)
             step = code & 3
             out_ref[q * stencil + k] = jnp.where(
-                step == 0, before_ref[row], jnp.where(step == 1, own_ref[row], after_ref[row])
+                step == 0, first_ref[row], jnp.where(step == 1, own_ref[row], second_ref[row])
             )
         return carry
 
     lax.fori_loop(0, count, body, 0, unroll=4)
-
-
-def pick_rows(index, before, own, after):
+    row = lax.broadcasted_iota(I32, (quarter, LANES), 0)
+    lane = lax.broadcasted_iota(I32, (quarter, LANES), 1)
+    pick = jnp.where(lane == row % 8 * 4 + row // 8, 1.0, 0.0).astype(BF16)
+    old = lax.broadcasted_iota(I32, (narrow, narrow), 0)
+    new = lax.broadcasted_iota(I32, (narrow, narrow), 1)
+    order = jnp.where(old == new % quarter * 2 + new // quarter, 1.0, 0.0).astype(BF16)
+
+    def turn(q, carry):
+        packed = mine_ref[q]
+        column = jnp.concatenate([packed] + [pltpu.roll(packed, LANES - h * quarter, 1) for h in range(1, 4)], axis=0)
+        turned = lax.dot_general(pick, column, (((1,), (1,)), ((), ())), preferred_element_type=F32)
+        turned_ref[q] = jnp.dot(turned.astype(BF16), order, preferred_element_type=F32).astype(BF16)
+        return carry
+
+    lax.fori_loop(0, count, turn, 0, unroll=4)
+
+
+def pick_rows(index, first, own, second, mine, waited):
     stencil, count = index.shape
     return pl.pallas_call(
         pick_kernel,
-        out_shape=jax.ShapeDtypeStruct((count * stencil,) + own.shape[1:], own.dtype),
-        in_specs=[smem(), vmem(), vmem(), vmem()],
-        out_specs=vmem(),
+        out_shape=(
+            jax.ShapeDtypeStruct((count * stencil,) + own.shape[1:], own.dtype),
+            jax.ShapeDtypeStruct((count, LANES // 4, LANES // 2), own.dtype),
+        ),
+        in_specs=[smem(), vmem(), vmem(), vmem(), vmem(), hbm()],
+        out_specs=(vmem(), vmem()),
         compiler_params=params(),
-    )(index, before, own, after)
+    )(index, first, own, second, mine, waited)
 
 
 def owner_kernel(
@@ -343,9 +377,13 @@
     block = lax.broadcasted_iota(I32, (16, LANES), 1) // quarter
     none = jnp.zeros((16, LANES), BF16)
 
-    def second(d, carry):
-        for r in range(capacity2):
-            q = plan_ref[second_slot + d * capacity2 + r]
+    batch = 2
+
+    def second(step, carry):
+        places = [(step * batch + n, r) for n in range(batch) for r in range(capacity2)]
+        names = [plan_ref[second_slot + d * capacity2 + r] for d, r in places]
+        products = []
+        for q in names:
             rows = []
             weights = []
             for k in range(0, stencil, 2):
@@ -365,14 +403,15 @@
                     shift = (k - h) % 4 * quarter
                     turned = pltpu.roll(packed, shift, 1) if shift else packed
                     weights.append(jnp.where(block == k % 4, turned, none))
-            own = own_ref[q]
             groups = []
             for g in range((stencil + 3) // 4):
                 lhs = jnp.concatenate(rows[2 * g : 2 * g + 2], axis=1)
                 rhs = jnp.concatenate(weights[16 * g : 16 * g + 16], axis=0)
                 product = jnp.dot(lhs[:, : rhs.shape[0]], rhs, preferred_element_type=F32)
                 groups.append(product.astype(BF16))
-            term = jnp.dot(own, jnp.concatenate(groups, axis=1), preferred_element_type=F32)
+            products.append(jnp.concatenate(groups, axis=1))
+        terms = [jnp.dot(own_ref[q], p, preferred_element_type=F32) for q, p in zip(names, products)]
+        for (d, r), term in zip(places, terms):
             for k in range(stencil):
                 g = k // 4
                 total = None
@@ -385,7 +424,7 @@
                 term_ref[d, pl.ds((r * stencil + k) * 8, 8), :] = total
         return carry
 
-    lax.fori_loop(0, parts, second, 0, unroll=4)
+    lax.fori_loop(0, parts // batch, second, 0)
     for d in range(parts):
         sends[d][...] = term_ref[d].astype(BF16)
 
@@ -440,8 +479,8 @@
 
 
 def chunks_of(parts):
-    order = list(range(parts - 1, -1, -1))
-    return [(order[0],)] + [tuple(order[i : i + 2]) for i in range(1, parts - 1, 2)] + [(order[-1],)]
+    order = sorted(range(parts), key=lambda d: (-(d >> 1).bit_count(), -(d & 1), -d))
+    return [tuple(order[i : i + 2]) for i in range(0, parts, 2)]
 
 
 def local(
@@ -459,7 +498,6 @@
 ):
     rows, stencil, width, _ = fine_blocks.shape
     narrow = interp.shape[1] // width
-    narrow2 = coarse_interp.shape[1] // narrow
     parts = lax.axis_size("dom")
     region = lax.axis_index("region")
     dom = lax.axis_index("dom")
@@ -471,20 +509,22 @@
     slots2 = parts * capacity2
     where = jnp.stack([region, dom]).astype(I32)
 
-    own, quarters = halves(interp, coarse_interp)
-    before, after = neighbours(own, "region")
-
-    plan, target = pl.pallas_call(
+    own = halves(interp)
+    halo = neighbours(own, "region")
+
+    plan, target, quarters = pl.pallas_call(
         functools.partial(
             index_kernel, parts=parts, capacity=capacity, capacity2=capacity2, owned=owned, owned2=owned2
         ),
         out_shape=(
             jax.ShapeDtypeStruct((slots * (stencil + 1) + slots2,), I32),
             jax.ShapeDtypeStruct(((slots + slots2) * stencil,), I32),
+            jax.ShapeDtypeStruct((owned, coarse_interp.shape[1] // LANES, LANES), BF16),
         ),
-        in_specs=[smem()] * 8,
-        out_specs=(smem(),) * 2,
-        scratch_shapes=[pltpu.SMEM((parts,), I32)],
+        in_specs=[smem()] * 8 + [vmem()],
+        out_specs=(smem(), smem(), vmem()),
+        scratch_shapes=[pltpu.SMEM((parts,), I32), pltpu.VMEM((coarse_interp.size // LANES, LANES), F32)],
+        compiler_params=params(),
     )(
         where,
         fine_cols.T,
@@ -493,7 +533,8 @@
         fine_place,
         coarse_slot.T,
         coarse_owner[:, 0],
-        coarse_place,
+        lax.optimization_barrier((coarse_place, own))[0],
+        coarse_interp,
     )
 
     size2 = coarse_interp.shape[1]
@@ -501,27 +542,35 @@
     codes = jnp.pad(target, (0, extra * size2 - target.shape[0])).astype(BF16)
     stacked = jnp.concatenate([quarters, codes.reshape((extra,) + quarters.shape[1:])], axis=0)
     table = lax.all_gather(stacked, "dom", axis=0, tiled=True)
-    table_before, table_after = neighbours(table, "region")
     pitch = owned + extra
     targets = table.reshape((parts, pitch) + quarters.shape[1:])[:, owned:].reshape(parts, extra * size2)
     targets = targets[:, : target.shape[0]].astype(I32)
+
+    tables = neighbours(table, "region")
+    arrived = [None] * parts
+    chunks = chunks_of(parts)
+    sent = ()
+    for n, offsets in enumerate(chunks):
+        waited = tuple(sent[:1])
+        if n == 2:
+            waited = waited + tables
+        if n >= 3:
+            waited = waited + (arrived[chunks[n - 3][0]],)
+        sent = level_one(plan, fine_blocks, halo[0], own, halo[1], offsets, capacity, slots, waited)
+        for offset, cells in zip(offsets, sent):
+            arrived[offset] = exchange(cells, "dom", offset) if offset else cells
     span2 = parts * owned
     inside = coarse_cols % span2
-    index2 = (inside // owned * pitch + inside % owned) * 4 + coarse_cols // span2 - region + 1
-    picked = pick_rows(index2.T, table_before, table, table_after)
-    turned = coarse_interp.reshape(owned, narrow // 2, 2, narrow2 // 4, 4)
-    turned = turned.transpose(0, 4, 3, 2, 1).reshape(owned, narrow2, narrow)
-
-    arrived = [None] * parts
-    for offsets in chunks_of(parts):
-        sent = level_one(plan, fine_blocks, before, own, after, offsets, capacity, slots)
-        for offset, cells in zip(offsets, sent):
-            arrived[offset] = exchange(cells, "dom", offset) if offset else cells
+    step2 = table_of(coarse_cols // span2 - region + 1, region)
+    index2 = (inside // owned * pitch + inside % owned) * 4 + step2
+    picked, turned = pick_rows(index2.T, tables[0], table, tables[1], quarters, sent[0])
     outs = owner_level(
         where, targets, plan, picked, turned, arrived, parts, capacity, capacity2, owned, stencil
     )
     coarse_blocks = outs[0].reshape(stencil, owned, narrow * narrow).transpose(1, 0, 2)
-    arrived2 = [exchange(cells, "dom", d) if d else cells for d, cells in enumerate(outs[1:])]
+    arrived2 = list(outs[1:])
+    for d in range(parts - 1, 0, -1):
+        arrived2[d] = exchange(arrived2[d], "dom", d)
     second = final_level(where, targets, arrived2, parts, slots, capacity2, owned2, stencil)
     return (coarse_blocks, second)
 

time: 114 us -> 87.3 us (0.77)
  waiting for transfers between devices: 23.7 us -> 5.93 us
  local copies, waits for them, and re-layouts: 9.43 us -> 3.18 us
  starting transfers between devices: 25.8 us -> 22.6 us
  Pallas kernels: 42.1 us -> 43.6 us
  other arithmetic: 1.39 us -> 0.13 us
    ppermute x14, waiting for transfers between devices: 23.7 us -> 3.52 us  [exchange(): return lax.ppermute(cells, axis, [(i, i ^ offset) for i in range(count)])]
    pallas_call x2, Pallas kernels: 3.9 us -> 9.29 us  [the longest x1 6.66 us: pick_rows(): pl.pallas_call(pick_kernel, out_shape=(jax.ShapeDtypeStruct((count * sten...]
    ppermute x4, starting transfers between devices: 13 us -> 9.69 us  [neighbours(): lax.ppermute(cells, axis, [(i, partner(i, odd, count)) for i in range(cou...]
    transpose x1 -> x0, local copies, waits for them, and re-layouts: 2.8 us -> none  [local(): turned = turned.transpose(0, 4, 3, 2, 1).reshape(owned, narrow2, narrow)]
    pallas_call x5 -> x4, Pallas kernels: 23.4 us -> 20.9 us  [level_one(): pl.pallas_call(functools.partial(terms_kernel, offsets=offsets, capacity=...]
    ppermute x4, waiting for transfers between devices: 0.01 us -> 2.41 us  [neighbours(): lax.ppermute(cells, axis, [(i, partner(i, odd, count)) for i in range(cou...]
    unnamed x16 -> x27, local copies, waits for them, and re-layouts: 3.73 us -> 1.51 us
    pallas_call x1, Pallas kernels: 7.57 us -> 5.73 us  [owner_level(): pl.pallas_call(functools.partial(owner_kernel, parts=parts, capacity=capa...]
  transfers between devices with their start and end apart: 18 -> 18, of which waited for: 4 -> 4; matrix products, arithmetic and copies ran while one was open for 7% -> 2% of each run, Pallas kernels for 26% -> 38%
where the time goes in v3:
time: 87.3 us; the launch traced here: 87 us
  Pallas kernels  43.6 us (50%)
  starting transfers between devices  22.6 us (26%)
  blocking collectives  10.6 us (12%)
  waiting for transfers between devices  5.93 us (7%)
  local copies, waits for them, and re-layouts  3.18 us (4%)
  between operations  0.93 us (1%)
    pallas_call x4, Pallas kernels, level_one(): pl.pallas_call(functools.partial(terms_kernel, offsets=offsets, capacity=...  20.9 us
    ppermute x14, starting transfers between devices, exchange(): return lax.ppermute(cells, axis, [(i, i ^ offset) for i in range(count)])  12.9 us
    all_gather x1, blocking collectives, local(): table = lax.all_gather(stacked, 'dom', axis=0, tiled=True)  10.6 us
    ppermute x4, starting transfers between devices, neighbours(): lax.ppermute(cells, axis, [(i, partner(i, odd, count)) for i in range(cou...  9.69 us
    pallas_call x1, Pallas kernels, pick_rows(): pl.pallas_call(pick_kernel, out_shape=(jax.ShapeDtypeStruct((count * sten...  6.66 us
    pallas_call x1, Pallas kernels, owner_level(): pl.pallas_call(functools.partial(owner_kernel, parts=parts, capacity=capa...  5.73 us
    pallas_call x1, Pallas kernels, local(): pl.pallas_call(functools.partial(index_kernel, parts=parts, capacity=capa...  5.12 us
    ppermute x14, waiting for transfers between devices, exchange(): return lax.ppermute(cells, axis, [(i, i ^ offset) for i in range(count)])  3.52 us
  transfers between devices with their start and end apart: 18, of which 4 were waited for; matrix products, arithmetic and copies ran while one was open for 2% of the time, Pallas kernels for 38%

profile of v3, /device:TPU:0, one launch (start us, length us, event | category | flops | bytes accessed | tf_op | source)
XLA Modules:
  0.0 87.0 jit_solution(13179601520055213133)
XLA Ops:
  0.7 2.6 %shard_map.122.own_ref = bf16[48,64,128]{2,1,0:T(8,128)(2,1)S(1)} custom-call(bf16[48,8192]{1,0:T(8,128)(2,1)} %flat_ref.1), custom_call_target="tpu_custom_call" | custom-call | tf_op jit(solution)/shard_map/pallas_call | solution.py:86
  3.3 3.1 %collective-permute-start.2 = (bf16[48,64,128]{2,1,0:T(8,128)(2,1)S(1)}, bf16[48,64,128]{2,1,0:T(8,128)(2,1)S(1)}, u32[]{:S(2)}, u32[]{:S(2)}) collective-permute-start(bf16[48,64,128]{2,1,0:T(8,128)(2,1)S(1)} %shard_map.122.own_ref), channel_id=1, source_target_pairs={{0,8},{8,0},{16,24},{24,16},{1,9},{9,1},{17,25},{25,17},{2,10},{10... | collective-permute-start | bytes 2359304 | tf_op jit(solution)/shard_map/ppermute | solution.py:49
  6.4 0.7 collective-permute-start.3
  7.2 0.1 pad_add_fusion.where_ref
  7.3 5.1 %shard_map.123 = (s32[408]{0:T(512)S(1)}, s32[504]{0:T(512)S(1)}, bf16[24,16,128]{2,1,0:T(8,128)(2,1)S(1)}) custom-call(s32[2]{0:T(128)S(1)} %pad_add_fusion.where_ref, s32[7,48]{1,0:T(8,128)S(1)} %bitcast.17, s32[7,48]{1,0:T(8,128)S(1)} %bitcast.18, s32[48]{0:T(128)S(1)} %bitcast.20, s32[48]{0:T(128)S(1)} %copy-done.7, s32[7,24]{1,0:T(8,128)S(1)} %bitcast.19, ...), custom_call_target="tpu_custom_call" | custom-call | tf_op jit(solution)/shard_map/pallas_call | solution.py:515
  12.4 0.0 copy-start
  12.5 10.6 %all_gather.3.own_ref = bf16[200,16,128]{2,1,0:T(8,128)(2,1)S(1)} all-gather(bf16[25,16,128]{2,1,0:T(8,128)(2,1)S(1)} %pad_maximum_fusion), channel_id=1, replica_groups=mesh['region'=4,'dom'=8] {'dom'}, dimensions={0}, use_global_device_ids=true | all-gather | bytes 921600 | tf_op jit(solution)/shard_map/all_gather | solution.py:544
  23.0 4.3 %collective-permute-start = (bf16[200,16,128]{2,1,0:T(8,128)(2,1)S(1)}, bf16[200,16,128]{2,1,0:T(8,128)(2,1)}, u32[]{:S(2)}, u32[]{:S(2)}) collective-permute-start(bf16[200,16,128]{2,1,0:T(8,128)(2,1)S(1)} %all_gather.3.own_ref), channel_id=1, source_target_pairs={{0,8},{8,0},{16,24},{24,16},{1,9},{9,1},{17,25},{25,17},{2,10},{10... | collective-permute-start | bytes 2457608 | tf_op jit(solution)/shard_map/ppermute | solution.py:49
  27.4 1.6 %collective-permute-start.1 = (bf16[200,16,128]{2,1,0:T(8,128)(2,1)S(1)}, bf16[200,16,128]{2,1,0:T(8,128)(2,1)}, u32[]{:S(2)}, u32[]{:S(2)}) collective-permute-start(bf16[200,16,128]{2,1,0:T(8,128)(2,1)S(1)} %all_gather.3.own_ref), channel_id=1, source_target_pairs={{0,0},{8,16},{16,8},{24,24},{1,1},{9,17},{17,9},{25,25},{2,2},{10,... | collective-permute-start | bytes 2457608 | tf_op jit(solution)/shard_map/ppermute | solution.py:49
  28.9 0.0 collective-permute-done.2.before_ref
  28.9 0.0 collective-permute-done.3.after_ref
  28.9 5.2 %shard_map.124 = (bf16[1344,128]{1,0:T(8,128)(2,1)}, bf16[1344,128]{1,0:T(8,128)(2,1)S(1)}) custom-call(s32[408]{0:T(512)S(1)} %get-tuple-element.28.plan_ref, bf16[48,7,128,128]{3,2,1,0:T(8,128)(2,1)} %blocks_ref.7, bf16[48,64,128]{2,1,0:T(8,128)(2,1)S(1)} %collective-permute-done.2.before_ref, bf16[48,64,128]{2,1,0:T(8,128)(2,1)S(1)} %shard_map.122.own_ref, ...), custom_call_target="tpu_custom_call" | custom-call | tf_op jit(solution)/shard_map/pallas_call | solution.py:280
  34.2 0.7 copy-done.10
  34.9 1.1 %collective-permute-start.4 = (bf16[1344,128]{1,0:T(8,128)(2,1)}, bf16[1344,128]{1,0:T(8,128)(2,1)S(1)}, u32[]{:S(2)}, u32[]{:S(2)}) collective-permute-start(bf16[1344,128]{1,0:T(8,128)(2,1)} %get-tuple-element.29.rest_0_), channel_id=1, source_target_pairs={{0,7},{1,6},{2,5},{3,4},{4,3},{5,2},{6,1},{7,0},{8,15},{9,14},{10,... | collective-permute-start | bytes 1032200 | tf_op jit(solution)/shard_map/ppermute | solution.py:39
  36.0 5.2 %shard_map.125 = (bf16[1344,128]{1,0:T(8,128)(2,1)}, bf16[1344,128]{1,0:T(8,128)(2,1)S(1)}) custom-call(s32[408]{0:T(512)S(1)} %get-tuple-element.28.plan_ref, bf16[48,7,128,128]{3,2,1,0:T(8,128)(2,1)} %blocks_ref.7, bf16[48,64,128]{2,1,0:T(8,128)(2,1)S(1)} %collective-permute-done.2.before_ref, bf16[48,64,128]{2,1,0:T(8,128)(2,1)S(1)} %shard_map.122.own_ref, ...), custom_call_target="tpu_custom_call" | custom-call | tf_op jit(solution)/shard_map/pallas_call | solution.py:280
  41.3 0.7 copy-done.11
  42.0 1.5 %collective-permute-start.9 = (bf16[1344,128]{1,0:T(8,128)(2,1)}, bf16[1344,128]{1,0:T(8,128)(2,1)}, u32[]{:S(2)}, u32[]{:S(2)}) collective-permute-start(bf16[1344,128]{1,0:T(8,128)(2,1)} %get-tuple-element.30.rest_0_), channel_id=1, source_target_pairs={{0,5},{1,4},{2,7},{3,6},{4,1},{5,0},{6,3},{7,2},{8,13},{9,12},{10,... | collective-permute-start | bytes 1032200 | tf_op jit(solution)/shard_map/ppermute | solution.py:39
  43.5 0.3 collective-permute-start.7
  43.8 2.4 %collective-permute-done.rest_1_.first_ref = bf16[200,16,128]{2,1,0:T(8,128)(2,1)} collective-permute-done((bf16[200,16,128]{2,1,0:T(8,128)(2,1)S(1)}, bf16[200,16,128]{2,1,0:T(8,128)(2,1)}, u32[]{:S(2)}, u32[]{:S(2)}) %collective-permute-start) | collective-permute-done | bytes 819232 | tf_op jit(solution)/shard_map/ppermute | solution.py:49
  46.2 1.5 %collective-permute-start.10 = (bf16[1344,128]{1,0:T(8,128)(2,1)}, bf16[1344,128]{1,0:T(8,128)(2,1)S(1)}, u32[]{:S(2)}, u32[]{:S(2)}) collective-permute-start(bf16[1344,128]{1,0:T(8,128)(2,1)} %copy-done.10), channel_id=1, source_target_pairs={{0,6},{1,7},{2,4},{3,5},{4,2},{5,3},{6,0},{7,1},{8,14},{9,15},{10,... | collective-permute-start | bytes 1032200 | tf_op jit(solution)/shard_map/ppermute | solution.py:39
  47.7 0.0 collective-permute-done.1.rest_2_.second_ref
  47.7 5.2 %shard_map.126 = (bf16[1344,128]{1,0:T(8,128)(2,1)S(1)}, bf16[1344,128]{1,0:T(8,128)(2,1)S(1)}) custom-call(s32[408]{0:T(512)S(1)} %get-tuple-element.28.plan_ref, bf16[48,7,128,128]{3,2,1,0:T(8,128)(2,1)} %blocks_ref.7, bf16[48,64,128]{2,1,0:T(8,128)(2,1)S(1)} %collective-permute-done.2.before_ref, bf16[48,64,128]{2,1,0:T(8,128)(2,1)S(1)} %shard_map.122.own_ref, ...), custom_call_target="tpu_custom_call" | custom-call | tf_op jit(solution)/shard_map/pallas_call | solution.py:280
  52.9 1.6 %collective-permute-start.6 = (bf16[1344,128]{1,0:T(8,128)(2,1)S(1)}, bf16[1344,128]{1,0:T(8,128)(2,1)S(1)}, u32[]{:S(2)}, u32[]{:S(2)}) collective-permute-start(bf16[1344,128]{1,0:T(8,128)(2,1)S(1)} %get-tuple-element.36), channel_id=1, source_target_pairs={{0,2},{1,3},{2,0},{3,1},{4,6},{5,7},{6,4},{7,5},{8,10},{9,11},{10,... | collective-permute-start | bytes 1032200 | tf_op jit(solution)/shard_map/ppermute | solution.py:39
  54.5 0.0 collective-permute-done.4.rest_1_.rest_7_
  54.5 0.5 collective-permute-start.8
  55.0 5.2 %shard_map.127 = (bf16[1344,128]{1,0:T(8,128)(2,1)S(1)}, bf16[1344,128]{1,0:T(8,128)(2,1)S(1)}) custom-call(s32[408]{0:T(512)S(1)} %get-tuple-element.28.plan_ref, bf16[48,7,128,128]{3,2,1,0:T(8,128)(2,1)} %blocks_ref.7, bf16[48,64,128]{2,1,0:T(8,128)(2,1)S(1)} %collective-permute-done.2.before_ref, bf16[48,64,128]{2,1,0:T(8,128)(2,1)S(1)} %shard_map.122.own_ref, ...), custom_call_target="tpu_custom_call" | custom-call | tf_op jit(solution)/shard_map/pallas_call | solution.py:280
  60.2 0.0 collective-permute-done.9.rest_5_
  60.2 0.1 collective-permute-start.5
  60.4 6.7 %shard_map.128 = (bf16[168,16,128]{2,1,0:T(8,128)(2,1)S(1)}, bf16[24,32,64]{2,1,0:T(8,128)(2,1)S(1)}) custom-call(s32[7,24]{1,0:T(8,128)S(1)} %fusion.4.index_ref, bf16[200,16,128]{2,1,0:T(8,128)(2,1)} %collective-permute-done.rest_1_.first_ref, bf16[200,16,128]{2,1,0:T(8,128)(2,1)S(1)} %all_gather.3.own_ref, ...), custom_call_target="tpu_custom_call" | custom-call | tf_op jit(solution)/shard_map/pallas_call | solution.py:328
  67.0 0.0 collective-permute-done.7.rest_3_
  67.0 0.0 collective-permute-done.10.rest_6_
  67.1 1.9 %collective-permute-done.6.rest_2_ = bf16[1344,128]{1,0:T(8,128)(2,1)S(1)} collective-permute-done((bf16[1344,128]{1,0:T(8,128)(2,1)S(1)}, bf16[1344,128]{1,0:T(8,128)(2,1)S(1)}, u32[]{:S(2)}, u32[]{:S(2)}) %collective-permute-start.6) | collective-permute-done | bytes 344096 | tf_op jit(solution)/shard_map/ppermute | solution.py:39
  69.0 5.7 %shard_map.129 = (bf16[168,32,128]{2,1,0:T(8,128)(2,1)S(1)}, bf16[168,128]{1,0:T(8,128)(2,1)S(1)}, bf16[168,128]{1,0:T(8,128)(2,1)S(1)}, bf16[168,128]{1,0:T(8,1...) custom-call(s32[2]{0:T(128)S(1)} %pad_add_fusion.where_ref, ...), custom_call_target="tpu_custom_call" | custom-call | tf_op jit(solution)/shard_map/pallas_call | solution.py:435
  74.7 0.1 collective-permute-start.11
  74.8 1.5 %collective-permute-start.12 = (bf16[168,128]{1,0:T(8,128)(2,1)S(1)}, bf16[168,128]{1,0:T(8,128)(2,1)S(1)}, u32[]{:S(2)}, u32[]{:S(2)}) collective-permute-start(bf16[168,128]{1,0:T(8,128)(2,1)S(1)} %get-tuple-element.42), channel_id=1, source_target_pairs={{0,2},{1,3},{2,0},{3,1},{4,6},{5,7},{6,4},{7,5},{8,10},{9,11},{10,... | collective-permute-start | bytes 129032 | tf_op jit(solution)/shard_map/ppermute | solution.py:39
  76.3 0.4 collective-permute-start.13
  76.7 1.4 %collective-permute-start.14 = (bf16[168,128]{1,0:T(8,128)(2,1)S(1)}, bf16[168,128]{1,0:T(8,128)(2,1)S(1)}, u32[]{:S(2)}, u32[]{:S(2)}) collective-permute-start(bf16[168,128]{1,0:T(8,128)(2,1)S(1)} %get-tuple-element.44), channel_id=1, source_target_pairs={{0,4},{1,5},{2,6},{3,7},{4,0},{5,1},{6,2},{7,3},{8,12},{9,13},{10,... | collective-permute-start | bytes 129032 | tf_op jit(solution)/shard_map/ppermute | solution.py:39
  78.1 0.3 collective-permute-start.15
  78.3 0.0 collective-permute-done.11.rest_1_
  78.3 1.5 %collective-permute-start.16 = (bf16[168,128]{1,0:T(8,128)(2,1)S(1)}, bf16[168,128]{1,0:T(8,128)(2,1)S(1)}, u32[]{:S(2)}, u32[]{:S(2)}) collective-permute-start(bf16[168,128]{1,0:T(8,128)(2,1)S(1)} %get-tuple-element.46), channel_id=1, source_target_pairs={{0,6},{1,7},{2,4},{3,5},{4,2},{5,3},{6,0},{7,1},{8,14},{9,15},{10,... | collective-permute-start | bytes 129032 | tf_op jit(solution)/shard_map/ppermute | solution.py:39
  79.8 0.0 collective-permute-done.12.rest_2_
  79.8 1.2 %collective-permute-start.17 = (bf16[168,128]{1,0:T(8,128)(2,1)S(1)}, bf16[168,128]{1,0:T(8,128)(2,1)S(1)}, u32[]{:S(2)}, u32[]{:S(2)}) collective-permute-start(bf16[168,128]{1,0:T(8,128)(2,1)S(1)} %get-tuple-element.47), channel_id=1, source_target_pairs={{0,7},{1,6},{2,5},{3,4},{4,3},{5,2},{6,1},{7,0},{8,15},{9,14},{10,... | collective-permute-start | bytes 129032 | tf_op jit(solution)/shard_map/ppermute | solution.py:39
  81.0 1.7 %reshape.19 = bf16[7,24,4096]{2,1,0:T(8,128)(2,1)} reshape(bf16[168,32,128]{2,1,0:T(8,128)(2,1)S(1)} %get-tuple-element.39) | data formatting | bytes 2752512 | tf_op jit(solution)/shard_map/reshape | solution.py:570
  82.7 0.0 collective-permute-done.14.rest_4_
  82.7 0.0 collective-permute-done.15.rest_5_
  82.7 0.6 collective-permute-done.16.rest_6_
  83.3 1.0 %collective-permute-done.17.rest_7_ = bf16[168,128]{1,0:T(8,128)(2,1)S(1)} collective-permute-done((bf16[168,128]{1,0:T(8,128)(2,1)S(1)}, bf16[168,128]{1,0:T(8,128)(2,1)S(1)}, u32[]{:S(2)}, u32[]{:S(2)}) %collective-permute-start.17) | collective-permute-done | bytes 43040 | tf_op jit(solution)/shard_map/ppermute | solution.py:39
  84.3 2.7 %shard_map.130 = bf16[12,7,1024]{2,1,0:T(8,128)(2,1)} custom-call(s32[2]{0:T(128)S(1)} %pad_add_fusion.where_ref, s32[8,504]{1,0:T(8,128)S(1)} %slice_convert_fusion.target_ref, bf16[168,128]{1,0:T(8,128)(2,1)S(1)} %get-tuple-element.40.rest_0_, bf16[168,128]{1,0:T(8,128)(2,1)S(1)} %collective-permute-done.11.rest_1_, ...), custom_call_target="tpu_custom_call" | custom-call | tf_op jit(solution)/shard_map/pallas_call | solution.py:471
  (33 shorter events, 0.1 us)
Async XLA Ops:
  0.6 6.6 %copy-start.9 = (s32[24]{0:T(128)S(1)}, s32[24]{0:T(128)}, u32[]{:S(2)}) copy-start(s32[24]{0:T(128)} %place2_ref) | copy-start | bytes 292
  0.6 6.6 %copy-start.3 = (s32[48,7]{0,1:T(8,128)S(1)}, s32[48,7]{0,1:T(8,128)}, u32[]{:S(2)}) copy-start(s32[48,7]{0,1:T(8,128)} %param.13) | copy-start | bytes 4036
  0.7 6.6 %copy-start.4 = (s32[48,7]{0,1:T(8,128)S(1)}, s32[48,7]{0,1:T(8,128)}, u32[]{:S(2)}) copy-start(s32[48,7]{0,1:T(8,128)} %param.14) | copy-start | bytes 4036
  0.7 6.6 %copy-start.6 = (s32[48,1]{0,1:T(1,128)S(1)}, s32[48,1]{0,1:T(1,128)}, u32[]{:S(2)}) copy-start(s32[48,1]{0,1:T(1,128)} %param.15) | copy-start | bytes 580
  0.7 6.6 %copy-start.5 = (s32[24,7]{0,1:T(8,128)S(1)}, s32[24,7]{0,1:T(8,128)}, u32[]{:S(2)}) copy-start(s32[24,7]{0,1:T(8,128)} %param.19) | copy-start | bytes 2020
  0.7 6.6 %copy-start.8 = (s32[24,1]{0,1:T(1,128)S(1)}, s32[24,1]{0,1:T(1,128)}, u32[]{:S(2)}) copy-start(s32[24,1]{0,1:T(1,128)} %param.20) | copy-start | bytes 292
  0.7 6.6 %copy-start.7 = (s32[48]{0:T(128)S(1)}, s32[48]{0:T(128)}, u32[]{:S(2)}) copy-start(s32[48]{0:T(128)} %place_ref.1) | copy-start | bytes 580
  0.7 6.6 %copy-start.2 = (bf16[24,2048]{1,0:T(8,128)(2,1)S(1)}, bf16[24,2048]{1,0:T(8,128)(2,1)}, u32[]{:S(2)}) copy-start(bf16[24,2048]{1,0:T(8,128)(2,1)} %coarse_ref.1) | copy-start | bytes 294916
  3.3 25.6 %collective-permute-start.2 = (bf16[48,64,128]{2,1,0:T(8,128)(2,1)S(1)}, bf16[48,64,128]{2,1,0:T(8,128)(2,1)S(1)}, u32[]{:S(2)}, u32[]{:S(2)}) collective-permute-start(bf16[48,64,128]{2,1,0:T(8,128)(2,1)S(1)} %shard_map.122.own_ref), channel_id=1, source_target_pairs={{0,8},{8,0},{16,24},{24,16},{1,9},{9,1},{17,25},{25,17},{2,10},{10... | collective-permute-start | bytes 2359304 | tf_op jit(solution)/shard_map/ppermute | solution.py:49
  6.4 22.5 %collective-permute-start.3 = (bf16[48,64,128]{2,1,0:T(8,128)(2,1)S(1)}, bf16[48,64,128]{2,1,0:T(8,128)(2,1)S(1)}, u32[]{:S(2)}, u32[]{:S(2)}) collective-permute-start(bf16[48,64,128]{2,1,0:T(8,128)(2,1)S(1)} %shard_map.122.own_ref), channel_id=1, source_target_pairs={{0,0},{8,16},{16,8},{24,24},{1,1},{9,17},{17,9},{25,25},{2,2},{10,... | collective-permute-start | bytes 2359304 | tf_op jit(solution)/shard_map/ppermute | solution.py:49
  12.4 21.7 %copy-start = (bf16[24,16,128]{2,1,0:T(8,128)(2,1)}, bf16[24,16,128]{2,1,0:T(8,128)(2,1)S(1)}, u32[]{:S(2)}) copy-start(bf16[24,16,128]{2,1,0:T(8,128)(2,1)S(1)} %get-tuple-element.26.mine_ref) | copy-start | bytes 294916
  23.0 23.2 %collective-permute-start = (bf16[200,16,128]{2,1,0:T(8,128)(2,1)S(1)}, bf16[200,16,128]{2,1,0:T(8,128)(2,1)}, u32[]{:S(2)}, u32[]{:S(2)}) collective-permute-start(bf16[200,16,128]{2,1,0:T(8,128)(2,1)S(1)} %all_gather.3.own_ref), channel_id=1, source_target_pairs={{0,8},{8,0},{16,24},{24,16},{1,9},{9,1},{17,25},{25,17},{2,10},{10... | collective-permute-start | bytes 2457608 | tf_op jit(solution)/shard_map/ppermute | solution.py:49
  27.4 20.3 %collective-permute-start.1 = (bf16[200,16,128]{2,1,0:T(8,128)(2,1)S(1)}, bf16[200,16,128]{2,1,0:T(8,128)(2,1)}, u32[]{:S(2)}, u32[]{:S(2)}) collective-permute-start(bf16[200,16,128]{2,1,0:T(8,128)(2,1)S(1)} %all_gather.3.own_ref), channel_id=1, source_target_pairs={{0,0},{8,16},{16,8},{24,24},{1,1},{9,17},{17,9},{25,25},{2,2},{10,... | collective-permute-start | bytes 2457608 | tf_op jit(solution)/shard_map/ppermute | solution.py:49
  34.2 0.7 copy-start.10
  34.9 19.6 %collective-permute-start.4 = (bf16[1344,128]{1,0:T(8,128)(2,1)}, bf16[1344,128]{1,0:T(8,128)(2,1)S(1)}, u32[]{:S(2)}, u32[]{:S(2)}) collective-permute-start(bf16[1344,128]{1,0:T(8,128)(2,1)} %get-tuple-element.29.rest_0_), channel_id=1, source_target_pairs={{0,7},{1,6},{2,5},{3,4},{4,3},{5,2},{6,1},{7,0},{8,15},{9,14},{10,... | collective-permute-start | bytes 1032200 | tf_op jit(solution)/shard_map/ppermute | solution.py:39
  41.3 0.7 copy-start.11
  42.0 18.2 %collective-permute-start.9 = (bf16[1344,128]{1,0:T(8,128)(2,1)}, bf16[1344,128]{1,0:T(8,128)(2,1)}, u32[]{:S(2)}, u32[]{:S(2)}) collective-permute-start(bf16[1344,128]{1,0:T(8,128)(2,1)} %get-tuple-element.30.rest_0_), channel_id=1, source_target_pairs={{0,5},{1,4},{2,7},{3,6},{4,1},{5,0},{6,3},{7,2},{8,13},{9,12},{10,... | collective-permute-start | bytes 1032200 | tf_op jit(solution)/shard_map/ppermute | solution.py:39
  43.5 23.5 %collective-permute-start.7 = (bf16[1344,128]{1,0:T(8,128)(2,1)}, bf16[1344,128]{1,0:T(8,128)(2,1)S(1)}, u32[]{:S(2)}, u32[]{:S(2)}) collective-permute-start(bf16[1344,128]{1,0:T(8,128)(2,1)} %copy-done.11), channel_id=1, source_target_pairs={{0,3},{1,2},{2,1},{3,0},{4,7},{5,6},{6,5},{7,4},{8,11},{9,10},{10,... | collective-permute-start | bytes 1032200 | tf_op jit(solution)/shard_map/ppermute | solution.py:39
  46.2 20.8 %collective-permute-start.10 = (bf16[1344,128]{1,0:T(8,128)(2,1)}, bf16[1344,128]{1,0:T(8,128)(2,1)S(1)}, u32[]{:S(2)}, u32[]{:S(2)}) collective-permute-start(bf16[1344,128]{1,0:T(8,128)(2,1)} %copy-done.10), channel_id=1, source_target_pairs={{0,6},{1,7},{2,4},{3,5},{4,2},{5,3},{6,0},{7,1},{8,14},{9,15},{10,... | collective-permute-start | bytes 1032200 | tf_op jit(solution)/shard_map/ppermute | solution.py:39
  52.9 16.1 %collective-permute-start.6 = (bf16[1344,128]{1,0:T(8,128)(2,1)S(1)}, bf16[1344,128]{1,0:T(8,128)(2,1)S(1)}, u32[]{:S(2)}, u32[]{:S(2)}) collective-permute-start(bf16[1344,128]{1,0:T(8,128)(2,1)S(1)} %get-tuple-element.36), channel_id=1, source_target_pairs={{0,2},{1,3},{2,0},{3,1},{4,6},{5,7},{6,4},{7,5},{8,10},{9,11},{10,... | collective-permute-start | bytes 1032200 | tf_op jit(solution)/shard_map/ppermute | solution.py:39
  54.5 5.8 %copy-start.12 = (s32[24,7]{0,1:T(8,128)S(1)}, s32[24,7]{0,1:T(8,128)}, u32[]{:S(2)}) copy-start(s32[24,7]{0,1:T(8,128)} %param.18) | copy-start | bytes 2020
  54.5 5.9 %copy-start.1 = (bf16[24,16,128]{2,1,0:T(8,128)(2,1)S(1)}, bf16[24,16,128]{2,1,0:T(8,128)(2,1)}, u32[]{:S(2)}) copy-start(bf16[24,16,128]{2,1,0:T(8,128)(2,1)} %copy-done) | copy-start | bytes 294916
  54.5 14.5 %collective-permute-start.8 = (bf16[1344,128]{1,0:T(8,128)(2,1)S(1)}, bf16[1344,128]{1,0:T(8,128)(2,1)S(1)}, u32[]{:S(2)}, u32[]{:S(2)}) collective-permute-start(bf16[1344,128]{1,0:T(8,128)(2,1)S(1)} %get-tuple-element.31.rest_0_), channel_id=1, source_target_pairs={{0,4},{1,5},{2,6},{3,7},{4,0},{5,1},{6,2},{7,3},{8,12},{9,13},{10,... | collective-permute-start | bytes 1032200 | tf_op jit(solution)/shard_map/ppermute | solution.py:39
  60.2 8.7 %collective-permute-start.5 = (bf16[1344,128]{1,0:T(8,128)(2,1)S(1)}, bf16[1344,128]{1,0:T(8,128)(2,1)S(1)}, u32[]{:S(2)}, u32[]{:S(2)}) collective-permute-start(bf16[1344,128]{1,0:T(8,128)(2,1)S(1)} %get-tuple-element.32.waited_ref), channel_id=1, source_target_pairs={{0,1},{1,0},{2,3},{3,2},{4,5},{5,4},{6,7},{7,6},{8,9},{9,8},{10,11... | collective-permute-start | bytes 1032200 | tf_op jit(solution)/shard_map/ppermute | solution.py:39
  74.7 3.6 %collective-permute-start.11 = (bf16[168,128]{1,0:T(8,128)(2,1)S(1)}, bf16[168,128]{1,0:T(8,128)(2,1)S(1)}, u32[]{:S(2)}, u32[]{:S(2)}) collective-permute-start(bf16[168,128]{1,0:T(8,128)(2,1)S(1)} %get-tuple-element.41), channel_id=1, source_target_pairs={{0,1},{1,0},{2,3},{3,2},{4,5},{5,4},{6,7},{7,6},{8,9},{9,8},{10,11... | collective-permute-start | bytes 129032 | tf_op jit(solution)/shard_map/ppermute | solution.py:39
  74.8 5.0 %collective-permute-start.12 = (bf16[168,128]{1,0:T(8,128)(2,1)S(1)}, bf16[168,128]{1,0:T(8,128)(2,1)S(1)}, u32[]{:S(2)}, u32[]{:S(2)}) collective-permute-start(bf16[168,128]{1,0:T(8,128)(2,1)S(1)} %get-tuple-element.42), channel_id=1, source_target_pairs={{0,2},{1,3},{2,0},{3,1},{4,6},{5,7},{6,4},{7,5},{8,10},{9,11},{10,... | collective-permute-start | bytes 129032 | tf_op jit(solution)/shard_map/ppermute | solution.py:39
  76.3 6.4 %collective-permute-start.13 = (bf16[168,128]{1,0:T(8,128)(2,1)S(1)}, bf16[168,128]{1,0:T(8,128)(2,1)S(1)}, u32[]{:S(2)}, u32[]{:S(2)}) collective-permute-start(bf16[168,128]{1,0:T(8,128)(2,1)S(1)} %get-tuple-element.43), channel_id=1, source_target_pairs={{0,3},{1,2},{2,1},{3,0},{4,7},{5,6},{6,5},{7,4},{8,11},{9,10},{10,... | collective-permute-start | bytes 129032 | tf_op jit(solution)/shard_map/ppermute | solution.py:39
  76.7 6.1 %collective-permute-start.14 = (bf16[168,128]{1,0:T(8,128)(2,1)S(1)}, bf16[168,128]{1,0:T(8,128)(2,1)S(1)}, u32[]{:S(2)}, u32[]{:S(2)}) collective-permute-start(bf16[168,128]{1,0:T(8,128)(2,1)S(1)} %get-tuple-element.44), channel_id=1, source_target_pairs={{0,4},{1,5},{2,6},{3,7},{4,0},{5,1},{6,2},{7,3},{8,12},{9,13},{10,... | collective-permute-start | bytes 129032 | tf_op jit(solution)/shard_map/ppermute | solution.py:39
  78.1 4.6 %collective-permute-start.15 = (bf16[168,128]{1,0:T(8,128)(2,1)S(1)}, bf16[168,128]{1,0:T(8,128)(2,1)S(1)}, u32[]{:S(2)}, u32[]{:S(2)}) collective-permute-start(bf16[168,128]{1,0:T(8,128)(2,1)S(1)} %get-tuple-element.45), channel_id=1, source_target_pairs={{0,5},{1,4},{2,7},{3,6},{4,1},{5,0},{6,3},{7,2},{8,13},{9,12},{10,... | collective-permute-start | bytes 129032 | tf_op jit(solution)/shard_map/ppermute | solution.py:39
  78.3 4.9 %collective-permute-start.16 = (bf16[168,128]{1,0:T(8,128)(2,1)S(1)}, bf16[168,128]{1,0:T(8,128)(2,1)S(1)}, u32[]{:S(2)}, u32[]{:S(2)}) collective-permute-start(bf16[168,128]{1,0:T(8,128)(2,1)S(1)} %get-tuple-element.46), channel_id=1, source_target_pairs={{0,6},{1,7},{2,4},{3,5},{4,2},{5,3},{6,0},{7,1},{8,14},{9,15},{10,... | collective-permute-start | bytes 129032 | tf_op jit(solution)/shard_map/ppermute | solution.py:39
  79.8 4.5 %collective-permute-start.17 = (bf16[168,128]{1,0:T(8,128)(2,1)S(1)}, bf16[168,128]{1,0:T(8,128)(2,1)S(1)}, u32[]{:S(2)}, u32[]{:S(2)}) collective-permute-start(bf16[168,128]{1,0:T(8,128)(2,1)S(1)} %get-tuple-element.47), channel_id=1, source_target_pairs={{0,7},{1,6},{2,5},{3,4},{4,3},{5,2},{6,1},{7,0},{8,15},{9,14},{10,... | collective-permute-start | bytes 129032 | tf_op jit(solution)/shard_map/ppermute | solution.py:39

commit v4 on v3

--- a/solution.py
+++ b/solution.py
@@ -115,7 +115,38 @@
         quarters_ref[r] = wide_ref[pl.ds(r * deep, deep), :].astype(BF16)
 
 
-def index_kernel(
+def owner_order(owner_ref, wide_ref, capacity):
+    count = owner_ref.shape[1]
+    square = (LANES, LANES)
+    down = lax.broadcasted_iota(I32, square, 0).astype(F32)
+    along = lax.broadcasted_iota(I32, square, 1).astype(F32)
+    wide_ref[...] = jnp.full(wide_ref.shape, -1.0, F32)
+    wide_ref[0:1, 0:count] = owner_ref[...].astype(F32)
+    owner = wide_ref[0:1, :]
+    across = jnp.broadcast_to(owner, square)
+    earlier = jnp.where((across == across.T) & (down < along), 1.0, 0.0)
+    rank = jnp.sum(earlier, axis=0, keepdims=True)
+    position = jnp.where(owner >= 0.0, owner * capacity + rank, -1.0)
+    named = jnp.broadcast_to(position, square).T == along
+    hit = jnp.sum(jnp.where(named, 1.0, 0.0), axis=0, keepdims=True)
+    row = jnp.sum(jnp.where(named, down, 0.0), axis=0, keepdims=True)
+    return (row + (1.0 - hit) * count).astype(I32)
+
+
+def index_kernel(where_ref, *rest, **sizes):
+    inputs = rest[:8]
+    info_ref, stacked_ref, wide_ref, narrow_ref = rest[9:13]
+    locals_ = rest[13:21]
+    sems = rest[21]
+    copies = [pltpu.make_async_copy(a, b, sems.at[n]) for n, (a, b) in enumerate(zip(inputs, locals_))]
+    for copy in copies:
+        copy.start()
+    for copy in copies:
+        copy.wait()
+    fill_tables(where_ref, *locals_, info_ref, stacked_ref, wide_ref, narrow_ref, **sizes)
+
+
+def fill_tables(
     where_ref,
     cols_ref,
     slot_ref,
@@ -125,11 +156,10 @@
     owner2_ref,
     place2_ref,
     coarse_ref,
-    plan_ref,
-    target_ref,
-    quarters_ref,
-    count_ref,
+    info_ref,
+    stacked_ref,
     wide_ref,
+    narrow_ref,
     *,
     parts,
     capacity,
@@ -137,88 +167,50 @@
     owned,
     owned2,
 ):
-    quarters_of(coarse_ref, quarters_ref, wide_ref)
     region = where_ref[0]
     dom = where_ref[1]
     stencil, rows = cols_ref.shape
     rows2 = slot2_ref.shape[1]
+    group = stencil + 1
     span = parts * rows
     first = region * span
-    slots = parts * capacity
-    slots2 = parts * capacity2
-    second = slots * (stencil + 1)
-
-    def clear_counts(d, carry):
-        count_ref[d] = 0
-        return carry
-
-    if slots > rows or slots2 > rows2:
-
-        def clear(p, carry):
-            plan_ref[p] = 0
-            for k in range(stencil):
-                plan_ref[slots + p * stencil + k] = 1
-                target_ref[p * stencil + k] = stencil * owned
-            return carry
-
-        lax.fori_loop(0, slots, clear, 0)
-
-        def clear2(p, carry):
-            plan_ref[second + p] = 0
-            for k in range(stencil):
-                target_ref[(slots + p) * stencil + k] = (stencil + 1) * owned2
-            return carry
-
-        lax.fori_loop(0, slots2, clear2, 0)
-    lax.fori_loop(0, parts, clear_counts, 0)
-
-    def fine(i, carry):
-        owner = owner_ref[i]
-        rank = count_ref[owner]
-        count_ref[owner] = rank + 1
-        here = (owner ^ dom) * capacity + rank
-        there = (owner * capacity + rank) * stencil
-        place = place_ref[i]
-        plan_ref[here] = i
-        for k in range(stencil):
-            col = cols_ref[k, i]
-            step = jnp.where(col < first, 0, jnp.where(col >= first + span, 2, 1))
-            begin = ((region + step - 1) * parts + dom) * rows
-            plan_ref[slots + here * stencil + k] = (col - begin) * 4 + table_of(step, region)
-            target_ref[there + k] = slot_ref[k, i] * owned + place
-        return carry
-
-    lax.fori_loop(0, rows, fine, 0)
-    lax.fori_loop(0, parts, clear_counts, 0)
-
-    def coarse(i, carry):
-        owner = owner2_ref[i]
-        rank = count_ref[owner]
-        count_ref[owner] = rank + 1
-        plan_ref[second + (owner ^ dom) * capacity2 + rank] = i
-        there = (slots + owner * capacity2 + rank) * stencil
-        place = place2_ref[i]
-        for k in range(stencil):
-            target_ref[there + k] = place * (stencil + 1) + slot2_ref[k, i]
-        return carry
-
-    lax.fori_loop(0, rows2, coarse, 0)
-
-
-def terms_kernel(plan_ref, blocks_ref, before_ref, own_ref, after_ref, *rest, offsets, capacity, slots, waited):
+    quarters_of(coarse_ref, stacked_ref, wide_ref)
+    info_ref[0:group, :] = jnp.full((group, LANES), stencil * owned, I32)
+    info_ref[group : 2 * group, :] = jnp.full((group, LANES), group * owned2, I32)
+    info_ref[2 * group :, :] = jnp.full((group, LANES), dom, I32)
+    info_ref[0:stencil, 0:rows] = slot_ref[...] * owned + place_ref[...]
+    info_ref[group : group + stencil, 0:rows2] = place2_ref[...] * group + slot2_ref[...]
+    cols = cols_ref[...]
+    step = jnp.where(cols < first, 0, jnp.where(cols >= first + span, 2, 1))
+    begin = ((region + step - 1) * parts + dom) * rows
+    info_ref[2 * group : 2 * group + stencil, 0:rows] = (cols - begin) * 4 + table_of(step, region)
+    info_ref[stencil : stencil + 1, :] = owner_order(owner_ref, narrow_ref, capacity)
+    info_ref[group + stencil : 2 * group, :] = owner_order(owner2_ref, narrow_ref, capacity2)
+    stacked_ref[rows2] = info_ref[0 : 2 * group, :].astype(F32).astype(BF16)
+
+
+def terms_kernel(table_ref, blocks_ref, before_ref, own_ref, after_ref, *rest, offsets, capacity, waited):
     outs = rest[waited : waited + len(offsets)]
-    buffer_ref, row_sem = rest[waited + len(offsets) :]
+    info_ref, buffer_ref, info_sem, row_sem = rest[waited + len(offsets) :]
     stencil, width = buffer_ref.shape[1], buffer_ref.shape[2]
     half = width // 2
     narrow = LANES // 2
     flat = narrow * narrow // LANES
 
-    def row_copy(n, slot):
-        return pltpu.make_async_copy(blocks_ref.at[plan_ref[slot]], buffer_ref.at[n], row_sem.at[n])
+    table_copy = pltpu.make_async_copy(table_ref, info_ref, info_sem)
+    table_copy.start()
+    table_copy.wait()
+    dom = info_ref[3 * (stencil + 1) - 1, 0]
+
+    def source_of(offset, r):
+        return jnp.minimum(info_ref[stencil, (dom ^ offset) * capacity + r], own_ref.shape[0] - 1)
+
+    def row_copy(n, source):
+        return pltpu.make_async_copy(blocks_ref.at[source], buffer_ref.at[n], row_sem.at[n])
 
     for n, offset in enumerate(offsets):
         for r in range(capacity):
-            row_copy(n * capacity + r, offset * capacity + r).start()
+            row_copy(n * capacity + r, source_of(offset, r)).start()
 
     left = low_lanes((half, LANES), narrow)
     left_flat = low_lanes((flat, LANES), narrow)
@@ -228,25 +220,25 @@
     pick = jnp.where(in_col == chosen, 1.0, 0.0).astype(BF16)
     zero = jnp.zeros((half, LANES), BF16)
 
-    def neighbour(slot, k):
-        code = plan_ref[slots + slot * stencil + k]
+    def neighbour(source, k):
+        code = info_ref[2 * (stencil + 1) + k, source]
         row = lax.shift_right_logical(code, 2)
         step = code & 3
         return jnp.where(step == 0, before_ref[row], jnp.where(step == 1, own_ref[row], after_ref[row]))
 
-    def one_row(n, slot, out_ref, r):
-        mine = own_ref[plan_ref[slot]]
+    def one_row(n, source, out_ref, r):
+        mine = own_ref[source]
         column = jnp.concatenate([mine, pltpu.roll(mine, narrow, 1)], axis=0)
         turned = lax.dot_general(
             pick, column, (((1,), (1,)), ((), ())), preferred_element_type=F32
         ).astype(BF16)
         products = []
         for k in range(0, stencil, 2):
-            one = neighbour(slot, k)
+            one = neighbour(source, k)
             weights = [jnp.where(left, one, zero), jnp.where(left, pltpu.roll(one, narrow, 1), zero)]
             lhs = buffer_ref[n, k]
             if k + 1 < stencil:
-                two = neighbour(slot, k + 1)
+                two = neighbour(source, k + 1)
                 weights += [jnp.where(left, zero, pltpu.roll(two, narrow, 1)), jnp.where(left, zero, two)]
                 lhs = jnp.concatenate([lhs, buffer_ref[n, k + 1]], axis=1)
             products.append(
@@ -265,29 +257,39 @@
                 ).astype(BF16)
 
     for n, offset in enumerate(offsets):
-        for r in range(capacity):
-            row_copy(n * capacity + r, offset * capacity + r).wait()
-        for r in range(capacity):
-            one_row(n * capacity + r, offset * capacity + r, outs[n], r)
-
-
-def level_one(plan, blocks, before, own, after, offsets, capacity, slots, waited):
+        sources = [source_of(offset, r) for r in range(capacity)]
+        for r, source in enumerate(sources):
+            row_copy(n * capacity + r, source).wait()
+        for r, source in enumerate(sources):
+            one_row(n * capacity + r, source, outs[n], r)
+
+
+def level_one(info, blocks, before, own, after, offsets, capacity, waited):
     rows, stencil, width, _ = blocks.shape
     narrow = LANES // 2
     flat = narrow * narrow // LANES
     shape = jax.ShapeDtypeStruct((capacity * stencil * flat, LANES), BF16)
     count = len(offsets) * capacity
     return pl.pallas_call(
-        functools.partial(terms_kernel, offsets=offsets, capacity=capacity, slots=slots, waited=len(waited)),
+        functools.partial(terms_kernel, offsets=offsets, capacity=capacity, waited=len(waited)),
         out_shape=tuple(shape for _ in offsets),
-        in_specs=[smem(), hbm(), vmem(), vmem(), vmem()] + [hbm()] * len(waited),
+        in_specs=[hbm(), hbm(), vmem(), vmem(), vmem()] + [hbm()] * len(waited),
         out_specs=tuple(vmem() for _ in offsets),
         scratch_shapes=[
+            pltpu.SMEM(info.shape, I32),
             pltpu.VMEM((count, stencil, width, width), BF16),
+            pltpu.SemaphoreType.DMA(()),
             pltpu.SemaphoreType.DMA((count,)),
         ],
         compiler_params=params(),
-    )(plan, pltpu.with_memory_space_constraint(blocks, pltpu.HBM), before, own, after, *waited)
+    )(
+        pltpu.with_memory_space_constraint(info, pltpu.HBM),
+        pltpu.with_memory_space_constraint(blocks, pltpu.HBM),
+        before,
+        own,
+        after,
+        *waited,
+    )
 
 
 def pick_kernel(index_ref, first_ref, own_ref, second_ref, mine_ref, waited_ref, out_ref, turned_ref):
@@ -306,21 +308,32 @@
         return carry
 
     lax.fori_loop(0, count, body, 0, unroll=4)
-    row = lax.broadcasted_iota(I32, (quarter, LANES), 0)
-    lane = lax.broadcasted_iota(I32, (quarter, LANES), 1)
-    pick = jnp.where(lane == row % 8 * 4 + row // 8, 1.0, 0.0).astype(BF16)
-    old = lax.broadcasted_iota(I32, (narrow, narrow), 0)
-    new = lax.broadcasted_iota(I32, (narrow, narrow), 1)
+    square = (LANES, LANES)
+    row = lax.broadcasted_iota(I32, square, 0)
+    lane = lax.broadcasted_iota(I32, square, 1)
+    old = row // quarter * quarter + row % 8 * 4 + row % quarter // 8
+    pick = jnp.where(lane == old, 1.0, 0.0).astype(BF16)
+    new = lax.broadcasted_iota(I32, (narrow, narrow), 0)
+    old = lax.broadcasted_iota(I32, (narrow, narrow), 1)
     order = jnp.where(old == new % quarter * 2 + new // quarter, 1.0, 0.0).astype(BF16)
-
-    def turn(q, carry):
-        packed = mine_ref[q]
-        column = jnp.concatenate([packed] + [pltpu.roll(packed, LANES - h * quarter, 1) for h in range(1, 4)], axis=0)
-        turned = lax.dot_general(pick, column, (((1,), (1,)), ((), ())), preferred_element_type=F32)
-        turned_ref[q] = jnp.dot(turned.astype(BF16), order, preferred_element_type=F32).astype(BF16)
-        return carry
-
-    lax.fori_loop(0, count, turn, 0, unroll=4)
+    block = lax.broadcasted_iota(I32, (16, LANES), 1) // quarter
+    columns = []
+    for g in range(count // 4):
+        pieces = []
+        for h in range(4):
+            total = None
+            for n in range(4):
+                shift = (n - h) % 4 * quarter
+                piece = mine_ref[4 * g + n]
+                piece = pltpu.roll(piece, shift, 1) if shift else piece
+                total = piece if total is None else jnp.where(block == n, piece, total)
+            pieces.append(total)
+        columns.append(jnp.concatenate(pieces, axis=0))
+    ordered = [jnp.dot(order, column, preferred_element_type=F32).astype(BF16) for column in columns]
+    for g, column in enumerate(ordered):
+        turned = lax.dot_general(pick, column, (((1,), (1,)), ((), ())), preferred_element_type=F32).astype(BF16)
+        for n in range(4):
+            turned_ref[4 * g + n] = turned[n * quarter : (n + 1) * quarter]
 
 
 def pick_rows(index, first, own, second, mine, waited):
@@ -337,39 +350,58 @@
     )(index, first, own, second, mine, waited)
 
 
+def add_terms(dom, target_ref, arrived, offsets, sum_ref, capacity, stencil):
+    flat = sum_ref.shape[1]
+    for d, part_ref in zip(offsets, arrived):
+        base = (dom ^ d) * 2 * (stencil + 1)
+        for r in range(capacity):
+            row = target_ref[base + stencil, dom * capacity + r]
+            for k in range(stencil):
+                target = target_ref[base + k, row]
+                sum_ref[target] += part_ref[pl.ds((r * stencil + k) * flat, flat), :].astype(F32)
+
+
+def early_kernel(where_ref, target_ref, *rest, offsets, capacity, stencil):
+    sum_ref = rest[-1]
+    sum_ref[...] = jnp.zeros(sum_ref.shape, F32)
+    add_terms(where_ref[1], target_ref, rest[: len(offsets)], offsets, sum_ref, capacity, stencil)
+
+
+def early_sums(where, targets, waited, arrived, offsets, capacity, owned, stencil):
+    return pl.pallas_call(
+        functools.partial(early_kernel, offsets=offsets, capacity=capacity, stencil=stencil),
+        out_shape=jax.ShapeDtypeStruct((stencil * owned + 1, LANES // 4, LANES), F32),
+        in_specs=[smem(), smem()] + [vmem()] * len(offsets) + [hbm()],
+        out_specs=vmem(),
+        compiler_params=params(),
+    )(where, targets, *arrived, waited)
+
+
 def owner_kernel(
     where_ref,
     target_ref,
-    plan_ref,
     picked_ref,
     own_ref,
+    early_ref,
     *rest,
     parts,
+    offsets,
     capacity,
     capacity2,
     owned,
     stencil,
 ):
-    arrived = rest[:parts]
-    out_ref = rest[parts]
-    sends = rest[parts + 1 : 2 * parts + 1]
-    sum_ref, term_ref = rest[2 * parts + 1 :]
+    arrived = rest[: len(offsets)]
+    out_ref = rest[len(offsets)]
+    sum_ref = rest[len(offsets) + 1]
+    sends = rest[len(offsets) + 2 : len(offsets) + 2 + parts]
+    (term_ref,) = rest[len(offsets) + 2 + parts :]
     dom = where_ref[1]
-    second_slot = parts * capacity * (stencil + 1)
+    group = stencil + 1
+    mine = dom * 2 * group
     flat = sum_ref.shape[1]
     narrow = LANES // 2
-    sum_ref[...] = jnp.zeros(sum_ref.shape, F32)
-    for d in range(parts):
-        part_ref = arrived[d]
-
-        def add(r, carry, d=d, part_ref=part_ref):
-            base = (dom * capacity + r) * stencil
-            for k in range(stencil):
-                target = target_ref[dom ^ d, base + k]
-                sum_ref[target] += part_ref[pl.ds((r * stencil + k) * flat, flat), :].astype(F32)
-            return carry
-
-        lax.fori_loop(0, capacity, add, 0, unroll=True)
+    add_terms(dom, target_ref, arrived, offsets, sum_ref, capacity, stencil)
 
     left = low_lanes((flat, LANES), narrow)
     quarter = LANES // 4
@@ -381,7 +413,9 @@
 
     def second(step, carry):
         places = [(step * batch + n, r) for n in range(batch) for r in range(capacity2)]
-        names = [plan_ref[second_slot + d * capacity2 + r] for d, r in places]
+        names = [
+            jnp.minimum(target_ref[mine + 2 * group - 1, (dom ^ d) * capacity2 + r], owned - 1) for d, r in places
+        ]
         products = []
         for q in names:
             rows = []
@@ -429,53 +463,65 @@
         sends[d][...] = term_ref[d].astype(BF16)
 
 
-def owner_level(where, targets, plan, picked, own, arrived, parts, capacity, capacity2, owned, stencil):
+def owner_level(where, targets, picked, own, early, arrived, offsets, parts, capacity, capacity2, owned, stencil):
     flat = LANES // 4
     send = jax.ShapeDtypeStruct((capacity2 * stencil * 8, LANES), BF16)
     return pl.pallas_call(
         functools.partial(
-            owner_kernel, parts=parts, capacity=capacity, capacity2=capacity2, owned=owned, stencil=stencil
+            owner_kernel,
+            parts=parts,
+            offsets=offsets,
+            capacity=capacity,
+            capacity2=capacity2,
+            owned=owned,
+            stencil=stencil,
         ),
-        out_shape=(jax.ShapeDtypeStruct((stencil * owned, flat, LANES), BF16),) + (send,) * parts,
-        in_specs=[smem(), smem(), smem()] + [vmem()] * (2 + parts),
-        out_specs=(vmem(),) * (1 + parts),
-        scratch_shapes=[
-            pltpu.VMEM((stencil * owned + 1, flat, LANES), F32),
-            pltpu.VMEM((parts, capacity2 * stencil * 8, LANES), F32),
-        ],
+        out_shape=(
+            jax.ShapeDtypeStruct((stencil * owned, flat, LANES), BF16),
+            jax.ShapeDtypeStruct(early.shape, F32),
+        )
+        + (send,) * parts,
+        in_specs=[smem(), smem()] + [vmem()] * (3 + len(offsets)),
+        out_specs=(vmem(),) * (2 + parts),
+        scratch_shapes=[pltpu.VMEM((parts, capacity2 * stencil * 8, LANES), F32)],
+        input_output_aliases={4: 1},
         compiler_params=params(),
-    )(where, targets, plan, picked, own, *arrived)
-
-
-def final_kernel(where_ref, target_ref, *rest, parts, first, capacity2, stencil):
-    arrived = rest[:parts]
+    )(where, targets, picked, own, early, *arrived)
+
+
+def final_kernel(where_ref, target_ref, *rest, parts, capacity2, stencil):
+    arrived = rest[:parts][::-1]
     out_ref = rest[parts]
-    (sum_ref,) = rest[parts + 1 :]
+    sum_ref, other_ref = rest[parts + 1 :]
     dom = where_ref[1]
     deep = stencil + 1
+    other_ref[...] = jnp.zeros(other_ref.shape, F32)
     sum_ref[...] = jnp.zeros(sum_ref.shape, F32)
-    for d in range(parts):
-        values = arrived[d][...].astype(F32)
+    for d in range(0, parts, 2):
+        pairs = [(sum_ref, d), (other_ref, d + 1)]
+        values = [arrived[e][...].astype(F32) for _, e in pairs]
         for r in range(capacity2):
-            base = (first + dom * capacity2 + r) * stencil
+            bases = [((dom ^ e) * 2 + 1) * deep for _, e in pairs]
+            rows = [target_ref[base + stencil, dom * capacity2 + r] for base in bases]
             for k in range(stencil):
                 at = r * stencil + k
-                sum_ref[target_ref[dom ^ d, base + k]] += values[at * 8 : (at + 1) * 8]
+                for (into_ref, _), base, row, value in zip(pairs, bases, rows, values):
+                    into_ref[target_ref[base + k, row]] += value[at * 8 : (at + 1) * 8]
     for u in range(out_ref.shape[0]):
         for t in range(8):
-            tile = sum_ref[pl.ds(u * deep, deep), t, :]
+            tile = sum_ref[pl.ds(u * deep, deep), t, :] + other_ref[pl.ds(u * deep, deep), t, :]
             out_ref[u, :, pl.ds(t * LANES, LANES)] = tile[:stencil].astype(BF16)
 
 
-def final_level(where, targets, arrived, parts, first, capacity2, owned2, stencil):
+def final_level(where, targets, arrived, parts, capacity2, owned2, stencil):
     return pl.pallas_call(
-        functools.partial(final_kernel, parts=parts, first=first, capacity2=capacity2, stencil=stencil),
+        functools.partial(final_kernel, parts=parts, capacity2=capacity2, stencil=stencil),
         out_shape=jax.ShapeDtypeStruct((owned2, stencil, 8 * LANES), BF16),
         in_specs=[smem(), smem()] + [vmem()] * parts,
         out_specs=vmem(),
-        scratch_shapes=[pltpu.VMEM((owned2 * (stencil + 1) + 1, 8, LANES), F32)],
+        scratch_shapes=[pltpu.VMEM((owned2 * (stencil + 1) + 1, 8, LANES), F32)] * 2,
         compiler_params=params(),
-    )(where, targets, *arrived)
+    )(where, targets, *arrived[::-1])
 
 
 def chunks_of(parts):
@@ -505,46 +551,42 @@
     owned2 = owned // 2
     capacity = max(2, rows // 8)
     capacity2 = max(2, owned // 8)
-    slots = parts * capacity
-    slots2 = parts * capacity2
     where = jnp.stack([region, dom]).astype(I32)
 
     own = halves(interp)
     halo = neighbours(own, "region")
 
-    plan, target, quarters = pl.pallas_call(
+    size2 = coarse_interp.shape[1]
+    group = stencil + 1
+    inputs = [
+        fine_cols.T,
+        fine_slot.T,
+        fine_owner.T,
+        fine_place.reshape(1, rows),
+        coarse_slot.T,
+        coarse_owner.T,
+        coarse_place.reshape(1, owned),
+        coarse_interp,
+    ]
+    info, stacked = pl.pallas_call(
         functools.partial(
             index_kernel, parts=parts, capacity=capacity, capacity2=capacity2, owned=owned, owned2=owned2
         ),
         out_shape=(
-            jax.ShapeDtypeStruct((slots * (stencil + 1) + slots2,), I32),
-            jax.ShapeDtypeStruct(((slots + slots2) * stencil,), I32),
-            jax.ShapeDtypeStruct((owned, coarse_interp.shape[1] // LANES, LANES), BF16),
+            jax.ShapeDtypeStruct((3 * group, LANES), I32),
+            jax.ShapeDtypeStruct((owned + 1, size2 // LANES, LANES), BF16),
         ),
-        in_specs=[smem()] * 8 + [vmem()],
-        out_specs=(smem(), smem(), vmem()),
-        scratch_shapes=[pltpu.SMEM((parts,), I32), pltpu.VMEM((coarse_interp.size // LANES, LANES), F32)],
+        in_specs=[smem()] + [hbm()] * 9,
+        out_specs=(vmem(), vmem()),
+        scratch_shapes=[pltpu.VMEM((coarse_interp.size // LANES, LANES), F32), pltpu.VMEM((8, LANES), F32)]
+        + [pltpu.VMEM(x.shape, x.dtype) for x in inputs]
+        + [pltpu.SemaphoreType.DMA((len(inputs),))],
         compiler_params=params(),
-    )(
-        where,
-        fine_cols.T,
-        fine_slot.T,
-        fine_owner[:, 0],
-        fine_place,
-        coarse_slot.T,
-        coarse_owner[:, 0],
-        lax.optimization_barrier((coarse_place, own))[0],
-        coarse_interp,
-    )
-
-    size2 = coarse_interp.shape[1]
-    extra = pl.cdiv(target.shape[0], size2)
-    codes = jnp.pad(target, (0, extra * size2 - target.shape[0])).astype(BF16)
-    stacked = jnp.concatenate([quarters, codes.reshape((extra,) + quarters.shape[1:])], axis=0)
+    )(where, *[pltpu.with_memory_space_constraint(x, pltpu.HBM) for x in inputs], own)
+
     table = lax.all_gather(stacked, "dom", axis=0, tiled=True)
-    pitch = owned + extra
-    targets = table.reshape((parts, pitch) + quarters.shape[1:])[:, owned:].reshape(parts, extra * size2)
-    targets = targets[:, : target.shape[0]].astype(I32)
+    pitch = owned + 1
+    targets = table.reshape((parts, pitch, 2 * group, LANES))[:, owned].reshape(parts * 2 * group, LANES).astype(I32)
 
     tables = neighbours(table, "region")
     arrived = [None] * parts
@@ -555,23 +597,37 @@
         if n == 2:
             waited = waited + tables
         if n >= 3:
-            waited = waited + (arrived[chunks[n - 3][0]],)
-        sent = level_one(plan, fine_blocks, halo[0], own, halo[1], offsets, capacity, slots, waited)
+            waited = waited + tuple(arrived[d] for d in chunks[n - 3])
+        sent = level_one(info, fine_blocks, halo[0], own, halo[1], offsets, capacity, waited)
         for offset, cells in zip(offsets, sent):
             arrived[offset] = exchange(cells, "dom", offset) if offset else cells
     span2 = parts * owned
     inside = coarse_cols % span2
     step2 = table_of(coarse_cols // span2 - region + 1, region)
     index2 = (inside // owned * pitch + inside % owned) * 4 + step2
-    picked, turned = pick_rows(index2.T, tables[0], table, tables[1], quarters, sent[0])
+    picked, turned = pick_rows(index2.T, tables[0], table, tables[1], stacked, sent[0])
+    soon = [0] + [d for offsets in chunks[: len(chunks) // 2] for d in offsets]
+    late = [d for d in range(parts) if d not in soon]
+    early = early_sums(where, targets, picked, [arrived[d] for d in soon], soon, capacity, owned, stencil)
     outs = owner_level(
-        where, targets, plan, picked, turned, arrived, parts, capacity, capacity2, owned, stencil
+        where,
+        targets,
+        picked,
+        turned,
+        early,
+        [arrived[d] for d in late],
+        late,
+        parts,
+        capacity,
+        capacity2,
+        owned,
+        stencil,
     )
     coarse_blocks = outs[0].reshape(stencil, owned, narrow * narrow).transpose(1, 0, 2)
-    arrived2 = list(outs[1:])
+    arrived2 = list(outs[2:])
     for d in range(parts - 1, 0, -1):
         arrived2[d] = exchange(arrived2[d], "dom", d)
-    second = final_level(where, targets, arrived2, parts, slots, capacity2, owned2, stencil)
+    second = final_level(where, targets, arrived2, parts, capacity2, owned2, stencil)
     return (coarse_blocks, second)
 
 

time: 87.3 us -> 84 us (0.962)
  Pallas kernels: 43.6 us -> 41.2 us
  local copies, waits for them, and re-layouts: 3.18 us -> 1.68 us
    pallas_call x1, Pallas kernels: 6.66 us -> 2.83 us  [pick_rows(): pl.pallas_call(pick_kernel, out_shape=(jax.ShapeDtypeStruct((count * sten...]
    pallas_call x1, Pallas kernels: 5.12 us -> 1.96 us  [local(): pl.pallas_call(functools.partial(index_kernel, parts=parts, capacity=capa...]
    pallas_call x2 -> x3, Pallas kernels: 8.39 us -> 11 us  [the longest x1 4.94 us: owner_level(): pl.pallas_call(functools.partial(owner_kernel, parts=parts, offsets=offse...]
    pallas_call x4, Pallas kernels: 20.9 us -> 22.8 us  [level_one(): pl.pallas_call(functools.partial(terms_kernel, offsets=offsets, capacity=...]
    unnamed x27 -> x8, local copies, waits for them, and re-layouts: 1.51 us -> 0.02 us
    ppermute x4, waiting for transfers between devices: 2.41 us -> 3.47 us  [neighbours(): lax.ppermute(cells, axis, [(i, partner(i, odd, count)) for i in range(cou...]
    ppermute x14, waiting for transfers between devices: 3.52 us -> 2.61 us  [exchange(): return lax.ppermute(cells, axis, [(i, i ^ offset) for i in range(count)])]
    ppermute x14, starting transfers between devices: 12.9 us -> 13.8 us  [exchange(): return lax.ppermute(cells, axis, [(i, i ^ offset) for i in range(count)])]
  transfers between devices with their start and end apart: 18 -> 18, of which waited for: 4 -> 5; matrix products, arithmetic and copies ran while one was open for 2% -> 2% of each run, Pallas kernels for 38% -> 37%
where the time goes in v4:
time: 84 us; the launch traced here: 83.4 us
  Pallas kernels  41.2 us (49%)
  starting transfers between devices  23 us (27%)
  blocking collectives  10.6 us (13%)
  waiting for transfers between devices  6.08 us (7%)
  local copies, waits for them, and re-layouts  1.68 us (2%)
    pallas_call x4, Pallas kernels, level_one(): pl.pallas_call(functools.partial(terms_kernel, offsets=offsets, capacity=...  22.8 us
    ppermute x14, starting transfers between devices, exchange(): return lax.ppermute(cells, axis, [(i, i ^ offset) for i in range(count)])  13.8 us
    all_gather x1, blocking collectives, local(): table = lax.all_gather(stacked, 'dom', axis=0, tiled=True)  10.6 us
    ppermute x4, starting transfers between devices, neighbours(): lax.ppermute(cells, axis, [(i, partner(i, odd, count)) for i in range(cou...  9.19 us
    pallas_call x1, Pallas kernels, owner_level(): pl.pallas_call(functools.partial(owner_kernel, parts=parts, offsets=offse...  4.94 us
    ppermute x4, waiting for transfers between devices, neighbours(): lax.ppermute(cells, axis, [(i, partner(i, odd, count)) for i in range(cou...  3.47 us
    pallas_call x1, Pallas kernels, final_level(): pl.pallas_call(functools.partial(final_kernel, parts=parts, capacity2=cap...  3.23 us
    pallas_call x1, Pallas kernels, early_sums(): pl.pallas_call(functools.partial(early_kernel, offsets=offsets, capacity=...  2.86 us
  transfers between devices with their start and end apart: 18, of which 5 were waited for; matrix products, arithmetic and copies ran while one was open for 2% of the time, Pallas kernels for 37%

profile of v4, /device:TPU:0, one launch (start us, length us, event | category | flops | bytes accessed | tf_op | source)
XLA Modules:
  0.0 83.4 jit_solution(7651276920403300683)
XLA Ops:
  0.6 2.6 %shard_map.122.rest_8_.own_ref = bf16[48,64,128]{2,1,0:T(8,128)(2,1)S(1)} custom-call(bf16[48,8192]{1,0:T(8,128)(2,1)} %flat_ref.1), custom_call_target="tpu_custom_call" | custom-call | tf_op jit(solution)/shard_map/pallas_call | solution.py:86
  3.2 0.7 collective-permute-start.3
  3.9 5.9 %collective-permute-start.2 = (bf16[48,64,128]{2,1,0:T(8,128)(2,1)S(1)}, bf16[48,64,128]{2,1,0:T(8,128)(2,1)S(1)}, u32[]{:S(2)}, u32[]{:S(2)}) collective-permute-start(bf16[48,64,128]{2,1,0:T(8,128)(2,1)S(1)} %shard_map.122.rest_8_.own_ref), channel_id=1, source_target_pairs={{0,8},{8,0},{16,24},{24,16},{1,9},{9,1},{17,25},{25,17},{2,10},{10... | collective-permute-start | bytes 2359304 | tf_op jit(solution)/shard_map/ppermute | solution.py:49
  9.8 0.1 pad_add_fusion.where_ref
  9.9 2.0 %shard_map.123 = (s32[24,128]{1,0:T(8,128)S(1)}, bf16[25,16,128]{2,1,0:T(8,128)(2,1)S(1)}) custom-call(s32[2]{0:T(128)S(1)} %pad_add_fusion.where_ref, s32[7,48]{1,0:T(8,128)} %bitcast.20, s32[7,48]{1,0:T(8,128)} %bitcast.21, s32[1,48]{1,0:T(1,128)} %bitcast.23, s32[1,48]{1,0:T(1,128)} %bitcast.24, s32[7,24]{1,0:T(8,128)} %bitcast.22, s32[1,24]{1,0:T(1,128)} %bitcast.25, ...), custom_call_target="tpu_custom_call" | custom-call | tf_op jit(solution)/shard_map/pallas_call | solution.py:571
  11.8 0.0 copy-start
  11.9 10.6 %all_gather.3.own_ref = bf16[200,16,128]{2,1,0:T(8,128)(2,1)S(1)} all-gather(bf16[25,16,128]{2,1,0:T(8,128)(2,1)S(1)} %get-tuple-element.23.mine_ref), channel_id=1, replica_groups=mesh['region'=4,'dom'=8] {'dom'}, dimensions={0}, use_global_device_ids=true | all-gather | bytes 921600 | tf_op jit(solution)/shard_map/all_gather | solution.py:587
  22.4 1.6 %collective-permute-start.1 = (bf16[200,16,128]{2,1,0:T(8,128)(2,1)S(1)}, bf16[200,16,128]{2,1,0:T(8,128)(2,1)}, u32[]{:S(2)}, u32[]{:S(2)}) collective-permute-start(bf16[200,16,128]{2,1,0:T(8,128)(2,1)S(1)} %all_gather.3.own_ref), channel_id=1, source_target_pairs={{0,0},{8,16},{16,8},{24,24},{1,1},{9,17},{17,9},{25,25},{2,2},{10,... | collective-permute-start | bytes 2457608 | tf_op jit(solution)/shard_map/ppermute | solution.py:49
  24.0 1.0 %collective-permute-start = (bf16[200,16,128]{2,1,0:T(8,128)(2,1)S(1)}, bf16[200,16,128]{2,1,0:T(8,128)(2,1)}, u32[]{:S(2)}, u32[]{:S(2)}) collective-permute-start(bf16[200,16,128]{2,1,0:T(8,128)(2,1)S(1)} %all_gather.3.own_ref), channel_id=1, source_target_pairs={{0,8},{8,0},{16,24},{24,16},{1,9},{9,1},{17,25},{25,17},{2,10},{10... | collective-permute-start | bytes 2457608 | tf_op jit(solution)/shard_map/ppermute | solution.py:49
  25.0 0.0 collective-permute-done.3.after_ref
  25.0 2.3 %collective-permute-done.2.before_ref = bf16[48,64,128]{2,1,0:T(8,128)(2,1)S(1)} collective-permute-done((bf16[48,64,128]{2,1,0:T(8,128)(2,1)S(1)}, bf16[48,64,128]{2,1,0:T(8,128)(2,1)S(1)}, u32[]{:S(2)}, u32[]{:S(2)}) %collective-permute-start.2) | collective-permute-done | bytes 786464 | tf_op jit(solution)/shard_map/ppermute | solution.py:49
  27.3 6.2 %shard_map.124 = (bf16[1344,128]{1,0:T(8,128)(2,1)}, bf16[1344,128]{1,0:T(8,128)(2,1)}) custom-call(s32[24,128]{1,0:T(8,128)} %copy-done.2, bf16[48,7,128,128]{3,2,1,0:T(8,128)(2,1)} %blocks_ref.7, bf16[48,64,128]{2,1,0:T(8,128)(2,1)S(1)} %collective-permute-done.2.before_ref, bf16[48,64,128]{2,1,0:T(8,128)(2,1)S(1)} %shard_map.122.rest_8_.own_ref, ...), custom_call_target="tpu_custom_call" | custom-call | tf_op jit(solution)/shard_map/pallas_call | solution.py:273
  33.6 3.3 %collective-permute-start.5 = (bf16[1344,128]{1,0:T(8,128)(2,1)}, bf16[1344,128]{1,0:T(8,128)(2,1)S(1)}, u32[]{:S(2)}, u32[]{:S(2)}) collective-permute-start(bf16[1344,128]{1,0:T(8,128)(2,1)} %get-tuple-element.28), channel_id=1, source_target_pairs={{0,6},{1,7},{2,4},{3,5},{4,2},{5,3},{6,0},{7,1},{8,14},{9,15},{10,... | collective-permute-start | bytes 1032200 | tf_op jit(solution)/shard_map/ppermute | solution.py:39
  36.9 0.0 collective-permute-start.4
  36.9 5.5 %shard_map.125 = (bf16[1344,128]{1,0:T(8,128)(2,1)S(1)}, bf16[1344,128]{1,0:T(8,128)(2,1)S(1)}) custom-call(s32[24,128]{1,0:T(8,128)} %copy-done.2, bf16[48,7,128,128]{3,2,1,0:T(8,128)(2,1)} %blocks_ref.7, bf16[48,64,128]{2,1,0:T(8,128)(2,1)S(1)} %collective-permute-done.2.before_ref, bf16[48,64,128]{2,1,0:T(8,128)(2,1)S(1)} %shard_map.122.rest_8_.own_ref, ...), custom_call_target="tpu_custom_call" | custom-call | tf_op jit(solution)/shard_map/pallas_call | solution.py:273
  42.4 1.0 %collective-permute-start.7 = (bf16[1344,128]{1,0:T(8,128)(2,1)S(1)}, bf16[1344,128]{1,0:T(8,128)(2,1)S(1)}, u32[]{:S(2)}, u32[]{:S(2)}) collective-permute-start(bf16[1344,128]{1,0:T(8,128)(2,1)S(1)} %get-tuple-element.33), channel_id=1, source_target_pairs={{0,3},{1,2},{2,1},{3,0},{4,7},{5,6},{6,5},{7,4},{8,11},{9,10},{10,... | collective-permute-start | bytes 1032200 | tf_op jit(solution)/shard_map/ppermute | solution.py:39
  43.4 0.0 collective-permute-done.1.rest_2_.second_ref
  43.4 0.1 collective-permute-start.6
  43.5 1.2 %collective-permute-done.rest_1_.first_ref = bf16[200,16,128]{2,1,0:T(8,128)(2,1)} collective-permute-done((bf16[200,16,128]{2,1,0:T(8,128)(2,1)S(1)}, bf16[200,16,128]{2,1,0:T(8,128)(2,1)}, u32[]{:S(2)}, u32[]{:S(2)}) %collective-permute-start) | collective-permute-done | bytes 819232 | tf_op jit(solution)/shard_map/ppermute | solution.py:49
  44.7 5.5 %shard_map.126 = (bf16[1344,128]{1,0:T(8,128)(2,1)S(1)}, bf16[1344,128]{1,0:T(8,128)(2,1)S(1)}) custom-call(s32[24,128]{1,0:T(8,128)} %copy-done.2, bf16[48,7,128,128]{3,2,1,0:T(8,128)(2,1)} %blocks_ref.7, bf16[48,64,128]{2,1,0:T(8,128)(2,1)S(1)} %collective-permute-done.2.before_ref, bf16[48,64,128]{2,1,0:T(8,128)(2,1)S(1)} %shard_map.122.rest_8_.own_ref, ...), custom_call_target="tpu_custom_call" | custom-call | tf_op jit(solution)/shard_map/pallas_call | solution.py:273
  50.2 1.6 %collective-permute-start.9 = (bf16[1344,128]{1,0:T(8,128)(2,1)S(1)}, bf16[1344,128]{1,0:T(8,128)(2,1)S(1)}, u32[]{:S(2)}, u32[]{:S(2)}) collective-permute-start(bf16[1344,128]{1,0:T(8,128)(2,1)S(1)} %get-tuple-element.34), channel_id=1, source_target_pairs={{0,2},{1,3},{2,0},{3,1},{4,6},{5,7},{6,4},{7,5},{8,10},{9,11},{10,... | collective-permute-start | bytes 1032200 | tf_op jit(solution)/shard_map/ppermute | solution.py:39
  51.8 0.0 collective-permute-done.5.rest_2_
  51.8 1.5 %collective-permute-start.10 = (bf16[1344,128]{1,0:T(8,128)(2,1)S(1)}, bf16[1344,128]{1,0:T(8,128)(2,1)S(1)}, u32[]{:S(2)}, u32[]{:S(2)}) collective-permute-start(bf16[1344,128]{1,0:T(8,128)(2,1)S(1)} %get-tuple-element.27.rest_0_), channel_id=1, source_target_pairs={{0,4},{1,5},{2,6},{3,7},{4,0},{5,1},{6,2},{7,3},{8,12},{9,13},{10,... | collective-permute-start | bytes 1032200 | tf_op jit(solution)/shard_map/ppermute | solution.py:39
  53.3 0.0 collective-permute-done.4.rest_1_
  53.3 5.5 %shard_map.127 = (bf16[1344,128]{1,0:T(8,128)(2,1)S(1)}, bf16[1344,128]{1,0:T(8,128)(2,1)S(1)}) custom-call(s32[24,128]{1,0:T(8,128)} %copy-done.2, bf16[48,7,128,128]{3,2,1,0:T(8,128)(2,1)} %blocks_ref.7, bf16[48,64,128]{2,1,0:T(8,128)(2,1)S(1)} %collective-permute-done.2.before_ref, bf16[48,64,128]{2,1,0:T(8,128)(2,1)S(1)} %shard_map.122.rest_8_.own_ref, ...), custom_call_target="tpu_custom_call" | custom-call | tf_op jit(solution)/shard_map/pallas_call | solution.py:273
  58.9 0.1 collective-permute-start.8
  59.0 2.8 %shard_map.128 = (bf16[168,16,128]{2,1,0:T(8,128)(2,1)S(1)}, bf16[24,32,64]{2,1,0:T(8,128)(2,1)S(1)}) custom-call(s32[7,24]{1,0:T(8,128)S(1)} %fusion.4.index_ref, bf16[200,16,128]{2,1,0:T(8,128)(2,1)} %collective-permute-done.rest_1_.first_ref, bf16[200,16,128]{2,1,0:T(8,128)(2,1)S(1)} %all_gather.3.own_ref, ...), custom_call_target="tpu_custom_call" | custom-call | tf_op jit(solution)/shard_map/pallas_call | solution.py:341
  61.8 0.0 collective-permute-done.7.rest_4_
  61.8 0.0 collective-permute-done.6.rest_3_
  61.9 2.9 %shard_map.129.early_ref = f32[169,32,128]{2,1,0:T(8,128)S(1)} custom-call(s32[2]{0:T(128)S(1)} %pad_add_fusion.where_ref, s32[128,128]{1,0:T(8,128)S(1)} %bitcast_convert_fusion.target_ref, bf16[1344,128]{1,0:T(8,128)(2,1)S(1)} %get-tuple-element.32.rest_0_, bf16[1344,128]{1,0:T(8,128)(2,1)} %collective-permute-done.4.rest_1_, ...), custom_call_target="tpu_custom_call" | custom-call | tf_op jit(solution)/shard_map/pallas_call | solution.py:371
  64.7 0.9 %collective-permute-done.9.rest_1_ = bf16[1344,128]{1,0:T(8,128)(2,1)S(1)} collective-permute-done((bf16[1344,128]{1,0:T(8,128)(2,1)S(1)}, bf16[1344,128]{1,0:T(8,128)(2,1)S(1)}, u32[]{:S(2)}, u32[]{:S(2)}) %collective-permute-start.9) | collective-permute-done | bytes 344096 | tf_op jit(solution)/shard_map/ppermute | solution.py:39
  65.6 0.0 collective-permute-done.10.rest_2_
  65.6 0.0 collective-permute-done.8.rest_0_
  65.6 4.9 %shard_map.130 = (bf16[168,32,128]{2,1,0:T(8,128)(2,1)S(1)}, f32[169,32,128]{2,1,0:T(8,128)S(1)}, bf16[168,128]{1,0:T(8,128)(2,1)S(1)}, bf16[168,128]{1,0:T(8,12...) custom-call(s32[2]{0:T(128)S(1)} %pad_add_fusion.where_ref, ...), custom_call_target="tpu_custom_call", output_to_operand_aliasing={{1}: (4, {})} | custom-call | tf_op jit(solution)/shard_map/pallas_call | solution.py:469
  70.6 2.0 %collective-permute-start.11 = (bf16[168,128]{1,0:T(8,128)(2,1)S(1)}, bf16[168,128]{1,0:T(8,128)(2,1)S(1)}, u32[]{:S(2)}, u32[]{:S(2)}) collective-permute-start(bf16[168,128]{1,0:T(8,128)(2,1)S(1)} %get-tuple-element.36), channel_id=1, source_target_pairs={{0,7},{1,6},{2,5},{3,4},{4,3},{5,2},{6,1},{7,0},{8,15},{9,14},{10,... | collective-permute-start | bytes 129032 | tf_op jit(solution)/shard_map/ppermute | solution.py:39
  72.6 0.5 collective-permute-start.12
  73.1 1.3 %collective-permute-start.13 = (bf16[168,128]{1,0:T(8,128)(2,1)S(1)}, bf16[168,128]{1,0:T(8,128)(2,1)S(1)}, u32[]{:S(2)}, u32[]{:S(2)}) collective-permute-start(bf16[168,128]{1,0:T(8,128)(2,1)S(1)} %get-tuple-element.38), channel_id=1, source_target_pairs={{0,5},{1,4},{2,7},{3,6},{4,1},{5,0},{6,3},{7,2},{8,13},{9,12},{10,... | collective-permute-start | bytes 129032 | tf_op jit(solution)/shard_map/ppermute | solution.py:39
  74.4 0.7 collective-permute-start.14
  75.0 1.1 %collective-permute-start.15 = (bf16[168,128]{1,0:T(8,128)(2,1)S(1)}, bf16[168,128]{1,0:T(8,128)(2,1)S(1)}, u32[]{:S(2)}, u32[]{:S(2)}) collective-permute-start(bf16[168,128]{1,0:T(8,128)(2,1)S(1)} %get-tuple-element.40), channel_id=1, source_target_pairs={{0,3},{1,2},{2,1},{3,0},{4,7},{5,6},{6,5},{7,4},{8,11},{9,10},{10,... | collective-permute-start | bytes 129032 | tf_op jit(solution)/shard_map/ppermute | solution.py:39
  76.1 0.0 collective-permute-done.11.rest_0_
  76.1 0.7 collective-permute-start.16
  76.8 0.8 collective-permute-done.12.rest_1_
  77.6 1.7 %reshape.21 = bf16[7,24,4096]{2,1,0:T(8,128)(2,1)} reshape(bf16[168,32,128]{2,1,0:T(8,128)(2,1)S(1)} %get-tuple-element.35) | data formatting | bytes 2752512 | tf_op jit(solution)/shard_map/reshape | solution.py:626
  79.3 0.0 collective-permute-done.13.rest_2_
  79.3 0.0 collective-permute-done.14.rest_3_
  79.3 0.0 collective-permute-done.15.rest_4_
  79.3 0.9 %collective-permute-done.16.rest_5_ = bf16[168,128]{1,0:T(8,128)(2,1)S(1)} collective-permute-done((bf16[168,128]{1,0:T(8,128)(2,1)S(1)}, bf16[168,128]{1,0:T(8,128)(2,1)S(1)}, u32[]{:S(2)}, u32[]{:S(2)}) %collective-permute-start.16) | collective-permute-done | bytes 43040 | tf_op jit(solution)/shard_map/ppermute | solution.py:39
  80.2 3.2 %shard_map.131 = bf16[12,7,1024]{2,1,0:T(8,128)(2,1)} custom-call(s32[2]{0:T(128)S(1)} %pad_add_fusion.where_ref, s32[128,128]{1,0:T(8,128)S(1)} %bitcast_convert_fusion.target_ref, bf16[168,128]{1,0:T(8,128)(2,1)S(1)} %collective-permute-done.11.rest_0_, bf16[168,128]{1,0:T(8,128)(2,1)S(1)} %collective-permute-done.12.rest_1_, ...), custom_call_target="tpu_custom_call" | custom-call | tf_op jit(solution)/shard_map/pallas_call | solution.py:517
  (12 shorter events, 0.1 us)
Async XLA Ops:
  3.2 21.8 %collective-permute-start.3 = (bf16[48,64,128]{2,1,0:T(8,128)(2,1)S(1)}, bf16[48,64,128]{2,1,0:T(8,128)(2,1)S(1)}, u32[]{:S(2)}, u32[]{:S(2)}) collective-permute-start(bf16[48,64,128]{2,1,0:T(8,128)(2,1)S(1)} %shard_map.122.rest_8_.own_ref), channel_id=1, source_target_pairs={{0,0},{8,16},{16,8},{24,24},{1,1},{9,17},{17,9},{25,25},{2,2},{10,... | collective-permute-start | bytes 2359304 | tf_op jit(solution)/shard_map/ppermute | solution.py:49
  3.9 23.4 %collective-permute-start.2 = (bf16[48,64,128]{2,1,0:T(8,128)(2,1)S(1)}, bf16[48,64,128]{2,1,0:T(8,128)(2,1)S(1)}, u32[]{:S(2)}, u32[]{:S(2)}) collective-permute-start(bf16[48,64,128]{2,1,0:T(8,128)(2,1)S(1)} %shard_map.122.rest_8_.own_ref), channel_id=1, source_target_pairs={{0,8},{8,0},{16,24},{24,16},{1,9},{9,1},{17,25},{25,17},{2,10},{10... | collective-permute-start | bytes 2359304 | tf_op jit(solution)/shard_map/ppermute | solution.py:49
  11.8 15.5 %copy-start.2 = (s32[24,128]{1,0:T(8,128)}, s32[24,128]{1,0:T(8,128)S(1)}, u32[]{:S(2)}) copy-start(s32[24,128]{1,0:T(8,128)S(1)} %get-tuple-element.24.table_ref) | copy-start | bytes 36868
  11.8 21.8 %copy-start = (bf16[25,16,128]{2,1,0:T(8,128)(2,1)}, bf16[25,16,128]{2,1,0:T(8,128)(2,1)S(1)}, u32[]{:S(2)}) copy-start(bf16[25,16,128]{2,1,0:T(8,128)(2,1)S(1)} %get-tuple-element.23.mine_ref) | copy-start | bytes 307204
  22.4 21.0 %collective-permute-start.1 = (bf16[200,16,128]{2,1,0:T(8,128)(2,1)S(1)}, bf16[200,16,128]{2,1,0:T(8,128)(2,1)}, u32[]{:S(2)}, u32[]{:S(2)}) collective-permute-start(bf16[200,16,128]{2,1,0:T(8,128)(2,1)S(1)} %all_gather.3.own_ref), channel_id=1, source_target_pairs={{0,0},{8,16},{16,8},{24,24},{1,1},{9,17},{17,9},{25,25},{2,2},{10,... | collective-permute-start | bytes 2457608 | tf_op jit(solution)/shard_map/ppermute | solution.py:49
  24.0 20.7 %collective-permute-start = (bf16[200,16,128]{2,1,0:T(8,128)(2,1)S(1)}, bf16[200,16,128]{2,1,0:T(8,128)(2,1)}, u32[]{:S(2)}, u32[]{:S(2)}) collective-permute-start(bf16[200,16,128]{2,1,0:T(8,128)(2,1)S(1)} %all_gather.3.own_ref), channel_id=1, source_target_pairs={{0,8},{8,0},{16,24},{24,16},{1,9},{9,1},{17,25},{25,17},{2,10},{10... | collective-permute-start | bytes 2457608 | tf_op jit(solution)/shard_map/ppermute | solution.py:49
  33.6 18.2 %collective-permute-start.5 = (bf16[1344,128]{1,0:T(8,128)(2,1)}, bf16[1344,128]{1,0:T(8,128)(2,1)S(1)}, u32[]{:S(2)}, u32[]{:S(2)}) collective-permute-start(bf16[1344,128]{1,0:T(8,128)(2,1)} %get-tuple-element.28), channel_id=1, source_target_pairs={{0,6},{1,7},{2,4},{3,5},{4,2},{5,3},{6,0},{7,1},{8,14},{9,15},{10,... | collective-permute-start | bytes 1032200 | tf_op jit(solution)/shard_map/ppermute | solution.py:39
  36.9 16.5 %collective-permute-start.4 = (bf16[1344,128]{1,0:T(8,128)(2,1)}, bf16[1344,128]{1,0:T(8,128)(2,1)}, u32[]{:S(2)}, u32[]{:S(2)}) collective-permute-start(bf16[1344,128]{1,0:T(8,128)(2,1)} %get-tuple-element.25.rest_0_), channel_id=1, source_target_pairs={{0,7},{1,6},{2,5},{3,4},{4,3},{5,2},{6,1},{7,0},{8,15},{9,14},{10,... | collective-permute-start | bytes 1032200 | tf_op jit(solution)/shard_map/ppermute | solution.py:39
  42.4 19.4 %collective-permute-start.7 = (bf16[1344,128]{1,0:T(8,128)(2,1)S(1)}, bf16[1344,128]{1,0:T(8,128)(2,1)S(1)}, u32[]{:S(2)}, u32[]{:S(2)}) collective-permute-start(bf16[1344,128]{1,0:T(8,128)(2,1)S(1)} %get-tuple-element.33), channel_id=1, source_target_pairs={{0,3},{1,2},{2,1},{3,0},{4,7},{5,6},{6,5},{7,4},{8,11},{9,10},{10,... | collective-permute-start | bytes 1032200 | tf_op jit(solution)/shard_map/ppermute | solution.py:39
  43.4 18.5 %collective-permute-start.6 = (bf16[1344,128]{1,0:T(8,128)(2,1)S(1)}, bf16[1344,128]{1,0:T(8,128)(2,1)S(1)}, u32[]{:S(2)}, u32[]{:S(2)}) collective-permute-start(bf16[1344,128]{1,0:T(8,128)(2,1)S(1)} %get-tuple-element.26.rest_0_), channel_id=1, source_target_pairs={{0,5},{1,4},{2,7},{3,6},{4,1},{5,0},{6,3},{7,2},{8,13},{9,12},{10,... | collective-permute-start | bytes 1032200 | tf_op jit(solution)/shard_map/ppermute | solution.py:39
  50.2 15.4 %collective-permute-start.9 = (bf16[1344,128]{1,0:T(8,128)(2,1)S(1)}, bf16[1344,128]{1,0:T(8,128)(2,1)S(1)}, u32[]{:S(2)}, u32[]{:S(2)}) collective-permute-start(bf16[1344,128]{1,0:T(8,128)(2,1)S(1)} %get-tuple-element.34), channel_id=1, source_target_pairs={{0,2},{1,3},{2,0},{3,1},{4,6},{5,7},{6,4},{7,5},{8,10},{9,11},{10,... | collective-permute-start | bytes 1032200 | tf_op jit(solution)/shard_map/ppermute | solution.py:39
  51.8 7.1 %copy-start.3 = (s32[24,7]{0,1:T(8,128)S(1)}, s32[24,7]{0,1:T(8,128)}, u32[]{:S(2)}) copy-start(s32[24,7]{0,1:T(8,128)} %param.18) | copy-start | bytes 2020
  51.8 7.2 %copy-start.1 = (bf16[25,16,128]{2,1,0:T(8,128)(2,1)S(1)}, bf16[25,16,128]{2,1,0:T(8,128)(2,1)}, u32[]{:S(2)}) copy-start(bf16[25,16,128]{2,1,0:T(8,128)(2,1)} %copy-done) | copy-start | bytes 307204
  51.8 13.8 %collective-permute-start.10 = (bf16[1344,128]{1,0:T(8,128)(2,1)S(1)}, bf16[1344,128]{1,0:T(8,128)(2,1)S(1)}, u32[]{:S(2)}, u32[]{:S(2)}) collective-permute-start(bf16[1344,128]{1,0:T(8,128)(2,1)S(1)} %get-tuple-element.27.rest_0_), channel_id=1, source_target_pairs={{0,4},{1,5},{2,6},{3,7},{4,0},{5,1},{6,2},{7,3},{8,12},{9,13},{10,... | collective-permute-start | bytes 1032200 | tf_op jit(solution)/shard_map/ppermute | solution.py:39
  58.9 6.8 %collective-permute-start.8 = (bf16[1344,128]{1,0:T(8,128)(2,1)S(1)}, bf16[1344,128]{1,0:T(8,128)(2,1)S(1)}, u32[]{:S(2)}, u32[]{:S(2)}) collective-permute-start(bf16[1344,128]{1,0:T(8,128)(2,1)S(1)} %get-tuple-element.29.waited_ref), channel_id=1, source_target_pairs={{0,1},{1,0},{2,3},{3,2},{4,5},{5,4},{6,7},{7,6},{8,9},{9,8},{10,11... | collective-permute-start | bytes 1032200 | tf_op jit(solution)/shard_map/ppermute | solution.py:39
  70.6 5.5 %collective-permute-start.11 = (bf16[168,128]{1,0:T(8,128)(2,1)S(1)}, bf16[168,128]{1,0:T(8,128)(2,1)S(1)}, u32[]{:S(2)}, u32[]{:S(2)}) collective-permute-start(bf16[168,128]{1,0:T(8,128)(2,1)S(1)} %get-tuple-element.36), channel_id=1, source_target_pairs={{0,7},{1,6},{2,5},{3,4},{4,3},{5,2},{6,1},{7,0},{8,15},{9,14},{10,... | collective-permute-start | bytes 129032 | tf_op jit(solution)/shard_map/ppermute | solution.py:39
  72.6 5.0 %collective-permute-start.12 = (bf16[168,128]{1,0:T(8,128)(2,1)S(1)}, bf16[168,128]{1,0:T(8,128)(2,1)S(1)}, u32[]{:S(2)}, u32[]{:S(2)}) collective-permute-start(bf16[168,128]{1,0:T(8,128)(2,1)S(1)} %get-tuple-element.37), channel_id=1, source_target_pairs={{0,6},{1,7},{2,4},{3,5},{4,2},{5,3},{6,0},{7,1},{8,14},{9,15},{10,... | collective-permute-start | bytes 129032 | tf_op jit(solution)/shard_map/ppermute | solution.py:39
  73.1 6.2 %collective-permute-start.13 = (bf16[168,128]{1,0:T(8,128)(2,1)S(1)}, bf16[168,128]{1,0:T(8,128)(2,1)S(1)}, u32[]{:S(2)}, u32[]{:S(2)}) collective-permute-start(bf16[168,128]{1,0:T(8,128)(2,1)S(1)} %get-tuple-element.38), channel_id=1, source_target_pairs={{0,5},{1,4},{2,7},{3,6},{4,1},{5,0},{6,3},{7,2},{8,13},{9,12},{10,... | collective-permute-start | bytes 129032 | tf_op jit(solution)/shard_map/ppermute | solution.py:39
  74.4 4.9 %collective-permute-start.14 = (bf16[168,128]{1,0:T(8,128)(2,1)S(1)}, bf16[168,128]{1,0:T(8,128)(2,1)S(1)}, u32[]{:S(2)}, u32[]{:S(2)}) collective-permute-start(bf16[168,128]{1,0:T(8,128)(2,1)S(1)} %get-tuple-element.39), channel_id=1, source_target_pairs={{0,4},{1,5},{2,6},{3,7},{4,0},{5,1},{6,2},{7,3},{8,12},{9,13},{10,... | collective-permute-start | bytes 129032 | tf_op jit(solution)/shard_map/ppermute | solution.py:39
  75.0 4.2 %collective-permute-start.15 = (bf16[168,128]{1,0:T(8,128)(2,1)S(1)}, bf16[168,128]{1,0:T(8,128)(2,1)S(1)}, u32[]{:S(2)}, u32[]{:S(2)}) collective-permute-start(bf16[168,128]{1,0:T(8,128)(2,1)S(1)} %get-tuple-element.40), channel_id=1, source_target_pairs={{0,3},{1,2},{2,1},{3,0},{4,7},{5,6},{6,5},{7,4},{8,11},{9,10},{10,... | collective-permute-start | bytes 129032 | tf_op jit(solution)/shard_map/ppermute | solution.py:39
  76.1 4.1 %collective-permute-start.16 = (bf16[168,128]{1,0:T(8,128)(2,1)S(1)}, bf16[168,128]{1,0:T(8,128)(2,1)S(1)}, u32[]{:S(2)}, u32[]{:S(2)}) collective-permute-start(bf16[168,128]{1,0:T(8,128)(2,1)S(1)} %get-tuple-element.41), channel_id=1, source_target_pairs={{0,2},{1,3},{2,0},{3,1},{4,6},{5,7},{6,4},{7,5},{8,10},{9,11},{10,... | collective-permute-start | bytes 129032 | tf_op jit(solution)/shard_map/ppermute | solution.py:39
  77.6 2.5 %collective-permute-start.17 = (bf16[168,128]{1,0:T(8,128)(2,1)S(1)}, bf16[168,128]{1,0:T(8,128)(2,1)S(1)}, u32[]{:S(2)}, u32[]{:S(2)}) collective-permute-start(bf16[168,128]{1,0:T(8,128)(2,1)S(1)} %get-tuple-element.42), channel_id=1, source_target_pairs={{0,1},{1,0},{2,3},{3,2},{4,5},{5,4},{6,7},{7,6},{8,9},{9,8},{10,11... | collective-permute-start | bytes 129032 | tf_op jit(solution)/shard_map/ppermute | solution.py:39

commit v5 on v4

--- a/solution.py
+++ b/solution.py
@@ -46,11 +46,11 @@
 
 def neighbours(cells, axis):
     count = lax.axis_size(axis)
-    return tuple(lax.ppermute(cells, axis, [(i, partner(i, odd, count)) for i in range(count)]) for odd in (0, 1))
+    return tuple(lax.ppermute(cells, axis, [(i, partner(i, odd, count)) for i in range(count)]) for odd in (1, 0))
 
 
 def table_of(step, region):
-    swapped = jnp.where(region % 2 == 0, 2 - step, step)
+    swapped = jnp.where(region % 2 == 0, step, 2 - step)
     return jnp.where(step == 1, 1, swapped)
 
 
@@ -350,36 +350,66 @@
     )(index, first, own, second, mine, waited)
 
 
-def add_terms(dom, target_ref, arrived, offsets, sum_ref, capacity, stencil):
+def add_terms(part_ref, target_of, sum_ref, capacity, stencil):
     flat = sum_ref.shape[1]
-    for d, part_ref in zip(offsets, arrived):
-        base = (dom ^ d) * 2 * (stencil + 1)
+    for r in range(capacity):
+        for k in range(stencil):
+            term = part_ref[pl.ds((r * stencil + k) * flat, flat), :].astype(F32)
+            sum_ref[target_of(r, k)] += term
+
+
+def early_kernel(where_ref, table_ref, *rest, soon, late, parts, capacity, capacity2, owned, stencil):
+    sum_ref, lists_ref = rest[-2:]
+    dom = where_ref[1]
+    group = stencil + 1
+
+    def row_of(d, level, slot):
+        return table_ref[((dom ^ d) * 2 + level) * group + stencil, slot]
+
+    def target_at(d, level, row, k):
+        return table_ref[((dom ^ d) * 2 + level) * group + k, row]
+
+    at = 0
+    for d in range(parts):
+        for r in range(capacity2):
+            row = table_ref[(dom * 2 + 2) * group - 1, (dom ^ d) * capacity2 + r]
+            lists_ref[at] = jnp.minimum(row, owned - 1)
+            at += 1
+    for d in late:
         for r in range(capacity):
-            row = target_ref[base + stencil, dom * capacity + r]
+            row = row_of(d, 0, dom * capacity + r)
             for k in range(stencil):
-                target = target_ref[base + k, row]
-                sum_ref[target] += part_ref[pl.ds((r * stencil + k) * flat, flat), :].astype(F32)
-
-
-def early_kernel(where_ref, target_ref, *rest, offsets, capacity, stencil):
-    sum_ref = rest[-1]
+                lists_ref[at] = target_at(d, 0, row, k)
+                at += 1
+    for d in range(parts):
+        for r in range(capacity2):
+            row = row_of(d, 1, dom * capacity2 + r)
+            for k in range(stencil):
+                lists_ref[at] = target_at(d, 1, row, k)
+                at += 1
     sum_ref[...] = jnp.zeros(sum_ref.shape, F32)
-    add_terms(where_ref[1], target_ref, rest[: len(offsets)], offsets, sum_ref, capacity, stencil)
-
-
-def early_sums(where, targets, waited, arrived, offsets, capacity, owned, stencil):
+    for d, part_ref in zip(soon, rest):
+        rows = [row_of(d, 0, dom * capacity + r) for r in range(capacity)]
+        add_terms(part_ref, lambda r, k: target_at(d, 0, rows[r], k), sum_ref, capacity, stencil)
+
+
+def early_sums(where, table, waited, arrived, soon, late, parts, capacity, capacity2, owned, stencil):
+    sizes = dict(parts=parts, capacity=capacity, capacity2=capacity2, owned=owned, stencil=stencil)
+    count = parts * capacity2 * (stencil + 1) + len(late) * capacity * stencil
     return pl.pallas_call(
-        functools.partial(early_kernel, offsets=offsets, capacity=capacity, stencil=stencil),
-        out_shape=jax.ShapeDtypeStruct((stencil * owned + 1, LANES // 4, LANES), F32),
-        in_specs=[smem(), smem()] + [vmem()] * len(offsets) + [hbm()],
-        out_specs=vmem(),
+        functools.partial(early_kernel, soon=soon, late=late, **sizes),
+        out_shape=(
+            jax.ShapeDtypeStruct((stencil * owned + 1, LANES // 4, LANES), F32),
+            jax.ShapeDtypeStruct((count,), I32),
+        ),
+        in_specs=[smem(), smem()] + [vmem()] * len(soon) + [hbm()],
+        out_specs=(vmem(), smem()),
         compiler_params=params(),
-    )(where, targets, *arrived, waited)
+    )(where, table, *arrived, waited)
 
 
 def owner_kernel(
-    where_ref,
-    target_ref,
+    lists_ref,
     picked_ref,
     own_ref,
     early_ref,
@@ -396,12 +426,11 @@
     sum_ref = rest[len(offsets) + 1]
     sends = rest[len(offsets) + 2 : len(offsets) + 2 + parts]
     (term_ref,) = rest[len(offsets) + 2 + parts :]
-    dom = where_ref[1]
-    group = stencil + 1
-    mine = dom * 2 * group
     flat = sum_ref.shape[1]
     narrow = LANES // 2
-    add_terms(dom, target_ref, arrived, offsets, sum_ref, capacity, stencil)
+    for n, part_ref in enumerate(arrived):
+        first = parts * capacity2 + n * capacity * stencil
+        add_terms(part_ref, lambda r, k: lists_ref[first + r * stencil + k], sum_ref, capacity, stencil)
 
     left = low_lanes((flat, LANES), narrow)
     quarter = LANES // 4
@@ -413,9 +442,7 @@
 
     def second(step, carry):
         places = [(step * batch + n, r) for n in range(batch) for r in range(capacity2)]
-        names = [
-            jnp.minimum(target_ref[mine + 2 * group - 1, (dom ^ d) * capacity2 + r], owned - 1) for d, r in places
-        ]
+        names = [lists_ref[d * capacity2 + r] for d, r in places]
         products = []
         for q in names:
             rows = []
@@ -463,7 +490,7 @@
         sends[d][...] = term_ref[d].astype(BF16)
 
 
-def owner_level(where, targets, picked, own, early, arrived, offsets, parts, capacity, capacity2, owned, stencil):
+def owner_level(lists, picked, own, early, arrived, offsets, parts, capacity, capacity2, owned, stencil):
     flat = LANES // 4
     send = jax.ShapeDtypeStruct((capacity2 * stencil * 8, LANES), BF16)
     return pl.pallas_call(
@@ -481,47 +508,46 @@
             jax.ShapeDtypeStruct(early.shape, F32),
         )
         + (send,) * parts,
-        in_specs=[smem(), smem()] + [vmem()] * (3 + len(offsets)),
+        in_specs=[smem()] + [vmem()] * (3 + len(offsets)),
         out_specs=(vmem(),) * (2 + parts),
         scratch_shapes=[pltpu.VMEM((parts, capacity2 * stencil * 8, LANES), F32)],
-        input_output_aliases={4: 1},
+        input_output_aliases={3: 1},
         compiler_params=params(),
-    )(where, targets, picked, own, early, *arrived)
-
-
-def final_kernel(where_ref, target_ref, *rest, parts, capacity2, stencil):
+    )(lists, picked, own, early, *arrived)
+
+
+def final_kernel(lists_ref, *rest, parts, capacity2, stencil):
     arrived = rest[:parts][::-1]
     out_ref = rest[parts]
     sum_ref, other_ref = rest[parts + 1 :]
-    dom = where_ref[1]
     deep = stencil + 1
+    first = lists_ref.shape[0] - parts * capacity2 * stencil
     other_ref[...] = jnp.zeros(other_ref.shape, F32)
     sum_ref[...] = jnp.zeros(sum_ref.shape, F32)
     for d in range(0, parts, 2):
         pairs = [(sum_ref, d), (other_ref, d + 1)]
         values = [arrived[e][...].astype(F32) for _, e in pairs]
         for r in range(capacity2):
-            bases = [((dom ^ e) * 2 + 1) * deep for _, e in pairs]
-            rows = [target_ref[base + stencil, dom * capacity2 + r] for base in bases]
             for k in range(stencil):
                 at = r * stencil + k
-                for (into_ref, _), base, row, value in zip(pairs, bases, rows, values):
-                    into_ref[target_ref[base + k, row]] += value[at * 8 : (at + 1) * 8]
+                for (into_ref, e), value in zip(pairs, values):
+                    target = lists_ref[first + e * capacity2 * stencil + at]
+                    into_ref[target] += value[at * 8 : (at + 1) * 8]
     for u in range(out_ref.shape[0]):
         for t in range(8):
             tile = sum_ref[pl.ds(u * deep, deep), t, :] + other_ref[pl.ds(u * deep, deep), t, :]
             out_ref[u, :, pl.ds(t * LANES, LANES)] = tile[:stencil].astype(BF16)
 
 
-def final_level(where, targets, arrived, parts, capacity2, owned2, stencil):
+def final_level(lists, arrived, parts, capacity2, owned2, stencil):
     return pl.pallas_call(
         functools.partial(final_kernel, parts=parts, capacity2=capacity2, stencil=stencil),
         out_shape=jax.ShapeDtypeStruct((owned2, stencil, 8 * LANES), BF16),
-        in_specs=[smem(), smem()] + [vmem()] * parts,
+        in_specs=[smem()] + [vmem()] * parts,
         out_specs=vmem(),
         scratch_shapes=[pltpu.VMEM((owned2 * (stencil + 1) + 1, 8, LANES), F32)] * 2,
         compiler_params=params(),
-    )(where, targets, *arrived[::-1])
+    )(lists, *arrived[::-1])
 
 
 def chunks_of(parts):
@@ -606,12 +632,23 @@
     step2 = table_of(coarse_cols // span2 - region + 1, region)
     index2 = (inside // owned * pitch + inside % owned) * 4 + step2
     picked, turned = pick_rows(index2.T, tables[0], table, tables[1], stacked, sent[0])
-    soon = [0] + [d for offsets in chunks[: len(chunks) // 2] for d in offsets]
+    soon = list(chunks[-1]) + [d for offsets in chunks[: len(chunks) // 2] for d in offsets]
     late = [d for d in range(parts) if d not in soon]
-    early = early_sums(where, targets, picked, [arrived[d] for d in soon], soon, capacity, owned, stencil)
-    outs = owner_level(
+    early, lists = early_sums(
         where,
         targets,
+        picked,
+        [arrived[d] for d in soon],
+        soon,
+        late,
+        parts,
+        capacity,
+        capacity2,
+        owned,
+        stencil,
+    )
+    outs = owner_level(
+        lists,
         picked,
         turned,
         early,
@@ -627,7 +664,7 @@
     arrived2 = list(outs[2:])
     for d in range(parts - 1, 0, -1):
         arrived2[d] = exchange(arrived2[d], "dom", d)
-    second = final_level(where, targets, arrived2, parts, capacity2, owned2, stencil)
+    second = final_level(lists, arrived2, parts, capacity2, owned2, stencil)
     return (coarse_blocks, second)
 
 

time: 84 us -> 81.5 us (0.970)
  waiting for transfers between devices: 6.08 us -> 3.93 us
  Pallas kernels: 41.2 us -> 40 us
    ppermute x4, waiting for transfers between devices: 3.47 us -> 1.25 us  [neighbours(): lax.ppermute(cells, axis, [(i, partner(i, odd, count)) for i in range(cou...]
    pallas_call x1, Pallas kernels: 4.94 us -> 3.58 us  [owner_level(): pl.pallas_call(functools.partial(owner_kernel, parts=parts, offsets=offse...]
    pallas_call x1, Pallas kernels: 2.86 us -> 4.17 us  [early_sums(): pl.pallas_call(functools.partial(early_kernel, soon=soon, late=late, **si...]
    pallas_call x1, Pallas kernels: 3.23 us -> 2.11 us  [final_level(): pl.pallas_call(functools.partial(final_kernel, parts=parts, capacity2=cap...]
  transfers between devices with their start and end apart: 18 -> 18, of which waited for: 5 -> 5; matrix products, arithmetic and copies ran while one was open for 2% -> 2% of each run, Pallas kernels for 37% -> 39%
where the time goes in v5:
time: 81.5 us; the launch traced here: 80.5 us
  Pallas kernels  40 us (49%)
  starting transfers between devices  23.4 us (29%)
  blocking collectives  10.6 us (13%)
  waiting for transfers between devices  3.93 us (5%)
  local copies, waits for them, and re-layouts  1.68 us (2%)
    pallas_call x4, Pallas kernels, level_one(): pl.pallas_call(functools.partial(terms_kernel, offsets=offsets, capacity=...  22.8 us
    ppermute x14, starting transfers between devices, exchange(): return lax.ppermute(cells, axis, [(i, i ^ offset) for i in range(count)])  13.7 us
    all_gather x1, blocking collectives, local(): table = lax.all_gather(stacked, 'dom', axis=0, tiled=True)  10.6 us
    ppermute x4, starting transfers between devices, neighbours(): lax.ppermute(cells, axis, [(i, partner(i, odd, count)) for i in range(cou...  9.69 us
    pallas_call x1, Pallas kernels, early_sums(): pl.pallas_call(functools.partial(early_kernel, soon=soon, late=late, **si...  4.17 us
    pallas_call x1, Pallas kernels, owner_level(): pl.pallas_call(functools.partial(owner_kernel, parts=parts, offsets=offse...  3.58 us
    pallas_call x1, Pallas kernels, pick_rows(): pl.pallas_call(pick_kernel, out_shape=(jax.ShapeDtypeStruct((count * sten...  2.83 us
    ppermute x14, waiting for transfers between devices, exchange(): return lax.ppermute(cells, axis, [(i, i ^ offset) for i in range(count)])  2.68 us
  transfers between devices with their start and end apart: 18, of which 5 were waited for; matrix products, arithmetic and copies ran while one was open for 2% of the time, Pallas kernels for 39%

profile of v5, /device:TPU:0, one launch (start us, length us, event | category | flops | bytes accessed | tf_op | source)
XLA Modules:
  0.0 80.5 jit_solution(11125412089819354467)
XLA Ops:
  0.6 2.6 %shard_map.122.rest_8_.own_ref = bf16[48,64,128]{2,1,0:T(8,128)(2,1)S(1)} custom-call(bf16[48,8192]{1,0:T(8,128)(2,1)} %flat_ref.1), custom_call_target="tpu_custom_call" | custom-call | tf_op jit(solution)/shard_map/pallas_call | solution.py:86
  3.2 3.1 %collective-permute-start.1 = (bf16[48,64,128]{2,1,0:T(8,128)(2,1)S(1)}, bf16[48,64,128]{2,1,0:T(8,128)(2,1)S(1)}, u32[]{:S(2)}, u32[]{:S(2)}) collective-permute-start(bf16[48,64,128]{2,1,0:T(8,128)(2,1)S(1)} %shard_map.122.rest_8_.own_ref), channel_id=1, source_target_pairs={{0,8},{8,0},{16,24},{24,16},{1,9},{9,1},{17,25},{25,17},{2,10},{10... | collective-permute-start | bytes 2359304 | tf_op jit(solution)/shard_map/ppermute | solution.py:49
  6.3 0.7 collective-permute-start
  7.0 0.1 pad_add_fusion.where_ref
  7.1 2.0 %shard_map.123 = (s32[24,128]{1,0:T(8,128)S(1)}, bf16[25,16,128]{2,1,0:T(8,128)(2,1)S(1)}) custom-call(s32[2]{0:T(128)S(1)} %pad_add_fusion.where_ref, s32[7,48]{1,0:T(8,128)} %bitcast.20, s32[7,48]{1,0:T(8,128)} %bitcast.21, s32[1,48]{1,0:T(1,128)} %bitcast.23, s32[1,48]{1,0:T(1,128)} %bitcast.24, s32[7,24]{1,0:T(8,128)} %bitcast.22, s32[1,24]{1,0:T(1,128)} %bitcast.25, ...), custom_call_target="tpu_custom_call" | custom-call | tf_op jit(solution)/shard_map/pallas_call | solution.py:597
  9.1 0.0 copy-start
  9.1 10.6 %all_gather.3.own_ref = bf16[200,16,128]{2,1,0:T(8,128)(2,1)S(1)} all-gather(bf16[25,16,128]{2,1,0:T(8,128)(2,1)S(1)} %get-tuple-element.25.mine_ref), channel_id=1, replica_groups=mesh['region'=4,'dom'=8] {'dom'}, dimensions={0}, use_global_device_ids=true | all-gather | bytes 921600 | tf_op jit(solution)/shard_map/all_gather | solution.py:613
  19.6 4.3 %collective-permute-start.3 = (bf16[200,16,128]{2,1,0:T(8,128)(2,1)S(1)}, bf16[200,16,128]{2,1,0:T(8,128)(2,1)}, u32[]{:S(2)}, u32[]{:S(2)}) collective-permute-start(bf16[200,16,128]{2,1,0:T(8,128)(2,1)S(1)} %all_gather.3.own_ref), channel_id=1, source_target_pairs={{0,8},{8,0},{16,24},{24,16},{1,9},{9,1},{17,25},{25,17},{2,10},{10... | collective-permute-start | bytes 2457608 | tf_op jit(solution)/shard_map/ppermute | solution.py:49
  24.0 1.6 %collective-permute-start.2 = (bf16[200,16,128]{2,1,0:T(8,128)(2,1)S(1)}, bf16[200,16,128]{2,1,0:T(8,128)(2,1)}, u32[]{:S(2)}, u32[]{:S(2)}) collective-permute-start(bf16[200,16,128]{2,1,0:T(8,128)(2,1)S(1)} %all_gather.3.own_ref), channel_id=1, source_target_pairs={{0,0},{8,16},{16,8},{24,24},{1,1},{9,17},{17,9},{25,25},{2,2},{10,... | collective-permute-start | bytes 2457608 | tf_op jit(solution)/shard_map/ppermute | solution.py:49
  25.5 0.0 collective-permute-done.1.after_ref
  25.5 0.0 collective-permute-done.before_ref
  25.5 6.2 %shard_map.124 = (bf16[1344,128]{1,0:T(8,128)(2,1)}, bf16[1344,128]{1,0:T(8,128)(2,1)}) custom-call(s32[24,128]{1,0:T(8,128)} %copy-done.2, bf16[48,7,128,128]{3,2,1,0:T(8,128)(2,1)} %blocks_ref.7, bf16[48,64,128]{2,1,0:T(8,128)(2,1)S(1)} %collective-permute-done.before_ref, bf16[48,64,128]{2,1,0:T(8,128)(2,1)S(1)} %shard_map.122.rest_8_.own_ref, ...), custom_call_target="tpu_custom_call" | custom-call | tf_op jit(solution)/shard_map/pallas_call | solution.py:273
  31.8 1.5 %collective-permute-start.5 = (bf16[1344,128]{1,0:T(8,128)(2,1)}, bf16[1344,128]{1,0:T(8,128)(2,1)S(1)}, u32[]{:S(2)}, u32[]{:S(2)}) collective-permute-start(bf16[1344,128]{1,0:T(8,128)(2,1)} %get-tuple-element.30), channel_id=1, source_target_pairs={{0,6},{1,7},{2,4},{3,5},{4,2},{5,3},{6,0},{7,1},{8,14},{9,15},{10,... | collective-permute-start | bytes 1032200 | tf_op jit(solution)/shard_map/ppermute | solution.py:39
  33.3 0.9 %collective-permute-start.4 = (bf16[1344,128]{1,0:T(8,128)(2,1)}, bf16[1344,128]{1,0:T(8,128)(2,1)}, u32[]{:S(2)}, u32[]{:S(2)}) collective-permute-start(bf16[1344,128]{1,0:T(8,128)(2,1)} %get-tuple-element.27.rest_0_), channel_id=1, source_target_pairs={{0,7},{1,6},{2,5},{3,4},{4,3},{5,2},{6,1},{7,0},{8,15},{9,14},{10,... | collective-permute-start | bytes 1032200 | tf_op jit(solution)/shard_map/ppermute | solution.py:39
  34.2 5.5 %shard_map.125 = (bf16[1344,128]{1,0:T(8,128)(2,1)S(1)}, bf16[1344,128]{1,0:T(8,128)(2,1)S(1)}) custom-call(s32[24,128]{1,0:T(8,128)} %copy-done.2, bf16[48,7,128,128]{3,2,1,0:T(8,128)(2,1)} %blocks_ref.7, bf16[48,64,128]{2,1,0:T(8,128)(2,1)S(1)} %collective-permute-done.before_ref, bf16[48,64,128]{2,1,0:T(8,128)(2,1)S(1)} %shard_map.122.rest_8_.own_ref, ...), custom_call_target="tpu_custom_call" | custom-call | tf_op jit(solution)/shard_map/pallas_call | solution.py:273
  39.7 1.9 %collective-permute-start.8 = (bf16[1344,128]{1,0:T(8,128)(2,1)S(1)}, bf16[1344,128]{1,0:T(8,128)(2,1)S(1)}, u32[]{:S(2)}, u32[]{:S(2)}) collective-permute-start(bf16[1344,128]{1,0:T(8,128)(2,1)S(1)} %get-tuple-element.33), channel_id=1, source_target_pairs={{0,3},{1,2},{2,1},{3,0},{4,7},{5,6},{6,5},{7,4},{8,11},{9,10},{10,... | collective-permute-start | bytes 1032200 | tf_op jit(solution)/shard_map/ppermute | solution.py:39
  41.6 1.2 %collective-permute-done.3.rest_2_.second_ref = bf16[200,16,128]{2,1,0:T(8,128)(2,1)} collective-permute-done((bf16[200,16,128]{2,1,0:T(8,128)(2,1)S(1)}, bf16[200,16,128]{2,1,0:T(8,128)(2,1)}, u32[]{:S(2)}, u32[]{:S(2)}) %collective-permute-start.3) | collective-permute-done | bytes 819232 | tf_op jit(solution)/shard_map/ppermute | solution.py:49
  42.8 0.9 %collective-permute-start.7 = (bf16[1344,128]{1,0:T(8,128)(2,1)S(1)}, bf16[1344,128]{1,0:T(8,128)(2,1)S(1)}, u32[]{:S(2)}, u32[]{:S(2)}) collective-permute-start(bf16[1344,128]{1,0:T(8,128)(2,1)S(1)} %get-tuple-element.28.rest_0_), channel_id=1, source_target_pairs={{0,5},{1,4},{2,7},{3,6},{4,1},{5,0},{6,3},{7,2},{8,13},{9,12},{10,... | collective-permute-start | bytes 1032200 | tf_op jit(solution)/shard_map/ppermute | solution.py:39
  43.7 0.0 collective-permute-done.2.rest_1_.first_ref
  43.7 5.5 %shard_map.126 = (bf16[1344,128]{1,0:T(8,128)(2,1)S(1)}, bf16[1344,128]{1,0:T(8,128)(2,1)S(1)}) custom-call(s32[24,128]{1,0:T(8,128)} %copy-done.2, bf16[48,7,128,128]{3,2,1,0:T(8,128)(2,1)} %blocks_ref.7, bf16[48,64,128]{2,1,0:T(8,128)(2,1)S(1)} %collective-permute-done.before_ref, bf16[48,64,128]{2,1,0:T(8,128)(2,1)S(1)} %shard_map.122.rest_8_.own_ref, ...), custom_call_target="tpu_custom_call" | custom-call | tf_op jit(solution)/shard_map/pallas_call | solution.py:273
  49.2 0.7 collective-permute-start.9
  49.9 0.0 collective-permute-done.5.rest_2_.rest_3_
  49.9 1.4 %collective-permute-start.10 = (bf16[1344,128]{1,0:T(8,128)(2,1)S(1)}, bf16[1344,128]{1,0:T(8,128)(2,1)S(1)}, u32[]{:S(2)}, u32[]{:S(2)}) collective-permute-start(bf16[1344,128]{1,0:T(8,128)(2,1)S(1)} %get-tuple-element.29.rest_0_), channel_id=1, source_target_pairs={{0,4},{1,5},{2,6},{3,7},{4,0},{5,1},{6,2},{7,3},{8,12},{9,13},{10,... | collective-permute-start | bytes 1032200 | tf_op jit(solution)/shard_map/ppermute | solution.py:39
  51.3 0.0 collective-permute-done.4.rest_1_.rest_2_
  51.3 5.5 %shard_map.127 = (bf16[1344,128]{1,0:T(8,128)(2,1)S(1)}, bf16[1344,128]{1,0:T(8,128)(2,1)S(1)}) custom-call(s32[24,128]{1,0:T(8,128)} %copy-done.2, bf16[48,7,128,128]{3,2,1,0:T(8,128)(2,1)} %blocks_ref.7, bf16[48,64,128]{2,1,0:T(8,128)(2,1)S(1)} %collective-permute-done.before_ref, bf16[48,64,128]{2,1,0:T(8,128)(2,1)S(1)} %shard_map.122.rest_8_.own_ref, ...), custom_call_target="tpu_custom_call" | custom-call | tf_op jit(solution)/shard_map/pallas_call | solution.py:273
  56.9 0.2 collective-permute-start.6
  57.2 2.8 %shard_map.128 = (bf16[168,16,128]{2,1,0:T(8,128)(2,1)S(1)}, bf16[24,32,64]{2,1,0:T(8,128)(2,1)S(1)}) custom-call(s32[7,24]{1,0:T(8,128)S(1)} %fusion.4.index_ref, bf16[200,16,128]{2,1,0:T(8,128)(2,1)} %collective-permute-done.2.rest_1_.first_ref, bf16[200,16,128]{2,1,0:T(8,128)(2,1)S(1)} %all_gather.3.own_ref, ...), custom_call_target="tpu_custom_call" | custom-call | tf_op jit(solution)/shard_map/pallas_call | solution.py:341
  60.0 0.0 collective-permute-done.8.rest_5_
  60.0 0.0 collective-permute-done.7.rest_4_
  60.0 0.0 collective-permute-done.6.rest_0_
  60.1 4.2 %shard_map.129 = (f32[169,32,128]{2,1,0:T(8,128)S(1)}, s32[276]{0:T(512)S(1)}) custom-call(s32[2]{0:T(128)S(1)} %pad_add_fusion.where_ref, s32[128,128]{1,0:T(8,128)S(1)} %bitcast_convert_fusion.table_ref, bf16[1344,128]{1,0:T(8,128)(2,1)S(1)} %collective-permute-done.6.rest_0_, bf16[1344,128]{1,0:T(8,128)(2,1)S(1)} %get-tuple-element.32.rest_1_, ...), custom_call_target="tpu_custom_call" | custom-call | tf_op jit(solution)/shard_map/pallas_call | solution.py:399
  64.2 1.0 %collective-permute-done.9.rest_0_ = bf16[1344,128]{1,0:T(8,128)(2,1)S(1)} collective-permute-done((bf16[1344,128]{1,0:T(8,128)(2,1)S(1)}, bf16[1344,128]{1,0:T(8,128)(2,1)S(1)}, u32[]{:S(2)}, u32[]{:S(2)}) %collective-permute-start.9) | collective-permute-done | bytes 344096 | tf_op jit(solution)/shard_map/ppermute | solution.py:39
  65.2 0.0 collective-permute-done.10.rest_1_
  65.2 3.6 %shard_map.130 = (bf16[168,32,128]{2,1,0:T(8,128)(2,1)S(1)}, f32[169,32,128]{2,1,0:T(8,128)S(1)}, bf16[168,128]{1,0:T(8,128)(2,1)S(1)}, bf16[168,128]{1,0:T(8,12...) custom-call(s32[276]{0:T(512)S(1)} %get-tuple-element.35.lists_ref, ...), custom_call_target="tpu_custom_call", output_to_operand_aliasing={{1}: (3, {})} | custom-call | tf_op jit(solution)/shard_map/pallas_call | solution.py:496
  68.8 1.1 %collective-permute-start.11 = (bf16[168,128]{1,0:T(8,128)(2,1)S(1)}, bf16[168,128]{1,0:T(8,128)(2,1)S(1)}, u32[]{:S(2)}, u32[]{:S(2)}) collective-permute-start(bf16[168,128]{1,0:T(8,128)(2,1)S(1)} %get-tuple-element.40), channel_id=1, source_target_pairs={{0,7},{1,6},{2,5},{3,4},{4,3},{5,2},{6,1},{7,0},{8,15},{9,14},{10,... | collective-permute-start | bytes 129032 | tf_op jit(solution)/shard_map/ppermute | solution.py:39
  69.9 1.4 %collective-permute-start.12 = (bf16[168,128]{1,0:T(8,128)(2,1)S(1)}, bf16[168,128]{1,0:T(8,128)(2,1)S(1)}, u32[]{:S(2)}, u32[]{:S(2)}) collective-permute-start(bf16[168,128]{1,0:T(8,128)(2,1)S(1)} %get-tuple-element.41), channel_id=1, source_target_pairs={{0,6},{1,7},{2,4},{3,5},{4,2},{5,3},{6,0},{7,1},{8,14},{9,15},{10,... | collective-permute-start | bytes 129032 | tf_op jit(solution)/shard_map/ppermute | solution.py:39
  71.4 1.2 %collective-permute-start.13 = (bf16[168,128]{1,0:T(8,128)(2,1)S(1)}, bf16[168,128]{1,0:T(8,128)(2,1)S(1)}, u32[]{:S(2)}, u32[]{:S(2)}) collective-permute-start(bf16[168,128]{1,0:T(8,128)(2,1)S(1)} %get-tuple-element.42), channel_id=1, source_target_pairs={{0,5},{1,4},{2,7},{3,6},{4,1},{5,0},{6,3},{7,2},{8,13},{9,12},{10,... | collective-permute-start | bytes 129032 | tf_op jit(solution)/shard_map/ppermute | solution.py:39
  72.6 0.7 collective-permute-start.14
  73.3 1.1 %collective-permute-start.15 = (bf16[168,128]{1,0:T(8,128)(2,1)S(1)}, bf16[168,128]{1,0:T(8,128)(2,1)S(1)}, u32[]{:S(2)}, u32[]{:S(2)}) collective-permute-start(bf16[168,128]{1,0:T(8,128)(2,1)S(1)} %get-tuple-element.44), channel_id=1, source_target_pairs={{0,3},{1,2},{2,1},{3,0},{4,7},{5,6},{6,5},{7,4},{8,11},{9,10},{10,... | collective-permute-start | bytes 129032 | tf_op jit(solution)/shard_map/ppermute | solution.py:39
  74.4 0.0 collective-permute-done.11.rest_0_
  74.4 0.5 collective-permute-start.16
  74.9 0.1 collective-permute-done.12.rest_1_
  75.0 0.2 collective-permute-start.17
  75.1 1.7 %reshape.21 = bf16[7,24,4096]{2,1,0:T(8,128)(2,1)} reshape(bf16[168,32,128]{2,1,0:T(8,128)(2,1)S(1)} %get-tuple-element.39) | data formatting | bytes 2752512 | tf_op jit(solution)/shard_map/reshape | solution.py:663
  76.8 0.0 collective-permute-done.14.rest_3_
  76.8 0.2 collective-permute-done.15.rest_4_
  77.0 1.4 %collective-permute-done.16.rest_5_ = bf16[168,128]{1,0:T(8,128)(2,1)S(1)} collective-permute-done((bf16[168,128]{1,0:T(8,128)(2,1)S(1)}, bf16[168,128]{1,0:T(8,128)(2,1)S(1)}, u32[]{:S(2)}, u32[]{:S(2)}) %collective-permute-start.16) | collective-permute-done | bytes 43040 | tf_op jit(solution)/shard_map/ppermute | solution.py:39
  78.4 2.1 %shard_map.131 = bf16[12,7,1024]{2,1,0:T(8,128)(2,1)} custom-call(s32[276]{0:T(512)S(1)} %get-tuple-element.35.lists_ref, bf16[168,128]{1,0:T(8,128)(2,1)S(1)} %collective-permute-done.11.rest_0_, bf16[168,128]{1,0:T(8,128)(2,1)S(1)} %collective-permute-done.12.rest_1_, bf16[168,128]{1,0:T(8,128)(2,1)S(1)} %collective-permute-done.13.rest_2_, ...), custom_call_target="tpu_custom_call" | custom-call | tf_op jit(solution)/shard_map/pallas_call | solution.py:543
  (12 shorter events, 0.1 us)
Async XLA Ops:
  3.2 22.3 %collective-permute-start.1 = (bf16[48,64,128]{2,1,0:T(8,128)(2,1)S(1)}, bf16[48,64,128]{2,1,0:T(8,128)(2,1)S(1)}, u32[]{:S(2)}, u32[]{:S(2)}) collective-permute-start(bf16[48,64,128]{2,1,0:T(8,128)(2,1)S(1)} %shard_map.122.rest_8_.own_ref), channel_id=1, source_target_pairs={{0,8},{8,0},{16,24},{24,16},{1,9},{9,1},{17,25},{25,17},{2,10},{10... | collective-permute-start | bytes 2359304 | tf_op jit(solution)/shard_map/ppermute | solution.py:49
  6.3 19.2 %collective-permute-start = (bf16[48,64,128]{2,1,0:T(8,128)(2,1)S(1)}, bf16[48,64,128]{2,1,0:T(8,128)(2,1)S(1)}, u32[]{:S(2)}, u32[]{:S(2)}) collective-permute-start(bf16[48,64,128]{2,1,0:T(8,128)(2,1)S(1)} %shard_map.122.rest_8_.own_ref), channel_id=1, source_target_pairs={{0,0},{8,16},{16,8},{24,24},{1,1},{9,17},{17,9},{25,25},{2,2},{10,... | collective-permute-start | bytes 2359304 | tf_op jit(solution)/shard_map/ppermute | solution.py:49
  9.1 16.5 %copy-start.2 = (s32[24,128]{1,0:T(8,128)}, s32[24,128]{1,0:T(8,128)S(1)}, u32[]{:S(2)}) copy-start(s32[24,128]{1,0:T(8,128)S(1)} %get-tuple-element.26.table_ref) | copy-start | bytes 36868
  9.1 22.7 %copy-start = (bf16[25,16,128]{2,1,0:T(8,128)(2,1)}, bf16[25,16,128]{2,1,0:T(8,128)(2,1)S(1)}, u32[]{:S(2)}) copy-start(bf16[25,16,128]{2,1,0:T(8,128)(2,1)S(1)} %get-tuple-element.25.mine_ref) | copy-start | bytes 307204
  19.6 23.2 %collective-permute-start.3 = (bf16[200,16,128]{2,1,0:T(8,128)(2,1)S(1)}, bf16[200,16,128]{2,1,0:T(8,128)(2,1)}, u32[]{:S(2)}, u32[]{:S(2)}) collective-permute-start(bf16[200,16,128]{2,1,0:T(8,128)(2,1)S(1)} %all_gather.3.own_ref), channel_id=1, source_target_pairs={{0,8},{8,0},{16,24},{24,16},{1,9},{9,1},{17,25},{25,17},{2,10},{10... | collective-permute-start | bytes 2457608 | tf_op jit(solution)/shard_map/ppermute | solution.py:49
  24.0 19.7 %collective-permute-start.2 = (bf16[200,16,128]{2,1,0:T(8,128)(2,1)S(1)}, bf16[200,16,128]{2,1,0:T(8,128)(2,1)}, u32[]{:S(2)}, u32[]{:S(2)}) collective-permute-start(bf16[200,16,128]{2,1,0:T(8,128)(2,1)S(1)} %all_gather.3.own_ref), channel_id=1, source_target_pairs={{0,0},{8,16},{16,8},{24,24},{1,1},{9,17},{17,9},{25,25},{2,2},{10,... | collective-permute-start | bytes 2457608 | tf_op jit(solution)/shard_map/ppermute | solution.py:49
  31.8 18.1 %collective-permute-start.5 = (bf16[1344,128]{1,0:T(8,128)(2,1)}, bf16[1344,128]{1,0:T(8,128)(2,1)S(1)}, u32[]{:S(2)}, u32[]{:S(2)}) collective-permute-start(bf16[1344,128]{1,0:T(8,128)(2,1)} %get-tuple-element.30), channel_id=1, source_target_pairs={{0,6},{1,7},{2,4},{3,5},{4,2},{5,3},{6,0},{7,1},{8,14},{9,15},{10,... | collective-permute-start | bytes 1032200 | tf_op jit(solution)/shard_map/ppermute | solution.py:39
  33.3 18.0 %collective-permute-start.4 = (bf16[1344,128]{1,0:T(8,128)(2,1)}, bf16[1344,128]{1,0:T(8,128)(2,1)}, u32[]{:S(2)}, u32[]{:S(2)}) collective-permute-start(bf16[1344,128]{1,0:T(8,128)(2,1)} %get-tuple-element.27.rest_0_), channel_id=1, source_target_pairs={{0,7},{1,6},{2,5},{3,4},{4,3},{5,2},{6,1},{7,0},{8,15},{9,14},{10,... | collective-permute-start | bytes 1032200 | tf_op jit(solution)/shard_map/ppermute | solution.py:39
  39.7 20.3 %collective-permute-start.8 = (bf16[1344,128]{1,0:T(8,128)(2,1)S(1)}, bf16[1344,128]{1,0:T(8,128)(2,1)S(1)}, u32[]{:S(2)}, u32[]{:S(2)}) collective-permute-start(bf16[1344,128]{1,0:T(8,128)(2,1)S(1)} %get-tuple-element.33), channel_id=1, source_target_pairs={{0,3},{1,2},{2,1},{3,0},{4,7},{5,6},{6,5},{7,4},{8,11},{9,10},{10,... | collective-permute-start | bytes 1032200 | tf_op jit(solution)/shard_map/ppermute | solution.py:39
  42.8 17.2 %collective-permute-start.7 = (bf16[1344,128]{1,0:T(8,128)(2,1)S(1)}, bf16[1344,128]{1,0:T(8,128)(2,1)S(1)}, u32[]{:S(2)}, u32[]{:S(2)}) collective-permute-start(bf16[1344,128]{1,0:T(8,128)(2,1)S(1)} %get-tuple-element.28.rest_0_), channel_id=1, source_target_pairs={{0,5},{1,4},{2,7},{3,6},{4,1},{5,0},{6,3},{7,2},{8,13},{9,12},{10,... | collective-permute-start | bytes 1032200 | tf_op jit(solution)/shard_map/ppermute | solution.py:39
  49.2 16.0 %collective-permute-start.9 = (bf16[1344,128]{1,0:T(8,128)(2,1)S(1)}, bf16[1344,128]{1,0:T(8,128)(2,1)S(1)}, u32[]{:S(2)}, u32[]{:S(2)}) collective-permute-start(bf16[1344,128]{1,0:T(8,128)(2,1)S(1)} %get-tuple-element.38), channel_id=1, source_target_pairs={{0,2},{1,3},{2,0},{3,1},{4,6},{5,7},{6,4},{7,5},{8,10},{9,11},{10,... | collective-permute-start | bytes 1032200 | tf_op jit(solution)/shard_map/ppermute | solution.py:39
  49.9 7.2 %copy-start.3 = (s32[24,7]{0,1:T(8,128)S(1)}, s32[24,7]{0,1:T(8,128)}, u32[]{:S(2)}) copy-start(s32[24,7]{0,1:T(8,128)} %param.18) | copy-start | bytes 2020
  49.9 7.2 %copy-start.1 = (bf16[25,16,128]{2,1,0:T(8,128)(2,1)S(1)}, bf16[25,16,128]{2,1,0:T(8,128)(2,1)}, u32[]{:S(2)}) copy-start(bf16[25,16,128]{2,1,0:T(8,128)(2,1)} %copy-done) | copy-start | bytes 307204
  49.9 15.3 %collective-permute-start.10 = (bf16[1344,128]{1,0:T(8,128)(2,1)S(1)}, bf16[1344,128]{1,0:T(8,128)(2,1)S(1)}, u32[]{:S(2)}, u32[]{:S(2)}) collective-permute-start(bf16[1344,128]{1,0:T(8,128)(2,1)S(1)} %get-tuple-element.29.rest_0_), channel_id=1, source_target_pairs={{0,4},{1,5},{2,6},{3,7},{4,0},{5,1},{6,2},{7,3},{8,12},{9,13},{10,... | collective-permute-start | bytes 1032200 | tf_op jit(solution)/shard_map/ppermute | solution.py:39
  56.9 3.2 %collective-permute-start.6 = (bf16[1344,128]{1,0:T(8,128)(2,1)S(1)}, bf16[1344,128]{1,0:T(8,128)(2,1)S(1)}, u32[]{:S(2)}, u32[]{:S(2)}) collective-permute-start(bf16[1344,128]{1,0:T(8,128)(2,1)S(1)} %get-tuple-element.31.waited_ref), channel_id=1, source_target_pairs={{0,1},{1,0},{2,3},{3,2},{4,5},{5,4},{6,7},{7,6},{8,9},{9,8},{10,11... | collective-permute-start | bytes 1032200 | tf_op jit(solution)/shard_map/ppermute | solution.py:39
  68.8 5.5 %collective-permute-start.11 = (bf16[168,128]{1,0:T(8,128)(2,1)S(1)}, bf16[168,128]{1,0:T(8,128)(2,1)S(1)}, u32[]{:S(2)}, u32[]{:S(2)}) collective-permute-start(bf16[168,128]{1,0:T(8,128)(2,1)S(1)} %get-tuple-element.40), channel_id=1, source_target_pairs={{0,7},{1,6},{2,5},{3,4},{4,3},{5,2},{6,1},{7,0},{8,15},{9,14},{10,... | collective-permute-start | bytes 129032 | tf_op jit(solution)/shard_map/ppermute | solution.py:39
  69.9 5.0 %collective-permute-start.12 = (bf16[168,128]{1,0:T(8,128)(2,1)S(1)}, bf16[168,128]{1,0:T(8,128)(2,1)S(1)}, u32[]{:S(2)}, u32[]{:S(2)}) collective-permute-start(bf16[168,128]{1,0:T(8,128)(2,1)S(1)} %get-tuple-element.41), channel_id=1, source_target_pairs={{0,6},{1,7},{2,4},{3,5},{4,2},{5,3},{6,0},{7,1},{8,14},{9,15},{10,... | collective-permute-start | bytes 129032 | tf_op jit(solution)/shard_map/ppermute | solution.py:39
  71.4 5.4 %collective-permute-start.13 = (bf16[168,128]{1,0:T(8,128)(2,1)S(1)}, bf16[168,128]{1,0:T(8,128)(2,1)S(1)}, u32[]{:S(2)}, u32[]{:S(2)}) collective-permute-start(bf16[168,128]{1,0:T(8,128)(2,1)S(1)} %get-tuple-element.42), channel_id=1, source_target_pairs={{0,5},{1,4},{2,7},{3,6},{4,1},{5,0},{6,3},{7,2},{8,13},{9,12},{10,... | collective-permute-start | bytes 129032 | tf_op jit(solution)/shard_map/ppermute | solution.py:39
  72.6 4.2 %collective-permute-start.14 = (bf16[168,128]{1,0:T(8,128)(2,1)S(1)}, bf16[168,128]{1,0:T(8,128)(2,1)S(1)}, u32[]{:S(2)}, u32[]{:S(2)}) collective-permute-start(bf16[168,128]{1,0:T(8,128)(2,1)S(1)} %get-tuple-element.43), channel_id=1, source_target_pairs={{0,4},{1,5},{2,6},{3,7},{4,0},{5,1},{6,2},{7,3},{8,12},{9,13},{10,... | collective-permute-start | bytes 129032 | tf_op jit(solution)/shard_map/ppermute | solution.py:39
  73.3 3.8 %collective-permute-start.15 = (bf16[168,128]{1,0:T(8,128)(2,1)S(1)}, bf16[168,128]{1,0:T(8,128)(2,1)S(1)}, u32[]{:S(2)}, u32[]{:S(2)}) collective-permute-start(bf16[168,128]{1,0:T(8,128)(2,1)S(1)} %get-tuple-element.44), channel_id=1, source_target_pairs={{0,3},{1,2},{2,1},{3,0},{4,7},{5,6},{6,5},{7,4},{8,11},{9,10},{10,... | collective-permute-start | bytes 129032 | tf_op jit(solution)/shard_map/ppermute | solution.py:39
  74.4 4.0 %collective-permute-start.16 = (bf16[168,128]{1,0:T(8,128)(2,1)S(1)}, bf16[168,128]{1,0:T(8,128)(2,1)S(1)}, u32[]{:S(2)}, u32[]{:S(2)}) collective-permute-start(bf16[168,128]{1,0:T(8,128)(2,1)S(1)} %get-tuple-element.45), channel_id=1, source_target_pairs={{0,2},{1,3},{2,0},{3,1},{4,6},{5,7},{6,4},{7,5},{8,10},{9,11},{10,... | collective-permute-start | bytes 129032 | tf_op jit(solution)/shard_map/ppermute | solution.py:39
  75.0 3.4 %collective-permute-start.17 = (bf16[168,128]{1,0:T(8,128)(2,1)S(1)}, bf16[168,128]{1,0:T(8,128)(2,1)S(1)}, u32[]{:S(2)}, u32[]{:S(2)}) collective-permute-start(bf16[168,128]{1,0:T(8,128)(2,1)S(1)} %get-tuple-element.46), channel_id=1, source_target_pairs={{0,1},{1,0},{2,3},{3,2},{4,5},{5,4},{6,7},{7,6},{8,9},{9,8},{10,11... | collective-permute-start | bytes 129032 | tf_op jit(solution)/shard_map/ppermute | solution.py:39

commit v6 on v5

--- a/solution.py
+++ b/solution.py
@@ -189,17 +189,14 @@
     stacked_ref[rows2] = info_ref[0 : 2 * group, :].astype(F32).astype(BF16)
 
 
-def terms_kernel(table_ref, blocks_ref, before_ref, own_ref, after_ref, *rest, offsets, capacity, waited):
+def terms_kernel(info_ref, blocks_ref, before_ref, own_ref, after_ref, *rest, offsets, capacity, waited):
     outs = rest[waited : waited + len(offsets)]
-    info_ref, buffer_ref, info_sem, row_sem = rest[waited + len(offsets) :]
+    buffer_ref, row_sem = rest[waited + len(offsets) :]
     stencil, width = buffer_ref.shape[1], buffer_ref.shape[2]
     half = width // 2
     narrow = LANES // 2
     flat = narrow * narrow // LANES
 
-    table_copy = pltpu.make_async_copy(table_ref, info_ref, info_sem)
-    table_copy.start()
-    table_copy.wait()
     dom = info_ref[3 * (stencil + 1) - 1, 0]
 
     def source_of(offset, r):
@@ -208,10 +205,11 @@
     def row_copy(n, source):
         return pltpu.make_async_copy(blocks_ref.at[source], buffer_ref.at[n], row_sem.at[n])
 
-    for n, offset in enumerate(offsets):
+    def fetch(n):
         for r in range(capacity):
-            row_copy(n * capacity + r, source_of(offset, r)).start()
-
+            row_copy(n * capacity + r, source_of(offsets[n], r)).start()
+
+    fetch(0)
     left = low_lanes((half, LANES), narrow)
     left_flat = low_lanes((flat, LANES), narrow)
     out_row = lax.broadcasted_iota(I32, (narrow, LANES), 0)
@@ -247,19 +245,19 @@
         term = jnp.dot(turned, jnp.concatenate(products, axis=1), preferred_element_type=F32)
         for k in range(0, stencil, 2):
             pair = term[:, k // 2 * LANES : (k // 2 + 1) * LANES]
-            even = pair[:flat]
-            odd = pair[flat:]
+            even = pair[:flat].astype(BF16)
+            odd = pair[flat:].astype(BF16)
             base = (r * stencil + k) * flat
-            out_ref[pl.ds(base, flat), :] = jnp.where(left_flat, even, pltpu.roll(odd, narrow, 1)).astype(BF16)
+            out_ref[pl.ds(base, flat), :] = jnp.where(left_flat, even, pltpu.roll(odd, narrow, 1))
             if k + 1 < stencil:
-                out_ref[pl.ds(base + flat, flat), :] = jnp.where(
-                    left_flat, pltpu.roll(even, narrow, 1), odd
-                ).astype(BF16)
+                out_ref[pl.ds(base + flat, flat), :] = jnp.where(left_flat, pltpu.roll(even, narrow, 1), odd)
 
     for n, offset in enumerate(offsets):
         sources = [source_of(offset, r) for r in range(capacity)]
         for r, source in enumerate(sources):
             row_copy(n * capacity + r, source).wait()
+        if n + 1 < len(offsets):
+            fetch(n + 1)
         for r, source in enumerate(sources):
             one_row(n * capacity + r, source, outs[n], r)
 
@@ -273,17 +271,15 @@
     return pl.pallas_call(
         functools.partial(terms_kernel, offsets=offsets, capacity=capacity, waited=len(waited)),
         out_shape=tuple(shape for _ in offsets),
-        in_specs=[hbm(), hbm(), vmem(), vmem(), vmem()] + [hbm()] * len(waited),
+        in_specs=[smem(), hbm(), vmem(), vmem(), vmem()] + [hbm()] * len(waited),
         out_specs=tuple(vmem() for _ in offsets),
         scratch_shapes=[
-            pltpu.SMEM(info.shape, I32),
             pltpu.VMEM((count, stencil, width, width), BF16),
-            pltpu.SemaphoreType.DMA(()),
             pltpu.SemaphoreType.DMA((count,)),
         ],
         compiler_params=params(),
     )(
-        pltpu.with_memory_space_constraint(info, pltpu.HBM),
+        info,
         pltpu.with_memory_space_constraint(blocks, pltpu.HBM),
         before,
         own,
@@ -552,7 +548,8 @@
 
 def chunks_of(parts):
     order = sorted(range(parts), key=lambda d: (-(d >> 1).bit_count(), -(d & 1), -d))
-    return [tuple(order[i : i + 2]) for i in range(0, parts, 2)]
+    pairs = [tuple(order[i : i + 2]) for i in range(0, parts, 2)]
+    return pairs[:-2] + [pairs[-2] + pairs[-1]]
 
 
 def local(
@@ -632,7 +629,7 @@
     step2 = table_of(coarse_cols // span2 - region + 1, region)
     index2 = (inside // owned * pitch + inside % owned) * 4 + step2
     picked, turned = pick_rows(index2.T, tables[0], table, tables[1], stacked, sent[0])
-    soon = list(chunks[-1]) + [d for offsets in chunks[: len(chunks) // 2] for d in offsets]
+    soon = list(chunks[-1][2:]) + [d for offsets in chunks[: (parts // 2) // 2] for d in offsets]
     late = [d for d in range(parts) if d not in soon]
     early, lists = early_sums(
         where,

time: 81.5 us -> 80.7 us (level)
  Pallas kernels: 40 us -> 37.2 us
  waiting for transfers between devices: 3.93 us -> 6.06 us
    pallas_call x4 -> x3, Pallas kernels: 22.8 us -> 20.1 us  [level_one(): pl.pallas_call(functools.partial(terms_kernel, offsets=offsets, capacity=...]
    ppermute x14, waiting for transfers between devices: 2.68 us -> 4.51 us  [exchange(): return lax.ppermute(cells, axis, [(i, i ^ offset) for i in range(count)])]
  transfers between devices with their start and end apart: 18 -> 18, of which waited for: 5 -> 4; matrix products, arithmetic and copies ran while one was open for 2% -> 2% of each run, Pallas kernels for 39% -> 36%
where the time goes in v6:
time: 80.7 us; the launch traced here: 80.3 us
  Pallas kernels  37.2 us (46%)
  starting transfers between devices  24 us (30%)
  blocking collectives  10.6 us (13%)
  waiting for transfers between devices  6.06 us (8%)
  local copies, waits for them, and re-layouts  1.66 us (2%)
    pallas_call x3, Pallas kernels, level_one(): pl.pallas_call(functools.partial(terms_kernel, offsets=offsets, capacity=...  20.1 us
    ppermute x14, starting transfers between devices, exchange(): return lax.ppermute(cells, axis, [(i, i ^ offset) for i in range(count)])  14.3 us
    all_gather x1, blocking collectives, local(): table = lax.all_gather(stacked, 'dom', axis=0, tiled=True)  10.6 us
    ppermute x4, starting transfers between devices, neighbours(): lax.ppermute(cells, axis, [(i, partner(i, odd, count)) for i in range(cou...  9.68 us
    ppermute x14, waiting for transfers between devices, exchange(): return lax.ppermute(cells, axis, [(i, i ^ offset) for i in range(count)])  4.51 us
    pallas_call x1, Pallas kernels, early_sums(): pl.pallas_call(functools.partial(early_kernel, soon=soon, late=late, **si...  4.16 us
    pallas_call x1, Pallas kernels, owner_level(): pl.pallas_call(functools.partial(owner_kernel, parts=parts, offsets=offse...  3.52 us
    pallas_call x1, Pallas kernels, pick_rows(): pl.pallas_call(pick_kernel, out_shape=(jax.ShapeDtypeStruct((count * sten...  2.83 us
  transfers between devices with their start and end apart: 18, of which 4 were waited for; matrix products, arithmetic and copies ran while one was open for 2% of the time, Pallas kernels for 36%

profile of v6, /device:TPU:0, one launch (start us, length us, event | category | flops | bytes accessed | tf_op | source)
XLA Modules:
  0.0 80.3 jit_solution(120386699943064516)
XLA Ops:
  0.6 2.6 %shard_map.122.rest_8_.own_ref = bf16[48,64,128]{2,1,0:T(8,128)(2,1)S(1)} custom-call(bf16[48,8192]{1,0:T(8,128)(2,1)} %flat_ref.1), custom_call_target="tpu_custom_call" | custom-call | tf_op jit(solution)/shard_map/pallas_call | solution.py:86
  3.2 3.1 %collective-permute-start.1 = (bf16[48,64,128]{2,1,0:T(8,128)(2,1)S(1)}, bf16[48,64,128]{2,1,0:T(8,128)(2,1)S(1)}, u32[]{:S(2)}, u32[]{:S(2)}) collective-permute-start(bf16[48,64,128]{2,1,0:T(8,128)(2,1)S(1)} %shard_map.122.rest_8_.own_ref), channel_id=1, source_target_pairs={{0,8},{8,0},{16,24},{24,16},{1,9},{9,1},{17,25},{25,17},{2,10},{10... | collective-permute-start | bytes 2359304 | tf_op jit(solution)/shard_map/ppermute | solution.py:49
  6.3 0.7 collective-permute-start
  7.0 0.1 pad_add_fusion.where_ref
  7.1 2.0 %shard_map.123 = (s32[24,128]{1,0:T(8,128)S(1)}, bf16[25,16,128]{2,1,0:T(8,128)(2,1)S(1)}) custom-call(s32[2]{0:T(128)S(1)} %pad_add_fusion.where_ref, s32[7,48]{1,0:T(8,128)} %bitcast.20, s32[7,48]{1,0:T(8,128)} %bitcast.21, s32[1,48]{1,0:T(1,128)} %bitcast.23, s32[1,48]{1,0:T(1,128)} %bitcast.24, s32[7,24]{1,0:T(8,128)} %bitcast.22, s32[1,24]{1,0:T(1,128)} %bitcast.25, ...), custom_call_target="tpu_custom_call" | custom-call | tf_op jit(solution)/shard_map/pallas_call | solution.py:594
  9.1 10.6 %all_gather.3.own_ref = bf16[200,16,128]{2,1,0:T(8,128)(2,1)S(1)} all-gather(bf16[25,16,128]{2,1,0:T(8,128)(2,1)S(1)} %get-tuple-element.25.mine_ref), channel_id=1, replica_groups=mesh['region'=4,'dom'=8] {'dom'}, dimensions={0}, use_global_device_ids=true | all-gather | bytes 921600 | tf_op jit(solution)/shard_map/all_gather | solution.py:610
  19.6 4.3 %collective-permute-start.3 = (bf16[200,16,128]{2,1,0:T(8,128)(2,1)S(1)}, bf16[200,16,128]{2,1,0:T(8,128)(2,1)}, u32[]{:S(2)}, u32[]{:S(2)}) collective-permute-start(bf16[200,16,128]{2,1,0:T(8,128)(2,1)S(1)} %all_gather.3.own_ref), channel_id=1, source_target_pairs={{0,8},{8,0},{16,24},{24,16},{1,9},{9,1},{17,25},{25,17},{2,10},{10... | collective-permute-start | bytes 2457608 | tf_op jit(solution)/shard_map/ppermute | solution.py:49
  24.0 1.5 %collective-permute-start.2 = (bf16[200,16,128]{2,1,0:T(8,128)(2,1)S(1)}, bf16[200,16,128]{2,1,0:T(8,128)(2,1)}, u32[]{:S(2)}, u32[]{:S(2)}) collective-permute-start(bf16[200,16,128]{2,1,0:T(8,128)(2,1)S(1)} %all_gather.3.own_ref), channel_id=1, source_target_pairs={{0,0},{8,16},{16,8},{24,24},{1,1},{9,17},{17,9},{25,25},{2,2},{10,... | collective-permute-start | bytes 2457608 | tf_op jit(solution)/shard_map/ppermute | solution.py:49
  25.5 0.0 collective-permute-done.1.after_ref
  25.5 0.0 collective-permute-done.before_ref
  25.5 6.1 %shard_map.124 = (bf16[1344,128]{1,0:T(8,128)(2,1)}, bf16[1344,128]{1,0:T(8,128)(2,1)}) custom-call(s32[24,128]{1,0:T(8,128)S(1)} %get-tuple-element.26.info_ref, bf16[48,7,128,128]{3,2,1,0:T(8,128)(2,1)} %blocks_ref.5, bf16[48,64,128]{2,1,0:T(8,128)(2,1)S(1)} %collective-permute-done.before_ref, bf16[48,64,128]{2,1,0:T(8,128)(2,1)S(1)} %shard_map.122.rest_8_.own_ref, ...), custom_call_target="tpu_custom_call" | custom-call | tf_op jit(solution)/shard_map/pallas_call | solution.py:271
  31.6 1.5 %collective-permute-start.6 = (bf16[1344,128]{1,0:T(8,128)(2,1)}, bf16[1344,128]{1,0:T(8,128)(2,1)}, u32[]{:S(2)}, u32[]{:S(2)}) collective-permute-start(bf16[1344,128]{1,0:T(8,128)(2,1)} %get-tuple-element.31), channel_id=1, source_target_pairs={{0,6},{1,7},{2,4},{3,5},{4,2},{5,3},{6,0},{7,1},{8,14},{9,15},{10,... | collective-permute-start | bytes 1032200 | tf_op jit(solution)/shard_map/ppermute | solution.py:39
  33.2 0.9 %collective-permute-start.5 = (bf16[1344,128]{1,0:T(8,128)(2,1)}, bf16[1344,128]{1,0:T(8,128)(2,1)}, u32[]{:S(2)}, u32[]{:S(2)}) collective-permute-start(bf16[1344,128]{1,0:T(8,128)(2,1)} %get-tuple-element.27.rest_0_), channel_id=1, source_target_pairs={{0,7},{1,6},{2,5},{3,4},{4,3},{5,2},{6,1},{7,0},{8,15},{9,14},{10,... | collective-permute-start | bytes 1032200 | tf_op jit(solution)/shard_map/ppermute | solution.py:39
  34.0 5.4 %shard_map.125 = (bf16[1344,128]{1,0:T(8,128)(2,1)S(1)}, bf16[1344,128]{1,0:T(8,128)(2,1)S(1)}) custom-call(s32[24,128]{1,0:T(8,128)S(1)} %get-tuple-element.26.info_ref, bf16[48,7,128,128]{3,2,1,0:T(8,128)(2,1)} %blocks_ref.5, bf16[48,64,128]{2,1,0:T(8,128)(2,1)S(1)} %collective-permute-done.before_ref, ...), custom_call_target="tpu_custom_call" | custom-call | tf_op jit(solution)/shard_map/pallas_call | solution.py:271
  39.4 1.9 %collective-permute-start.8 = (bf16[1344,128]{1,0:T(8,128)(2,1)S(1)}, bf16[1344,128]{1,0:T(8,128)(2,1)S(1)}, u32[]{:S(2)}, u32[]{:S(2)}) collective-permute-start(bf16[1344,128]{1,0:T(8,128)(2,1)S(1)} %get-tuple-element.32), channel_id=1, source_target_pairs={{0,3},{1,2},{2,1},{3,0},{4,7},{5,6},{6,5},{7,4},{8,11},{9,10},{10,... | collective-permute-start | bytes 1032200 | tf_op jit(solution)/shard_map/ppermute | solution.py:39
  41.3 1.5 %collective-permute-done.3.rest_2_.second_ref = bf16[200,16,128]{2,1,0:T(8,128)(2,1)} collective-permute-done((bf16[200,16,128]{2,1,0:T(8,128)(2,1)S(1)}, bf16[200,16,128]{2,1,0:T(8,128)(2,1)}, u32[]{:S(2)}, u32[]{:S(2)}) %collective-permute-start.3) | collective-permute-done | bytes 819232 | tf_op jit(solution)/shard_map/ppermute | solution.py:49
  42.8 0.9 %collective-permute-start.7 = (bf16[1344,128]{1,0:T(8,128)(2,1)S(1)}, bf16[1344,128]{1,0:T(8,128)(2,1)S(1)}, u32[]{:S(2)}, u32[]{:S(2)}) collective-permute-start(bf16[1344,128]{1,0:T(8,128)(2,1)S(1)} %get-tuple-element.28.rest_0_), channel_id=1, source_target_pairs={{0,5},{1,4},{2,7},{3,6},{4,1},{5,0},{6,3},{7,2},{8,13},{9,12},{10,... | collective-permute-start | bytes 1032200 | tf_op jit(solution)/shard_map/ppermute | solution.py:39
  43.7 0.0 collective-permute-done.2.rest_1_.first_ref
  43.7 8.6 %shard_map.126 = (bf16[1344,128]{1,0:T(8,128)(2,1)S(1)}, bf16[1344,128]{1,0:T(8,128)(2,1)S(1)}, bf16[1344,128]{1,0:T(8,128)(2,1)S(1)}, bf16[1344,128]{1,0:T(8,128)(2,1)S(1)}) custom-call(s32[24,128]{1,0:T(8,128)S(1)} %get-tuple-element.26.info_ref, bf16[48,7,128,128]{3,2,1,0:T(8,128)(2,1)} %blocks_ref.5, ...), custom_call_target="tpu_custom_call" | custom-call | tf_op jit(solution)/shard_map/pallas_call | solution.py:271
  52.3 0.8 collective-permute-start.4
  53.1 0.0 collective-permute-done.6.rest_3_
  53.1 0.5 collective-permute-start.9
  53.6 0.0 collective-permute-done.5.rest_2_
  53.6 1.5 %collective-permute-start.10 = (bf16[1344,128]{1,0:T(8,128)(2,1)S(1)}, bf16[1344,128]{1,0:T(8,128)(2,1)S(1)}, u32[]{:S(2)}, u32[]{:S(2)}) collective-permute-start(bf16[1344,128]{1,0:T(8,128)(2,1)S(1)} %get-tuple-element.33.waited_ref), channel_id=1, source_target_pairs={{0,4},{1,5},{2,6},{3,7},{4,0},{5,1},{6,2},{7,3},{8,12},{9,13},{10,... | collective-permute-start | bytes 1032200 | tf_op jit(solution)/shard_map/ppermute | solution.py:39
  55.2 2.8 %shard_map.127 = (bf16[168,16,128]{2,1,0:T(8,128)(2,1)S(1)}, bf16[24,32,64]{2,1,0:T(8,128)(2,1)S(1)}) custom-call(s32[7,24]{1,0:T(8,128)S(1)} %fusion.4.index_ref, bf16[200,16,128]{2,1,0:T(8,128)(2,1)} %collective-permute-done.2.rest_1_.first_ref, bf16[200,16,128]{2,1,0:T(8,128)(2,1)S(1)} %all_gather.3.own_ref, ...), custom_call_target="tpu_custom_call" | custom-call | tf_op jit(solution)/shard_map/pallas_call | solution.py:337
  58.0 0.0 collective-permute-done.8.rest_5_
  58.0 0.0 collective-permute-done.7.rest_4_
  58.0 0.0 collective-permute-done.4.rest_0_
  58.0 4.2 %shard_map.128 = (f32[169,32,128]{2,1,0:T(8,128)S(1)}, s32[276]{0:T(512)S(1)}) custom-call(s32[2]{0:T(128)S(1)} %pad_add_fusion.where_ref, s32[128,128]{1,0:T(8,128)S(1)} %bitcast_convert_fusion.table_ref, bf16[1344,128]{1,0:T(8,128)(2,1)S(1)} %collective-permute-done.4.rest_0_, bf16[1344,128]{1,0:T(8,128)(2,1)S(1)} %get-tuple-element.30.rest_1_, ...), custom_call_target="tpu_custom_call" | custom-call | tf_op jit(solution)/shard_map/pallas_call | solution.py:395
  62.2 2.8 %collective-permute-done.9.rest_0_ = bf16[1344,128]{1,0:T(8,128)(2,1)S(1)} collective-permute-done((bf16[1344,128]{1,0:T(8,128)(2,1)S(1)}, bf16[1344,128]{1,0:T(8,128)(2,1)S(1)}, u32[]{:S(2)}, u32[]{:S(2)}) %collective-permute-start.9) | collective-permute-done | bytes 344096 | tf_op jit(solution)/shard_map/ppermute | solution.py:39
  65.0 0.0 collective-permute-done.10.rest_1_
  65.0 3.5 %shard_map.129 = (bf16[168,32,128]{2,1,0:T(8,128)(2,1)S(1)}, f32[169,32,128]{2,1,0:T(8,128)S(1)}, bf16[168,128]{1,0:T(8,128)(2,1)S(1)}, bf16[168,128]{1,0:T(8,12...) custom-call(s32[276]{0:T(512)S(1)} %get-tuple-element.35.lists_ref, ...), custom_call_target="tpu_custom_call", output_to_operand_aliasing={{1}: (3, {})} | custom-call | tf_op jit(solution)/shard_map/pallas_call | solution.py:492
  68.6 1.2 %collective-permute-start.11 = (bf16[168,128]{1,0:T(8,128)(2,1)S(1)}, bf16[168,128]{1,0:T(8,128)(2,1)S(1)}, u32[]{:S(2)}, u32[]{:S(2)}) collective-permute-start(bf16[168,128]{1,0:T(8,128)(2,1)S(1)} %get-tuple-element.40), channel_id=1, source_target_pairs={{0,7},{1,6},{2,5},{3,4},{4,3},{5,2},{6,1},{7,0},{8,15},{9,14},{10,... | collective-permute-start | bytes 129032 | tf_op jit(solution)/shard_map/ppermute | solution.py:39
  69.7 1.5 %collective-permute-start.12 = (bf16[168,128]{1,0:T(8,128)(2,1)S(1)}, bf16[168,128]{1,0:T(8,128)(2,1)S(1)}, u32[]{:S(2)}, u32[]{:S(2)}) collective-permute-start(bf16[168,128]{1,0:T(8,128)(2,1)S(1)} %get-tuple-element.41), channel_id=1, source_target_pairs={{0,6},{1,7},{2,4},{3,5},{4,2},{5,3},{6,0},{7,1},{8,14},{9,15},{10,... | collective-permute-start | bytes 129032 | tf_op jit(solution)/shard_map/ppermute | solution.py:39
  71.2 1.2 %collective-permute-start.13 = (bf16[168,128]{1,0:T(8,128)(2,1)S(1)}, bf16[168,128]{1,0:T(8,128)(2,1)S(1)}, u32[]{:S(2)}, u32[]{:S(2)}) collective-permute-start(bf16[168,128]{1,0:T(8,128)(2,1)S(1)} %get-tuple-element.42), channel_id=1, source_target_pairs={{0,5},{1,4},{2,7},{3,6},{4,1},{5,0},{6,3},{7,2},{8,13},{9,12},{10,... | collective-permute-start | bytes 129032 | tf_op jit(solution)/shard_map/ppermute | solution.py:39
  72.4 0.6 collective-permute-start.14
  73.0 1.1 %collective-permute-start.15 = (bf16[168,128]{1,0:T(8,128)(2,1)S(1)}, bf16[168,128]{1,0:T(8,128)(2,1)S(1)}, u32[]{:S(2)}, u32[]{:S(2)}) collective-permute-start(bf16[168,128]{1,0:T(8,128)(2,1)S(1)} %get-tuple-element.44), channel_id=1, source_target_pairs={{0,3},{1,2},{2,1},{3,0},{4,7},{5,6},{6,5},{7,4},{8,11},{9,10},{10,... | collective-permute-start | bytes 129032 | tf_op jit(solution)/shard_map/ppermute | solution.py:39
  74.2 0.0 collective-permute-done.11.rest_0_
  74.2 0.5 collective-permute-start.16
  74.7 0.0 collective-permute-done.12.rest_1_
  74.7 0.2 collective-permute-start.17
  74.9 1.7 %reshape.21 = bf16[7,24,4096]{2,1,0:T(8,128)(2,1)} reshape(bf16[168,32,128]{2,1,0:T(8,128)(2,1)S(1)} %get-tuple-element.39) | data formatting | bytes 2752512 | tf_op jit(solution)/shard_map/reshape | solution.py:660
  76.6 0.0 collective-permute-done.13.rest_2_
  76.6 0.0 collective-permute-done.14.rest_3_
  76.6 0.2 collective-permute-done.15.rest_4_
  76.7 1.5 %collective-permute-done.16.rest_5_ = bf16[168,128]{1,0:T(8,128)(2,1)S(1)} collective-permute-done((bf16[168,128]{1,0:T(8,128)(2,1)S(1)}, bf16[168,128]{1,0:T(8,128)(2,1)S(1)}, u32[]{:S(2)}, u32[]{:S(2)}) %collective-permute-start.16) | collective-permute-done | bytes 43040 | tf_op jit(solution)/shard_map/ppermute | solution.py:39
  78.2 0.0 collective-permute-done.17.rest_6_
  78.2 2.1 %shard_map.130 = bf16[12,7,1024]{2,1,0:T(8,128)(2,1)} custom-call(s32[276]{0:T(512)S(1)} %get-tuple-element.35.lists_ref, bf16[168,128]{1,0:T(8,128)(2,1)S(1)} %collective-permute-done.11.rest_0_, bf16[168,128]{1,0:T(8,128)(2,1)S(1)} %collective-permute-done.12.rest_1_, bf16[168,128]{1,0:T(8,128)(2,1)S(1)} %collective-permute-done.13.rest_2_, ...), custom_call_target="tpu_custom_call" | custom-call | tf_op jit(solution)/shard_map/pallas_call | solution.py:539
  (5 shorter events, 0.1 us)
Async XLA Ops:
  3.2 22.3 %collective-permute-start.1 = (bf16[48,64,128]{2,1,0:T(8,128)(2,1)S(1)}, bf16[48,64,128]{2,1,0:T(8,128)(2,1)S(1)}, u32[]{:S(2)}, u32[]{:S(2)}) collective-permute-start(bf16[48,64,128]{2,1,0:T(8,128)(2,1)S(1)} %shard_map.122.rest_8_.own_ref), channel_id=1, source_target_pairs={{0,8},{8,0},{16,24},{24,16},{1,9},{9,1},{17,25},{25,17},{2,10},{10... | collective-permute-start | bytes 2359304 | tf_op jit(solution)/shard_map/ppermute | solution.py:49
  6.3 19.2 %collective-permute-start = (bf16[48,64,128]{2,1,0:T(8,128)(2,1)S(1)}, bf16[48,64,128]{2,1,0:T(8,128)(2,1)S(1)}, u32[]{:S(2)}, u32[]{:S(2)}) collective-permute-start(bf16[48,64,128]{2,1,0:T(8,128)(2,1)S(1)} %shard_map.122.rest_8_.own_ref), channel_id=1, source_target_pairs={{0,0},{8,16},{16,8},{24,24},{1,1},{9,17},{17,9},{25,25},{2,2},{10,... | collective-permute-start | bytes 2359304 | tf_op jit(solution)/shard_map/ppermute | solution.py:49
  19.6 23.2 %collective-permute-start.3 = (bf16[200,16,128]{2,1,0:T(8,128)(2,1)S(1)}, bf16[200,16,128]{2,1,0:T(8,128)(2,1)}, u32[]{:S(2)}, u32[]{:S(2)}) collective-permute-start(bf16[200,16,128]{2,1,0:T(8,128)(2,1)S(1)} %all_gather.3.own_ref), channel_id=1, source_target_pairs={{0,8},{8,0},{16,24},{24,16},{1,9},{9,1},{17,25},{25,17},{2,10},{10... | collective-permute-start | bytes 2457608 | tf_op jit(solution)/shard_map/ppermute | solution.py:49
  24.0 19.7 %collective-permute-start.2 = (bf16[200,16,128]{2,1,0:T(8,128)(2,1)S(1)}, bf16[200,16,128]{2,1,0:T(8,128)(2,1)}, u32[]{:S(2)}, u32[]{:S(2)}) collective-permute-start(bf16[200,16,128]{2,1,0:T(8,128)(2,1)S(1)} %all_gather.3.own_ref), channel_id=1, source_target_pairs={{0,0},{8,16},{16,8},{24,24},{1,1},{9,17},{17,9},{25,25},{2,2},{10,... | collective-permute-start | bytes 2457608 | tf_op jit(solution)/shard_map/ppermute | solution.py:49
  31.6 21.4 %collective-permute-start.6 = (bf16[1344,128]{1,0:T(8,128)(2,1)}, bf16[1344,128]{1,0:T(8,128)(2,1)}, u32[]{:S(2)}, u32[]{:S(2)}) collective-permute-start(bf16[1344,128]{1,0:T(8,128)(2,1)} %get-tuple-element.31), channel_id=1, source_target_pairs={{0,6},{1,7},{2,4},{3,5},{4,2},{5,3},{6,0},{7,1},{8,14},{9,15},{10,... | collective-permute-start | bytes 1032200 | tf_op jit(solution)/shard_map/ppermute | solution.py:39
  33.2 20.4 %collective-permute-start.5 = (bf16[1344,128]{1,0:T(8,128)(2,1)}, bf16[1344,128]{1,0:T(8,128)(2,1)}, u32[]{:S(2)}, u32[]{:S(2)}) collective-permute-start(bf16[1344,128]{1,0:T(8,128)(2,1)} %get-tuple-element.27.rest_0_), channel_id=1, source_target_pairs={{0,7},{1,6},{2,5},{3,4},{4,3},{5,2},{6,1},{7,0},{8,15},{9,14},{10,... | collective-permute-start | bytes 1032200 | tf_op jit(solution)/shard_map/ppermute | solution.py:39
  39.4 18.6 %collective-permute-start.8 = (bf16[1344,128]{1,0:T(8,128)(2,1)S(1)}, bf16[1344,128]{1,0:T(8,128)(2,1)S(1)}, u32[]{:S(2)}, u32[]{:S(2)}) collective-permute-start(bf16[1344,128]{1,0:T(8,128)(2,1)S(1)} %get-tuple-element.32), channel_id=1, source_target_pairs={{0,3},{1,2},{2,1},{3,0},{4,7},{5,6},{6,5},{7,4},{8,11},{9,10},{10,... | collective-permute-start | bytes 1032200 | tf_op jit(solution)/shard_map/ppermute | solution.py:39
  42.8 12.3 %copy-start = (s32[24,7]{0,1:T(8,128)S(1)}, s32[24,7]{0,1:T(8,128)}, u32[]{:S(2)}) copy-start(s32[24,7]{0,1:T(8,128)} %param.18) | copy-start | bytes 2020
  42.8 15.2 %collective-permute-start.7 = (bf16[1344,128]{1,0:T(8,128)(2,1)S(1)}, bf16[1344,128]{1,0:T(8,128)(2,1)S(1)}, u32[]{:S(2)}, u32[]{:S(2)}) collective-permute-start(bf16[1344,128]{1,0:T(8,128)(2,1)S(1)} %get-tuple-element.28.rest_0_), channel_id=1, source_target_pairs={{0,5},{1,4},{2,7},{3,6},{4,1},{5,0},{6,3},{7,2},{8,13},{9,12},{10,... | collective-permute-start | bytes 1032200 | tf_op jit(solution)/shard_map/ppermute | solution.py:39
  52.3 5.8 %collective-permute-start.4 = (bf16[1344,128]{1,0:T(8,128)(2,1)S(1)}, bf16[1344,128]{1,0:T(8,128)(2,1)S(1)}, u32[]{:S(2)}, u32[]{:S(2)}) collective-permute-start(bf16[1344,128]{1,0:T(8,128)(2,1)S(1)} %get-tuple-element.29), channel_id=1, source_target_pairs={{0,1},{1,0},{2,3},{3,2},{4,5},{5,4},{6,7},{7,6},{8,9},{9,8},{10,11... | collective-permute-start | bytes 1032200 | tf_op jit(solution)/shard_map/ppermute | solution.py:39
  53.1 12.0 %collective-permute-start.9 = (bf16[1344,128]{1,0:T(8,128)(2,1)S(1)}, bf16[1344,128]{1,0:T(8,128)(2,1)S(1)}, u32[]{:S(2)}, u32[]{:S(2)}) collective-permute-start(bf16[1344,128]{1,0:T(8,128)(2,1)S(1)} %get-tuple-element.38), channel_id=1, source_target_pairs={{0,2},{1,3},{2,0},{3,1},{4,6},{5,7},{6,4},{7,5},{8,10},{9,11},{10,... | collective-permute-start | bytes 1032200 | tf_op jit(solution)/shard_map/ppermute | solution.py:39
  53.6 11.4 %collective-permute-start.10 = (bf16[1344,128]{1,0:T(8,128)(2,1)S(1)}, bf16[1344,128]{1,0:T(8,128)(2,1)S(1)}, u32[]{:S(2)}, u32[]{:S(2)}) collective-permute-start(bf16[1344,128]{1,0:T(8,128)(2,1)S(1)} %get-tuple-element.33.waited_ref), channel_id=1, source_target_pairs={{0,4},{1,5},{2,6},{3,7},{4,0},{5,1},{6,2},{7,3},{8,12},{9,13},{10,... | collective-permute-start | bytes 1032200 | tf_op jit(solution)/shard_map/ppermute | solution.py:39
  68.6 5.6 %collective-permute-start.11 = (bf16[168,128]{1,0:T(8,128)(2,1)S(1)}, bf16[168,128]{1,0:T(8,128)(2,1)S(1)}, u32[]{:S(2)}, u32[]{:S(2)}) collective-permute-start(bf16[168,128]{1,0:T(8,128)(2,1)S(1)} %get-tuple-element.40), channel_id=1, source_target_pairs={{0,7},{1,6},{2,5},{3,4},{4,3},{5,2},{6,1},{7,0},{8,15},{9,14},{10,... | collective-permute-start | bytes 129032 | tf_op jit(solution)/shard_map/ppermute | solution.py:39
  69.7 5.0 %collective-permute-start.12 = (bf16[168,128]{1,0:T(8,128)(2,1)S(1)}, bf16[168,128]{1,0:T(8,128)(2,1)S(1)}, u32[]{:S(2)}, u32[]{:S(2)}) collective-permute-start(bf16[168,128]{1,0:T(8,128)(2,1)S(1)} %get-tuple-element.41), channel_id=1, source_target_pairs={{0,6},{1,7},{2,4},{3,5},{4,2},{5,3},{6,0},{7,1},{8,14},{9,15},{10,... | collective-permute-start | bytes 129032 | tf_op jit(solution)/shard_map/ppermute | solution.py:39
  71.2 5.3 %collective-permute-start.13 = (bf16[168,128]{1,0:T(8,128)(2,1)S(1)}, bf16[168,128]{1,0:T(8,128)(2,1)S(1)}, u32[]{:S(2)}, u32[]{:S(2)}) collective-permute-start(bf16[168,128]{1,0:T(8,128)(2,1)S(1)} %get-tuple-element.42), channel_id=1, source_target_pairs={{0,5},{1,4},{2,7},{3,6},{4,1},{5,0},{6,3},{7,2},{8,13},{9,12},{10,... | collective-permute-start | bytes 129032 | tf_op jit(solution)/shard_map/ppermute | solution.py:39
  72.4 4.1 %collective-permute-start.14 = (bf16[168,128]{1,0:T(8,128)(2,1)S(1)}, bf16[168,128]{1,0:T(8,128)(2,1)S(1)}, u32[]{:S(2)}, u32[]{:S(2)}) collective-permute-start(bf16[168,128]{1,0:T(8,128)(2,1)S(1)} %get-tuple-element.43), channel_id=1, source_target_pairs={{0,4},{1,5},{2,6},{3,7},{4,0},{5,1},{6,2},{7,3},{8,12},{9,13},{10,... | collective-permute-start | bytes 129032 | tf_op jit(solution)/shard_map/ppermute | solution.py:39
  73.0 3.7 %collective-permute-start.15 = (bf16[168,128]{1,0:T(8,128)(2,1)S(1)}, bf16[168,128]{1,0:T(8,128)(2,1)S(1)}, u32[]{:S(2)}, u32[]{:S(2)}) collective-permute-start(bf16[168,128]{1,0:T(8,128)(2,1)S(1)} %get-tuple-element.44), channel_id=1, source_target_pairs={{0,3},{1,2},{2,1},{3,0},{4,7},{5,6},{6,5},{7,4},{8,11},{9,10},{10,... | collective-permute-start | bytes 129032 | tf_op jit(solution)/shard_map/ppermute | solution.py:39
  74.2 4.0 %collective-permute-start.16 = (bf16[168,128]{1,0:T(8,128)(2,1)S(1)}, bf16[168,128]{1,0:T(8,128)(2,1)S(1)}, u32[]{:S(2)}, u32[]{:S(2)}) collective-permute-start(bf16[168,128]{1,0:T(8,128)(2,1)S(1)} %get-tuple-element.45), channel_id=1, source_target_pairs={{0,2},{1,3},{2,0},{3,1},{4,6},{5,7},{6,4},{7,5},{8,10},{9,11},{10,... | collective-permute-start | bytes 129032 | tf_op jit(solution)/shard_map/ppermute | solution.py:39
  74.7 3.5 %collective-permute-start.17 = (bf16[168,128]{1,0:T(8,128)(2,1)S(1)}, bf16[168,128]{1,0:T(8,128)(2,1)S(1)}, u32[]{:S(2)}, u32[]{:S(2)}) collective-permute-start(bf16[168,128]{1,0:T(8,128)(2,1)S(1)} %get-tuple-element.46), channel_id=1, source_target_pairs={{0,1},{1,0},{2,3},{3,2},{4,5},{5,4},{6,7},{7,6},{8,9},{9,8},{10,11... | collective-permute-start | bytes 129032 | tf_op jit(solution)/shard_map/ppermute | solution.py:39

commit v7 on v6

--- a/solution.py
+++ b/solution.py
@@ -434,7 +434,7 @@
     block = lax.broadcasted_iota(I32, (16, LANES), 1) // quarter
     none = jnp.zeros((16, LANES), BF16)
 
-    batch = 2
+    batch = 4
 
     def second(step, carry):
         places = [(step * batch + n, r) for n in range(batch) for r in range(capacity2)]

time: 80.7 us -> 80.1 us (level)
  transfers between devices with their start and end apart: 18 -> 18, of which waited for: 4 -> 5; matrix products, arithmetic and copies ran while one was open for 2% -> 2% of each run, Pallas kernels for 36% -> 36%
where the time goes in v7:
time: 80.1 us; the launch traced here: 79.8 us
  Pallas kernels  36.7 us (46%)
  starting transfers between devices  23.9 us (30%)
  blocking collectives  10.6 us (13%)
  waiting for transfers between devices  6.12 us (8%)
  local copies, waits for them, and re-layouts  1.66 us (2%)
    pallas_call x3, Pallas kernels, level_one(): pl.pallas_call(functools.partial(terms_kernel, offsets=offsets, capacity=...  20.1 us
    ppermute x14, starting transfers between devices, exchange(): return lax.ppermute(cells, axis, [(i, i ^ offset) for i in range(count)])  14.2 us
    all_gather x1, blocking collectives, local(): table = lax.all_gather(stacked, 'dom', axis=0, tiled=True)  10.6 us
    ppermute x4, starting transfers between devices, neighbours(): lax.ppermute(cells, axis, [(i, partner(i, odd, count)) for i in range(cou...  9.68 us
    ppermute x14, waiting for transfers between devices, exchange(): return lax.ppermute(cells, axis, [(i, i ^ offset) for i in range(count)])  4.57 us
    pallas_call x1, Pallas kernels, early_sums(): pl.pallas_call(functools.partial(early_kernel, soon=soon, late=late, **si...  4.16 us
    pallas_call x1, Pallas kernels, owner_level(): pl.pallas_call(functools.partial(owner_kernel, parts=parts, offsets=offse...  2.97 us
    pallas_call x1, Pallas kernels, pick_rows(): pl.pallas_call(pick_kernel, out_shape=(jax.ShapeDtypeStruct((count * sten...  2.83 us
  transfers between devices with their start and end apart: 18, of which 5 were waited for; matrix products, arithmetic and copies ran while one was open for 2% of the time, Pallas kernels for 36%

profile of v7, /device:TPU:0, one launch (start us, length us, event | category | flops | bytes accessed | tf_op | source)
XLA Modules:
  0.0 79.8 jit_solution(3384410025771432904)
XLA Ops:
  0.6 2.6 %shard_map.122.rest_8_.own_ref = bf16[48,64,128]{2,1,0:T(8,128)(2,1)S(1)} custom-call(bf16[48,8192]{1,0:T(8,128)(2,1)} %flat_ref.1), custom_call_target="tpu_custom_call" | custom-call | tf_op jit(solution)/shard_map/pallas_call | solution.py:86
  3.2 3.1 %collective-permute-start.1 = (bf16[48,64,128]{2,1,0:T(8,128)(2,1)S(1)}, bf16[48,64,128]{2,1,0:T(8,128)(2,1)S(1)}, u32[]{:S(2)}, u32[]{:S(2)}) collective-permute-start(bf16[48,64,128]{2,1,0:T(8,128)(2,1)S(1)} %shard_map.122.rest_8_.own_ref), channel_id=1, source_target_pairs={{0,8},{8,0},{16,24},{24,16},{1,9},{9,1},{17,25},{25,17},{2,10},{10... | collective-permute-start | bytes 2359304 | tf_op jit(solution)/shard_map/ppermute | solution.py:49
  6.3 0.7 collective-permute-start
  7.0 0.1 pad_add_fusion.where_ref
  7.1 2.0 %shard_map.123 = (s32[24,128]{1,0:T(8,128)S(1)}, bf16[25,16,128]{2,1,0:T(8,128)(2,1)S(1)}) custom-call(s32[2]{0:T(128)S(1)} %pad_add_fusion.where_ref, s32[7,48]{1,0:T(8,128)} %bitcast.20, s32[7,48]{1,0:T(8,128)} %bitcast.21, s32[1,48]{1,0:T(1,128)} %bitcast.23, s32[1,48]{1,0:T(1,128)} %bitcast.24, s32[7,24]{1,0:T(8,128)} %bitcast.22, s32[1,24]{1,0:T(1,128)} %bitcast.25, ...), custom_call_target="tpu_custom_call" | custom-call | tf_op jit(solution)/shard_map/pallas_call | solution.py:594
  9.1 10.6 %all_gather.3.own_ref = bf16[200,16,128]{2,1,0:T(8,128)(2,1)S(1)} all-gather(bf16[25,16,128]{2,1,0:T(8,128)(2,1)S(1)} %get-tuple-element.25.mine_ref), channel_id=1, replica_groups=mesh['region'=4,'dom'=8] {'dom'}, dimensions={0}, use_global_device_ids=true | all-gather | bytes 921600 | tf_op jit(solution)/shard_map/all_gather | solution.py:610
  19.6 4.3 %collective-permute-start.3 = (bf16[200,16,128]{2,1,0:T(8,128)(2,1)S(1)}, bf16[200,16,128]{2,1,0:T(8,128)(2,1)}, u32[]{:S(2)}, u32[]{:S(2)}) collective-permute-start(bf16[200,16,128]{2,1,0:T(8,128)(2,1)S(1)} %all_gather.3.own_ref), channel_id=1, source_target_pairs={{0,8},{8,0},{16,24},{24,16},{1,9},{9,1},{17,25},{25,17},{2,10},{10... | collective-permute-start | bytes 2457608 | tf_op jit(solution)/shard_map/ppermute | solution.py:49
  24.0 1.5 %collective-permute-start.2 = (bf16[200,16,128]{2,1,0:T(8,128)(2,1)S(1)}, bf16[200,16,128]{2,1,0:T(8,128)(2,1)}, u32[]{:S(2)}, u32[]{:S(2)}) collective-permute-start(bf16[200,16,128]{2,1,0:T(8,128)(2,1)S(1)} %all_gather.3.own_ref), channel_id=1, source_target_pairs={{0,0},{8,16},{16,8},{24,24},{1,1},{9,17},{17,9},{25,25},{2,2},{10,... | collective-permute-start | bytes 2457608 | tf_op jit(solution)/shard_map/ppermute | solution.py:49
  25.5 0.0 collective-permute-done.1.after_ref
  25.5 0.0 collective-permute-done.before_ref
  25.5 6.1 %shard_map.124 = (bf16[1344,128]{1,0:T(8,128)(2,1)}, bf16[1344,128]{1,0:T(8,128)(2,1)}) custom-call(s32[24,128]{1,0:T(8,128)S(1)} %get-tuple-element.26.info_ref, bf16[48,7,128,128]{3,2,1,0:T(8,128)(2,1)} %blocks_ref.5, bf16[48,64,128]{2,1,0:T(8,128)(2,1)S(1)} %collective-permute-done.before_ref, bf16[48,64,128]{2,1,0:T(8,128)(2,1)S(1)} %shard_map.122.rest_8_.own_ref, ...), custom_call_target="tpu_custom_call" | custom-call | tf_op jit(solution)/shard_map/pallas_call | solution.py:271
  31.6 1.5 %collective-permute-start.6 = (bf16[1344,128]{1,0:T(8,128)(2,1)}, bf16[1344,128]{1,0:T(8,128)(2,1)}, u32[]{:S(2)}, u32[]{:S(2)}) collective-permute-start(bf16[1344,128]{1,0:T(8,128)(2,1)} %get-tuple-element.31), channel_id=1, source_target_pairs={{0,6},{1,7},{2,4},{3,5},{4,2},{5,3},{6,0},{7,1},{8,14},{9,15},{10,... | collective-permute-start | bytes 1032200 | tf_op jit(solution)/shard_map/ppermute | solution.py:39
  33.2 0.9 %collective-permute-start.5 = (bf16[1344,128]{1,0:T(8,128)(2,1)}, bf16[1344,128]{1,0:T(8,128)(2,1)}, u32[]{:S(2)}, u32[]{:S(2)}) collective-permute-start(bf16[1344,128]{1,0:T(8,128)(2,1)} %get-tuple-element.27.rest_0_), channel_id=1, source_target_pairs={{0,7},{1,6},{2,5},{3,4},{4,3},{5,2},{6,1},{7,0},{8,15},{9,14},{10,... | collective-permute-start | bytes 1032200 | tf_op jit(solution)/shard_map/ppermute | solution.py:39
  34.0 5.4 %shard_map.125 = (bf16[1344,128]{1,0:T(8,128)(2,1)S(1)}, bf16[1344,128]{1,0:T(8,128)(2,1)S(1)}) custom-call(s32[24,128]{1,0:T(8,128)S(1)} %get-tuple-element.26.info_ref, bf16[48,7,128,128]{3,2,1,0:T(8,128)(2,1)} %blocks_ref.5, bf16[48,64,128]{2,1,0:T(8,128)(2,1)S(1)} %collective-permute-done.before_ref, ...), custom_call_target="tpu_custom_call" | custom-call | tf_op jit(solution)/shard_map/pallas_call | solution.py:271
  39.4 1.9 %collective-permute-start.8 = (bf16[1344,128]{1,0:T(8,128)(2,1)S(1)}, bf16[1344,128]{1,0:T(8,128)(2,1)S(1)}, u32[]{:S(2)}, u32[]{:S(2)}) collective-permute-start(bf16[1344,128]{1,0:T(8,128)(2,1)S(1)} %get-tuple-element.32), channel_id=1, source_target_pairs={{0,3},{1,2},{2,1},{3,0},{4,7},{5,6},{6,5},{7,4},{8,11},{9,10},{10,... | collective-permute-start | bytes 1032200 | tf_op jit(solution)/shard_map/ppermute | solution.py:39
  41.3 1.5 %collective-permute-done.3.rest_2_.second_ref = bf16[200,16,128]{2,1,0:T(8,128)(2,1)} collective-permute-done((bf16[200,16,128]{2,1,0:T(8,128)(2,1)S(1)}, bf16[200,16,128]{2,1,0:T(8,128)(2,1)}, u32[]{:S(2)}, u32[]{:S(2)}) %collective-permute-start.3) | collective-permute-done | bytes 819232 | tf_op jit(solution)/shard_map/ppermute | solution.py:49
  42.8 0.9 %collective-permute-start.7 = (bf16[1344,128]{1,0:T(8,128)(2,1)S(1)}, bf16[1344,128]{1,0:T(8,128)(2,1)S(1)}, u32[]{:S(2)}, u32[]{:S(2)}) collective-permute-start(bf16[1344,128]{1,0:T(8,128)(2,1)S(1)} %get-tuple-element.28.rest_0_), channel_id=1, source_target_pairs={{0,5},{1,4},{2,7},{3,6},{4,1},{5,0},{6,3},{7,2},{8,13},{9,12},{10,... | collective-permute-start | bytes 1032200 | tf_op jit(solution)/shard_map/ppermute | solution.py:39
  43.7 0.0 collective-permute-done.2.rest_1_.first_ref
  43.7 8.6 %shard_map.126 = (bf16[1344,128]{1,0:T(8,128)(2,1)S(1)}, bf16[1344,128]{1,0:T(8,128)(2,1)S(1)}, bf16[1344,128]{1,0:T(8,128)(2,1)S(1)}, bf16[1344,128]{1,0:T(8,128)(2,1)S(1)}) custom-call(s32[24,128]{1,0:T(8,128)S(1)} %get-tuple-element.26.info_ref, bf16[48,7,128,128]{3,2,1,0:T(8,128)(2,1)} %blocks_ref.5, ...), custom_call_target="tpu_custom_call" | custom-call | tf_op jit(solution)/shard_map/pallas_call | solution.py:271
  52.3 0.8 %collective-permute-start.4 = (bf16[1344,128]{1,0:T(8,128)(2,1)S(1)}, bf16[1344,128]{1,0:T(8,128)(2,1)S(1)}, u32[]{:S(2)}, u32[]{:S(2)}) collective-permute-start(bf16[1344,128]{1,0:T(8,128)(2,1)S(1)} %get-tuple-element.29), channel_id=1, source_target_pairs={{0,1},{1,0},{2,3},{3,2},{4,5},{5,4},{6,7},{7,6},{8,9},{9,8},{10,11... | collective-permute-start | bytes 1032200 | tf_op jit(solution)/shard_map/ppermute | solution.py:39
  53.1 0.0 collective-permute-done.6.rest_3_
  53.1 0.5 collective-permute-start.9
  53.6 0.0 collective-permute-done.5.rest_2_
  53.6 1.5 %collective-permute-start.10 = (bf16[1344,128]{1,0:T(8,128)(2,1)S(1)}, bf16[1344,128]{1,0:T(8,128)(2,1)S(1)}, u32[]{:S(2)}, u32[]{:S(2)}) collective-permute-start(bf16[1344,128]{1,0:T(8,128)(2,1)S(1)} %get-tuple-element.33.waited_ref), channel_id=1, source_target_pairs={{0,4},{1,5},{2,6},{3,7},{4,0},{5,1},{6,2},{7,3},{8,12},{9,13},{10,... | collective-permute-start | bytes 1032200 | tf_op jit(solution)/shard_map/ppermute | solution.py:39
  55.2 2.8 %shard_map.127 = (bf16[168,16,128]{2,1,0:T(8,128)(2,1)S(1)}, bf16[24,32,64]{2,1,0:T(8,128)(2,1)S(1)}) custom-call(s32[7,24]{1,0:T(8,128)S(1)} %fusion.4.index_ref, bf16[200,16,128]{2,1,0:T(8,128)(2,1)} %collective-permute-done.2.rest_1_.first_ref, bf16[200,16,128]{2,1,0:T(8,128)(2,1)S(1)} %all_gather.3.own_ref, ...), custom_call_target="tpu_custom_call" | custom-call | tf_op jit(solution)/shard_map/pallas_call | solution.py:337
  58.0 0.0 collective-permute-done.8.rest_5_
  58.0 0.0 collective-permute-done.7.rest_4_
  58.0 0.0 collective-permute-done.4.rest_0_
  58.0 4.2 %shard_map.128 = (f32[169,32,128]{2,1,0:T(8,128)S(1)}, s32[276]{0:T(512)S(1)}) custom-call(s32[2]{0:T(128)S(1)} %pad_add_fusion.where_ref, s32[128,128]{1,0:T(8,128)S(1)} %bitcast_convert_fusion.table_ref, bf16[1344,128]{1,0:T(8,128)(2,1)S(1)} %collective-permute-done.4.rest_0_, bf16[1344,128]{1,0:T(8,128)(2,1)S(1)} %get-tuple-element.30.rest_1_, ...), custom_call_target="tpu_custom_call" | custom-call | tf_op jit(solution)/shard_map/pallas_call | solution.py:395
  62.2 2.8 %collective-permute-done.9.rest_0_ = bf16[1344,128]{1,0:T(8,128)(2,1)S(1)} collective-permute-done((bf16[1344,128]{1,0:T(8,128)(2,1)S(1)}, bf16[1344,128]{1,0:T(8,128)(2,1)S(1)}, u32[]{:S(2)}, u32[]{:S(2)}) %collective-permute-start.9) | collective-permute-done | bytes 344096 | tf_op jit(solution)/shard_map/ppermute | solution.py:39
  65.0 0.0 collective-permute-done.10.rest_1_
  65.0 3.0 %shard_map.129 = (bf16[168,32,128]{2,1,0:T(8,128)(2,1)S(1)}, f32[169,32,128]{2,1,0:T(8,128)S(1)}, bf16[168,128]{1,0:T(8,128)(2,1)S(1)}, bf16[168,128]{1,0:T(8,12...) custom-call(s32[276]{0:T(512)S(1)} %get-tuple-element.35.lists_ref, ...), custom_call_target="tpu_custom_call", output_to_operand_aliasing={{1}: (3, {})} | custom-call | tf_op jit(solution)/shard_map/pallas_call | solution.py:492
  68.0 1.2 %collective-permute-start.11 = (bf16[168,128]{1,0:T(8,128)(2,1)S(1)}, bf16[168,128]{1,0:T(8,128)(2,1)S(1)}, u32[]{:S(2)}, u32[]{:S(2)}) collective-permute-start(bf16[168,128]{1,0:T(8,128)(2,1)S(1)} %get-tuple-element.40), channel_id=1, source_target_pairs={{0,7},{1,6},{2,5},{3,4},{4,3},{5,2},{6,1},{7,0},{8,15},{9,14},{10,... | collective-permute-start | bytes 129032 | tf_op jit(solution)/shard_map/ppermute | solution.py:39
  69.2 1.5 %collective-permute-start.12 = (bf16[168,128]{1,0:T(8,128)(2,1)S(1)}, bf16[168,128]{1,0:T(8,128)(2,1)S(1)}, u32[]{:S(2)}, u32[]{:S(2)}) collective-permute-start(bf16[168,128]{1,0:T(8,128)(2,1)S(1)} %get-tuple-element.41), channel_id=1, source_target_pairs={{0,6},{1,7},{2,4},{3,5},{4,2},{5,3},{6,0},{7,1},{8,14},{9,15},{10,... | collective-permute-start | bytes 129032 | tf_op jit(solution)/shard_map/ppermute | solution.py:39
  70.7 1.2 %collective-permute-start.13 = (bf16[168,128]{1,0:T(8,128)(2,1)S(1)}, bf16[168,128]{1,0:T(8,128)(2,1)S(1)}, u32[]{:S(2)}, u32[]{:S(2)}) collective-permute-start(bf16[168,128]{1,0:T(8,128)(2,1)S(1)} %get-tuple-element.42), channel_id=1, source_target_pairs={{0,5},{1,4},{2,7},{3,6},{4,1},{5,0},{6,3},{7,2},{8,13},{9,12},{10,... | collective-permute-start | bytes 129032 | tf_op jit(solution)/shard_map/ppermute | solution.py:39
  71.9 0.6 collective-permute-start.14
  72.5 1.1 %collective-permute-start.15 = (bf16[168,128]{1,0:T(8,128)(2,1)S(1)}, bf16[168,128]{1,0:T(8,128)(2,1)S(1)}, u32[]{:S(2)}, u32[]{:S(2)}) collective-permute-start(bf16[168,128]{1,0:T(8,128)(2,1)S(1)} %get-tuple-element.44), channel_id=1, source_target_pairs={{0,3},{1,2},{2,1},{3,0},{4,7},{5,6},{6,5},{7,4},{8,11},{9,10},{10,... | collective-permute-start | bytes 129032 | tf_op jit(solution)/shard_map/ppermute | solution.py:39
  73.6 0.0 collective-permute-done.11.rest_0_
  73.6 0.5 collective-permute-start.16
  74.2 0.1 collective-permute-done.12.rest_1_
  74.2 0.1 collective-permute-start.17
  74.3 1.7 %reshape.21 = bf16[7,24,4096]{2,1,0:T(8,128)(2,1)} reshape(bf16[168,32,128]{2,1,0:T(8,128)(2,1)S(1)} %get-tuple-element.39) | data formatting | bytes 2752512 | tf_op jit(solution)/shard_map/reshape | solution.py:660
  76.0 0.0 collective-permute-done.13.rest_2_
  76.0 0.0 collective-permute-done.14.rest_3_
  76.0 0.1 collective-permute-done.15.rest_4_
  76.1 1.5 %collective-permute-done.16.rest_5_ = bf16[168,128]{1,0:T(8,128)(2,1)S(1)} collective-permute-done((bf16[168,128]{1,0:T(8,128)(2,1)S(1)}, bf16[168,128]{1,0:T(8,128)(2,1)S(1)}, u32[]{:S(2)}, u32[]{:S(2)}) %collective-permute-start.16) | collective-permute-done | bytes 43040 | tf_op jit(solution)/shard_map/ppermute | solution.py:39
  77.6 0.0 collective-permute-done.17.rest_6_
  77.6 2.1 %shard_map.130 = bf16[12,7,1024]{2,1,0:T(8,128)(2,1)} custom-call(s32[276]{0:T(512)S(1)} %get-tuple-element.35.lists_ref, bf16[168,128]{1,0:T(8,128)(2,1)S(1)} %collective-permute-done.11.rest_0_, bf16[168,128]{1,0:T(8,128)(2,1)S(1)} %collective-permute-done.12.rest_1_, bf16[168,128]{1,0:T(8,128)(2,1)S(1)} %collective-permute-done.13.rest_2_, ...), custom_call_target="tpu_custom_call" | custom-call | tf_op jit(solution)/shard_map/pallas_call | solution.py:539
  (5 shorter events, 0.1 us)
Async XLA Ops:
  3.2 22.3 %collective-permute-start.1 = (bf16[48,64,128]{2,1,0:T(8,128)(2,1)S(1)}, bf16[48,64,128]{2,1,0:T(8,128)(2,1)S(1)}, u32[]{:S(2)}, u32[]{:S(2)}) collective-permute-start(bf16[48,64,128]{2,1,0:T(8,128)(2,1)S(1)} %shard_map.122.rest_8_.own_ref), channel_id=1, source_target_pairs={{0,8},{8,0},{16,24},{24,16},{1,9},{9,1},{17,25},{25,17},{2,10},{10... | collective-permute-start | bytes 2359304 | tf_op jit(solution)/shard_map/ppermute | solution.py:49
  6.3 19.2 %collective-permute-start = (bf16[48,64,128]{2,1,0:T(8,128)(2,1)S(1)}, bf16[48,64,128]{2,1,0:T(8,128)(2,1)S(1)}, u32[]{:S(2)}, u32[]{:S(2)}) collective-permute-start(bf16[48,64,128]{2,1,0:T(8,128)(2,1)S(1)} %shard_map.122.rest_8_.own_ref), channel_id=1, source_target_pairs={{0,0},{8,16},{16,8},{24,24},{1,1},{9,17},{17,9},{25,25},{2,2},{10,... | collective-permute-start | bytes 2359304 | tf_op jit(solution)/shard_map/ppermute | solution.py:49
  19.6 23.2 %collective-permute-start.3 = (bf16[200,16,128]{2,1,0:T(8,128)(2,1)S(1)}, bf16[200,16,128]{2,1,0:T(8,128)(2,1)}, u32[]{:S(2)}, u32[]{:S(2)}) collective-permute-start(bf16[200,16,128]{2,1,0:T(8,128)(2,1)S(1)} %all_gather.3.own_ref), channel_id=1, source_target_pairs={{0,8},{8,0},{16,24},{24,16},{1,9},{9,1},{17,25},{25,17},{2,10},{10... | collective-permute-start | bytes 2457608 | tf_op jit(solution)/shard_map/ppermute | solution.py:49
  24.0 19.7 %collective-permute-start.2 = (bf16[200,16,128]{2,1,0:T(8,128)(2,1)S(1)}, bf16[200,16,128]{2,1,0:T(8,128)(2,1)}, u32[]{:S(2)}, u32[]{:S(2)}) collective-permute-start(bf16[200,16,128]{2,1,0:T(8,128)(2,1)S(1)} %all_gather.3.own_ref), channel_id=1, source_target_pairs={{0,0},{8,16},{16,8},{24,24},{1,1},{9,17},{17,9},{25,25},{2,2},{10,... | collective-permute-start | bytes 2457608 | tf_op jit(solution)/shard_map/ppermute | solution.py:49
  31.6 21.4 %collective-permute-start.6 = (bf16[1344,128]{1,0:T(8,128)(2,1)}, bf16[1344,128]{1,0:T(8,128)(2,1)}, u32[]{:S(2)}, u32[]{:S(2)}) collective-permute-start(bf16[1344,128]{1,0:T(8,128)(2,1)} %get-tuple-element.31), channel_id=1, source_target_pairs={{0,6},{1,7},{2,4},{3,5},{4,2},{5,3},{6,0},{7,1},{8,14},{9,15},{10,... | collective-permute-start | bytes 1032200 | tf_op jit(solution)/shard_map/ppermute | solution.py:39
  33.2 20.4 %collective-permute-start.5 = (bf16[1344,128]{1,0:T(8,128)(2,1)}, bf16[1344,128]{1,0:T(8,128)(2,1)}, u32[]{:S(2)}, u32[]{:S(2)}) collective-permute-start(bf16[1344,128]{1,0:T(8,128)(2,1)} %get-tuple-element.27.rest_0_), channel_id=1, source_target_pairs={{0,7},{1,6},{2,5},{3,4},{4,3},{5,2},{6,1},{7,0},{8,15},{9,14},{10,... | collective-permute-start | bytes 1032200 | tf_op jit(solution)/shard_map/ppermute | solution.py:39
  39.4 18.6 %collective-permute-start.8 = (bf16[1344,128]{1,0:T(8,128)(2,1)S(1)}, bf16[1344,128]{1,0:T(8,128)(2,1)S(1)}, u32[]{:S(2)}, u32[]{:S(2)}) collective-permute-start(bf16[1344,128]{1,0:T(8,128)(2,1)S(1)} %get-tuple-element.32), channel_id=1, source_target_pairs={{0,3},{1,2},{2,1},{3,0},{4,7},{5,6},{6,5},{7,4},{8,11},{9,10},{10,... | collective-permute-start | bytes 1032200 | tf_op jit(solution)/shard_map/ppermute | solution.py:39
  42.8 12.3 %copy-start = (s32[24,7]{0,1:T(8,128)S(1)}, s32[24,7]{0,1:T(8,128)}, u32[]{:S(2)}) copy-start(s32[24,7]{0,1:T(8,128)} %param.18) | copy-start | bytes 2020
  42.8 15.2 %collective-permute-start.7 = (bf16[1344,128]{1,0:T(8,128)(2,1)S(1)}, bf16[1344,128]{1,0:T(8,128)(2,1)S(1)}, u32[]{:S(2)}, u32[]{:S(2)}) collective-permute-start(bf16[1344,128]{1,0:T(8,128)(2,1)S(1)} %get-tuple-element.28.rest_0_), channel_id=1, source_target_pairs={{0,5},{1,4},{2,7},{3,6},{4,1},{5,0},{6,3},{7,2},{8,13},{9,12},{10,... | collective-permute-start | bytes 1032200 | tf_op jit(solution)/shard_map/ppermute | solution.py:39
  52.3 5.8 %collective-permute-start.4 = (bf16[1344,128]{1,0:T(8,128)(2,1)S(1)}, bf16[1344,128]{1,0:T(8,128)(2,1)S(1)}, u32[]{:S(2)}, u32[]{:S(2)}) collective-permute-start(bf16[1344,128]{1,0:T(8,128)(2,1)S(1)} %get-tuple-element.29), channel_id=1, source_target_pairs={{0,1},{1,0},{2,3},{3,2},{4,5},{5,4},{6,7},{7,6},{8,9},{9,8},{10,11... | collective-permute-start | bytes 1032200 | tf_op jit(solution)/shard_map/ppermute | solution.py:39
  53.1 12.0 %collective-permute-start.9 = (bf16[1344,128]{1,0:T(8,128)(2,1)S(1)}, bf16[1344,128]{1,0:T(8,128)(2,1)S(1)}, u32[]{:S(2)}, u32[]{:S(2)}) collective-permute-start(bf16[1344,128]{1,0:T(8,128)(2,1)S(1)} %get-tuple-element.38), channel_id=1, source_target_pairs={{0,2},{1,3},{2,0},{3,1},{4,6},{5,7},{6,4},{7,5},{8,10},{9,11},{10,... | collective-permute-start | bytes 1032200 | tf_op jit(solution)/shard_map/ppermute | solution.py:39
  53.6 11.4 %collective-permute-start.10 = (bf16[1344,128]{1,0:T(8,128)(2,1)S(1)}, bf16[1344,128]{1,0:T(8,128)(2,1)S(1)}, u32[]{:S(2)}, u32[]{:S(2)}) collective-permute-start(bf16[1344,128]{1,0:T(8,128)(2,1)S(1)} %get-tuple-element.33.waited_ref), channel_id=1, source_target_pairs={{0,4},{1,5},{2,6},{3,7},{4,0},{5,1},{6,2},{7,3},{8,12},{9,13},{10,... | collective-permute-start | bytes 1032200 | tf_op jit(solution)/shard_map/ppermute | solution.py:39
  68.0 5.6 %collective-permute-start.11 = (bf16[168,128]{1,0:T(8,128)(2,1)S(1)}, bf16[168,128]{1,0:T(8,128)(2,1)S(1)}, u32[]{:S(2)}, u32[]{:S(2)}) collective-permute-start(bf16[168,128]{1,0:T(8,128)(2,1)S(1)} %get-tuple-element.40), channel_id=1, source_target_pairs={{0,7},{1,6},{2,5},{3,4},{4,3},{5,2},{6,1},{7,0},{8,15},{9,14},{10,... | collective-permute-start | bytes 129032 | tf_op jit(solution)/shard_map/ppermute | solution.py:39
  69.2 5.0 %collective-permute-start.12 = (bf16[168,128]{1,0:T(8,128)(2,1)S(1)}, bf16[168,128]{1,0:T(8,128)(2,1)S(1)}, u32[]{:S(2)}, u32[]{:S(2)}) collective-permute-start(bf16[168,128]{1,0:T(8,128)(2,1)S(1)} %get-tuple-element.41), channel_id=1, source_target_pairs={{0,6},{1,7},{2,4},{3,5},{4,2},{5,3},{6,0},{7,1},{8,14},{9,15},{10,... | collective-permute-start | bytes 129032 | tf_op jit(solution)/shard_map/ppermute | solution.py:39
  70.7 5.3 %collective-permute-start.13 = (bf16[168,128]{1,0:T(8,128)(2,1)S(1)}, bf16[168,128]{1,0:T(8,128)(2,1)S(1)}, u32[]{:S(2)}, u32[]{:S(2)}) collective-permute-start(bf16[168,128]{1,0:T(8,128)(2,1)S(1)} %get-tuple-element.42), channel_id=1, source_target_pairs={{0,5},{1,4},{2,7},{3,6},{4,1},{5,0},{6,3},{7,2},{8,13},{9,12},{10,... | collective-permute-start | bytes 129032 | tf_op jit(solution)/shard_map/ppermute | solution.py:39
  71.9 4.1 %collective-permute-start.14 = (bf16[168,128]{1,0:T(8,128)(2,1)S(1)}, bf16[168,128]{1,0:T(8,128)(2,1)S(1)}, u32[]{:S(2)}, u32[]{:S(2)}) collective-permute-start(bf16[168,128]{1,0:T(8,128)(2,1)S(1)} %get-tuple-element.43), channel_id=1, source_target_pairs={{0,4},{1,5},{2,6},{3,7},{4,0},{5,1},{6,2},{7,3},{8,12},{9,13},{10,... | collective-permute-start | bytes 129032 | tf_op jit(solution)/shard_map/ppermute | solution.py:39
  72.5 3.7 %collective-permute-start.15 = (bf16[168,128]{1,0:T(8,128)(2,1)S(1)}, bf16[168,128]{1,0:T(8,128)(2,1)S(1)}, u32[]{:S(2)}, u32[]{:S(2)}) collective-permute-start(bf16[168,128]{1,0:T(8,128)(2,1)S(1)} %get-tuple-element.44), channel_id=1, source_target_pairs={{0,3},{1,2},{2,1},{3,0},{4,7},{5,6},{6,5},{7,4},{8,11},{9,10},{10,... | collective-permute-start | bytes 129032 | tf_op jit(solution)/shard_map/ppermute | solution.py:39
  73.6 4.0 %collective-permute-start.16 = (bf16[168,128]{1,0:T(8,128)(2,1)S(1)}, bf16[168,128]{1,0:T(8,128)(2,1)S(1)}, u32[]{:S(2)}, u32[]{:S(2)}) collective-permute-start(bf16[168,128]{1,0:T(8,128)(2,1)S(1)} %get-tuple-element.45), channel_id=1, source_target_pairs={{0,2},{1,3},{2,0},{3,1},{4,6},{5,7},{6,4},{7,5},{8,10},{9,11},{10,... | collective-permute-start | bytes 129032 | tf_op jit(solution)/shard_map/ppermute | solution.py:39
  74.2 3.4 %collective-permute-start.17 = (bf16[168,128]{1,0:T(8,128)(2,1)S(1)}, bf16[168,128]{1,0:T(8,128)(2,1)S(1)}, u32[]{:S(2)}, u32[]{:S(2)}) collective-permute-start(bf16[168,128]{1,0:T(8,128)(2,1)S(1)} %get-tuple-element.46), channel_id=1, source_target_pairs={{0,1},{1,0},{2,3},{3,2},{4,5},{5,4},{6,7},{7,6},{8,9},{9,8},{10,11... | collective-permute-start | bytes 129032 | tf_op jit(solution)/shard_map/ppermute | solution.py:39
